TPU v7x, 32 devices: a whole 2x2x4 slice. The times are simulated.
32 devices in a mesh: grp: 4 (over x, core), dev: 8 (over z, y).
Axes of the slice: x: 2, y: 2, z: 4, core: 2. Of those that a mesh axis runs over, the one named last changes fastest.
Arguments:
- charges: bfloat16 [32, 131072], P(None, ('grp', 'dev')), may hold values from -6 to 6
- points: bfloat16 [3, 131072], P(None, ('grp', 'dev')), may hold values from -1.1953125 to 1.1953125
- basis: bfloat16 [64, 131072], P(None, ('grp', 'dev')), may hold values from -0.75 to 0.75
- up_leaf: bfloat16 [64, 64, 2048], P(None, None, ('grp', 'dev')), may hold values from -0.25 to 0.25
- up_branch: bfloat16 [64, 64, 256], P(None, None, ('grp', 'dev')), may hold values from -0.25 to 0.25
- up_device: bfloat16 [64, 64, 32], P(None, None, ('grp', 'dev')), may hold values from -0.25 to 0.25
- down_leaf: bfloat16 [64, 64, 2048], P(None, None, ('grp', 'dev')), may hold values from -0.75 to 0.75
- down_branch: bfloat16 [64, 64, 256], P(None, None, ('grp', 'dev')), may hold values from -0.75 to 0.75
- down_device: bfloat16 [64, 64, 32], P(None, None, ('grp', 'dev')), may hold values from -0.75 to 0.75
- proxy_leaf: bfloat16 [3, 64, 2048], P(None, None, ('grp', 'dev')), may hold values from -12 to 12
- proxy_branch: bfloat16 [3, 64, 256], P(None, None, ('grp', 'dev')), may hold values from -12 to 12
- proxy_device: bfloat16 [3, 64, 32], P(None, None, ('grp', 'dev')), may hold values from -12 to 12
- proxy_group: bfloat16 [3, 64, 4], P(None, None, 'grp'), may hold values from -12 to 12
- far_leaf: int32 [16, 2048], P(None, ('grp', 'dev')), may hold values from 0 to 191
- send_leaf: int32 [4, 1024], P(None, ('grp', 'dev')), may hold values from 0 to 63
- far_branch: int32 [16, 256], P(None, ('grp', 'dev')), may hold values from 0 to 63
- near_leaf: int32 [16, 2048], P(None, ('grp', 'dev')), may hold values from -4 to 4
Outputs:
- potential: float32 [32, 131072], P(None, ('grp', 'dev'))
All inputs are finite; a program needn't handle non-finite values.
Results may differ from a plain program's by a relative error of at most 0.0034.
Values may be sent and summed in bfloat16 or wider, within the bound.
No kernel may reach another device: no remote copies, remote signals or barrier semaphores. Data moves between devices by JAX's collectives and lax.ppermute only.
A program may use at most 192 MiB of HBM per device.

v0:
```python
import math

import jax
import jax.numpy as jnp
from jax import lax
from jax.sharding import PartitionSpec as P

REACH = 4


INV_FOUR_PI = 1.0 / (4.0 * math.pi)
SOFTEN = 0.25


def padded(cells, sides, width):
    for axis, dim in sides:
        count = lax.axis_size(axis)
        ends = count - 1
        head = lax.slice_in_dim(cells, 0, width, axis=dim)
        tail = lax.slice_in_dim(cells, cells.shape[dim] - width, cells.shape[dim], axis=dim)
        cells = jnp.concatenate(
            [
                lax.ppermute(tail, axis, [(i, (i + 1) % count) for i in range(ends)]),
                cells,
                lax.ppermute(head, axis, [((i + 1) % count, i) for i in range(ends)]),
            ],
            axis=dim,
        )
    return cells


def kernel_block(target, source):
    delta = target.astype(jnp.float32)[:, :, None] - source.astype(jnp.float32)[:, None, :]
    square = jnp.sum(delta * delta, axis=0)
    return (INV_FOUR_PI * lax.rsqrt(square + SOFTEN)).astype(jnp.bfloat16)


def split_last(array, count_blocks, width):
    shaped = array.reshape(array.shape[:-1] + (count_blocks, width))
    return jnp.moveaxis(shaped, -2, 0)


def on_device(
    charges,
    points,
    basis,
    up_leaf,
    up_branch,
    up_device,
    down_leaf,
    down_branch,
    down_device,
    proxy_leaf,
    proxy_branch,
    proxy_device,
    proxy_group,
    far_leaf,
    send_leaf,
    far_branch,
    near_leaf,
):
    rhs_count, point_count = charges.shape
    rank_size = basis.shape[0]
    leaf_count = up_leaf.shape[2]
    leaf_size = point_count // leaf_count
    branch_count = leaf_count // 8
    slot_count = send_leaf.shape[0]
    groups = lax.axis_size("grp")
    members = lax.axis_size("dev")
    devices = groups * members
    my_group = lax.axis_index("grp")
    my_member = lax.axis_index("dev")
    m_leaf = jnp.einsum(
        "kbp,rbp->rkb",
        basis.reshape(rank_size, leaf_count, leaf_size),
        charges.reshape(rhs_count, leaf_count, leaf_size),
        preferred_element_type=jnp.float32,
    ).astype(jnp.bfloat16)
    m_branch = jnp.einsum(
        "kjci,rjci->rkc",
        up_leaf.reshape(rank_size, rank_size, branch_count, 8),
        m_leaf.reshape(rhs_count, rank_size, branch_count, 8),
        preferred_element_type=jnp.float32,
    ).astype(jnp.bfloat16)
    m_device = jnp.einsum(
        "kjc,rjc->rk", up_branch, m_branch, preferred_element_type=jnp.float32
    ).astype(jnp.bfloat16)[:, :, None]
    picks = send_leaf.T
    sent_m = jnp.take(m_leaf, picks, axis=2)
    sent_p = jnp.take(proxy_leaf, picks, axis=2)
    recv_m, recv_p = (
        lax.all_to_all(
            sent_m.reshape(rhs_count, rank_size, devices * slot_count),
            ("grp", "dev"),
            split_axis=2,
            concat_axis=2,
            tiled=True,
        ),
        lax.all_to_all(
            sent_p.reshape(3, rank_size, devices * slot_count),
            ("grp", "dev"),
            split_axis=2,
            concat_axis=2,
            tiled=True,
        ),
    )
    table_m = jnp.concatenate([m_leaf, recv_m], axis=2)
    table_p = jnp.concatenate([proxy_leaf, recv_p], axis=2)
    all_m1, all_p1, all_md, all_pd, all_up = (
        lax.all_gather(m_branch, "dev", axis=2, tiled=True),
        lax.all_gather(proxy_branch, "dev", axis=2, tiled=True),
        lax.all_gather(m_device, "dev", axis=2, tiled=True),
        lax.all_gather(proxy_device, "dev", axis=2, tiled=True),
        lax.all_gather(up_device, "dev", axis=2, tiled=True),
    )
    m_group = jnp.einsum("kjv,rjv->rk", all_up, all_md, preferred_element_type=jnp.float32).astype(
        jnp.bfloat16
    )
    top_m, top_p = (
        lax.all_gather(m_group[:, :, None], "grp", axis=2, tiled=True),
        lax.all_gather(proxy_group, "grp", axis=2, tiled=True),
    )
    far_top = (jnp.abs(jnp.arange(groups, dtype=jnp.int32) - my_group) >= 2).astype(jnp.bfloat16)
    kern_top = kernel_block(proxy_group, top_p) * far_top
    l_group = jnp.einsum("kjg,rjg->rk", kern_top, top_m, preferred_element_type=jnp.float32).astype(
        jnp.bfloat16
    )
    far_dev = (jnp.abs(jnp.arange(members, dtype=jnp.int32) - my_member) >= 2).astype(jnp.bfloat16)
    kern_dev = kernel_block(proxy_device, all_pd) * far_dev
    l_device = jnp.einsum("kjv,rjv->rk", kern_dev, all_md, preferred_element_type=jnp.float32)
    l_device = l_device + jnp.einsum(
        "kj,rj->rk", down_device[:, :, 0], l_group, preferred_element_type=jnp.float32
    )
    l_device = l_device.astype(jnp.bfloat16)
    src_branch = jnp.take(all_m1, far_branch, axis=2)
    src_bproxy = jnp.take(all_p1, far_branch, axis=2)
    kern_branch = kernel_block(proxy_branch[:, :, None, :], src_bproxy)
    l_branch = jnp.einsum(
        "kjeb,rjeb->rkb", kern_branch, src_branch, preferred_element_type=jnp.float32
    )
    l_branch = l_branch + jnp.einsum(
        "kjb,rj->rkb", down_branch, l_device, preferred_element_type=jnp.float32
    )
    l_branch = l_branch.astype(jnp.bfloat16)
    stacked = jnp.concatenate([charges, points], axis=0)
    wide = padded(stacked, ((("grp", "dev"), 1),), REACH * leaf_size)
    wide = wide.reshape(rhs_count + 3, leaf_count + 2 * REACH, leaf_size)
    parents = jnp.repeat(l_branch, 8, axis=2)
    width = math.gcd(leaf_count, 64)
    count_blocks = leaf_count // width
    starts = jnp.arange(count_blocks, dtype=jnp.int32) * width
    offsets = jnp.arange(width, dtype=jnp.int32)[None, :] + REACH

    def leaf_step(inputs):
        far_ids, near_ids, target_p, down_blk, parent_blk, basis_blk, point_blk, start = inputs
        src_m = jnp.take(table_m, far_ids, axis=2)
        src_p = jnp.take(table_p, far_ids, axis=2)
        kern = kernel_block(target_p[:, :, None, :], src_p)
        local = jnp.einsum("kjeb,rjeb->rkb", kern, src_m, preferred_element_type=jnp.float32)
        local = local + jnp.einsum(
            "kjb,rjb->rkb", down_blk, parent_blk, preferred_element_type=jnp.float32
        )
        l_leaf = local.astype(jnp.bfloat16)
        result = jnp.einsum("kbp,rkb->rbp", basis_blk, l_leaf, preferred_element_type=jnp.float32)
        rows = near_ids + start + offsets
        source = jnp.take(wide, rows, axis=1)
        src_x = source[:rhs_count]
        src_pt = jnp.moveaxis(source[rhs_count:], 3, 1)
        target_pt = jnp.moveaxis(point_blk, 2, 1)[:, :, None, :]
        kern_near = kernel_block(target_pt, src_pt)
        return result + jnp.einsum(
            "ijeb,rebj->rbi", kern_near, src_x, preferred_element_type=jnp.float32
        )

    basis_blocks = jnp.moveaxis(basis.reshape(rank_size, count_blocks, width, leaf_size), 1, 0)
    point_blocks = jnp.moveaxis(points.reshape(3, count_blocks, width, leaf_size), 1, 0)
    blocks = lax.map(
        leaf_step,
        (
            split_last(far_leaf, count_blocks, width),
            split_last(near_leaf, count_blocks, width),
            split_last(proxy_leaf, count_blocks, width),
            split_last(down_leaf, count_blocks, width),
            split_last(parents, count_blocks, width),
            basis_blocks,
            point_blocks,
            starts,
        ),
    )
    return jnp.moveaxis(blocks, 0, 1).reshape(rhs_count, point_count)


def solution(mesh):
    placed = (
        P(None, ("grp", "dev")),
        P(None, ("grp", "dev")),
        P(None, ("grp", "dev")),
        P(None, None, ("grp", "dev")),
        P(None, None, ("grp", "dev")),
        P(None, None, ("grp", "dev")),
        P(None, None, ("grp", "dev")),
        P(None, None, ("grp", "dev")),
        P(None, None, ("grp", "dev")),
        P(None, None, ("grp", "dev")),
        P(None, None, ("grp", "dev")),
        P(None, None, ("grp", "dev")),
        P(None, None, "grp"),
        P(None, ("grp", "dev")),
        P(None, ("grp", "dev")),
        P(None, ("grp", "dev")),
        P(None, ("grp", "dev")),
    )
    return jax.shard_map(
        on_device, mesh=mesh, in_specs=placed, out_specs=P(None, ("grp", "dev")), check_vma=False
    )
```

profile of v0, /device:TPU:0, one launch (start us, length us, event | category | flops | bytes accessed | tf_op | source)
XLA Modules:
  0.0 455.1 jit_solution(15265806583267256885)
XLA Ops:
  4.5 6.1 %collective-permute-start = (bf16[35,256]{1,0:T(8,128)(2,1)}, bf16[35,256]{1,0:T(8,128)(2,1)}, u32[]{:S(2)}, u32[]{:S(2)}) collective-permute-start(bf16[35,256]{1,0:T(8,128)(2,1)} %get-tuple-element.31), channel_id=1, source_target_pairs={{0,1},{1,2},{2,3},{3,4},{4,5},{5,6},{6,7},{7,8},{8,9},{9,10},{10,1... | collective-permute-start | bytes 53768 | tf_op jit(solution)/shard_map/ppermute | solution.py:23
  16.4 8.2 %all-to-all-start.1 = ((bf16[32,2,384]{2,1,0:T(2,128)(2,1)}), bf16[32,2,384]{2,1,0:T(2,128)(2,1)S(1)}, u32[]{:S(2)}, u32[]{:S(2)}) async-start(bf16[32,2,384]{2,1,0:T(2,128)(2,1)} %reshape.203), calls=%async_computation.1 | async-start | bytes 98304 | tf_op jit(solution)/shard_map/all_to_all | solution.py:99
  29.4 26.6 %all_gather.22 = bf16[3,64,64]{1,2,0:T(8,128)(2,1)S(1)} all-gather(bf16[3,64,8]{1,2,0:T(8,128)(2,1)} %param.27), channel_id=1, replica_groups=mesh['grp'=4,'dev'=8] {'dev'}, dimensions={2}, use_global_device_ids=true | all-gather | bytes 27648 | tf_op jit(solution)/shard_map/all_gather | solution.py:111
  56.8 19.0 %all_gather.24 = bf16[3,64,8]{1,0,2:T(4,128)(2,1)S(1)} all-gather(bf16[3,64,1]{1,0,2:T(4,128)(2,1)} %param.28), channel_id=1, replica_groups=mesh['grp'=4,'dev'=8] {'dev'}, dimensions={2}, use_global_device_ids=true | all-gather | bytes 3456 | tf_op jit(solution)/shard_map/all_gather | solution.py:113
  77.1 6.4 %all_gather.27 = bf16[3,64,4]{1,0,2:T(4,128)(2,1)} all-gather(bf16[3,64,1]{1,0,2:T(4,128)(2,1)} %param.29), channel_id=1, replica_groups=mesh['grp'=4,'dev'=8] {'grp'}, dimensions={2}, use_global_device_ids=true | all-gather | bytes 1920 | tf_op jit(solution)/shard_map/all_gather | solution.py:121
  98.3 31.2 %all_gather.21 = bf16[32,64,64]{1,0,2:T(8,128)(2,1)S(1)} all-gather(bf16[32,64,8]{1,0,2:T(8,128)(2,1)S(1)} %fusion.24), channel_id=1, replica_groups=mesh['grp'=4,'dev'=8] {'dev'}, dimensions={2}, use_global_device_ids=true | all-gather | bytes 294912 | tf_op jit(solution)/shard_map/all_gather | solution.py:110
  131.4 30.5 %all_gather.23 = bf16[32,64,8]{1,0,2:T(8,128)(2,1)S(1)} all-gather(bf16[32,64,1]{1,0,2:T(8,128)(2,1)S(1)} %fusion.31), channel_id=1, replica_groups=mesh['grp'=4,'dev'=8] {'dev'}, dimensions={2}, use_global_device_ids=true | all-gather | bytes 36864 | tf_op jit(solution)/shard_map/all_gather | solution.py:112
  161.9 30.7 %all_gather.25 = bf16[64,64,8]{1,0,2:T(8,128)(2,1)S(1)} all-gather(bf16[64,64,1]{1,0,2:T(8,128)(2,1)} %param.22), channel_id=1, replica_groups=mesh['grp'=4,'dev'=8] {'dev'}, dimensions={2}, use_global_device_ids=true | all-gather | bytes 73728 | tf_op jit(solution)/shard_map/all_gather | solution.py:114
  194.0 5.2 %all_gather.26 = bf16[32,64,4]{1,0,2:T(8,128)(2,1)S(1)} all-gather(bf16[32,64,1]{1,0,2:T(8,128)(2,1)S(1)} %fusion.30), channel_id=1, replica_groups=mesh['grp'=4,'dev'=8] {'grp'}, dimensions={2}, use_global_device_ids=true | all-gather | bytes 20480 | tf_op jit(solution)/shard_map/all_gather | solution.py:120
  215.9 11.0 %gather_fusion.6 = bf16[1024,35,64]{2,1,0:T(8,128)(2,1)} fusion(bf16[35,72,64]{2,0,1:T(8,128)(2,1)S(1)} %copy.165, s32[1024]{0:T(1024)S(1)} %get-tuple-element.34), kind=kCustom, calls=%fused_computation.6 | custom fusion | bytes 9179136 | tf_op jit(solution)/shard_map/while/body/eval_jaxpr/jit(_take)/gather | solution.py:166
  227.0 6.0 %fusion = bf16[35,16,64,64]{3,0,1,2:T(8,128)(2,1)S(1)} fusion(bf16[16,64,35,64]{3,2,1,0:T(8,128)(2,1)} %bitcast.129, pred[16,64]{0,1:T(8,128)(4,1)S(1)} %copy.164), kind=kLoop, calls=%fused_computation.13 | loop fusion | flops 2293760 | bytes 9176064 | tf_op jit(solution)/shard_map/while/body/eval_jaxpr/jit(_take)/select_n | solution.py:166
  233.0 3.9 copy-done.2
  241.0 33.6 %multiply_reduce_fusion = f32[64,64,16,64]{3,2,1,0:T(8,128)} fusion(f32[3,64,16,64]{3,2,1,0:T(8,128)S(1)} %copy.169, f32[3,64,64]{2,1,0:T(8,128)S(1)} %copy.168), kind=kLoop, calls=%fused_computation.7 | loop fusion | flops 33554432 | bytes 17612800 | tf_op jit(solution)/shard_map/while/body/eval_jaxpr/reduce_sum | solution.py:34
  274.6 18.3 %multiply_convert_fusion = bf16[64,64,16,64]{3,2,1,0:T(8,128)(2,1)} fusion(f32[64,64,16,64]{3,2,1,0:T(8,128)} %multiply_reduce_fusion), kind=kLoop, calls=%fused_computation.9 | loop fusion | flops 12582912 | bytes 25165824 | tf_op jit(solution)/shard_map/while/body/eval_jaxpr/convert_element_type | solution.py:35
  292.9 31.7 %copy.170 = bf16[64,64,16,64]{1,0,2,3:T(8,128)(2,1)} copy(bf16[64,64,16,64]{3,2,1,0:T(8,128)(2,1)} %multiply_convert_fusion) | data formatting | bytes 16777216 | tf_op jit(solution)/shard_map/while/body/eval_jaxpr/convert_element_type | solution.py:35
  324.6 11.5 %fusion.14 = f32[64,32,64]{2,1,0:T(8,128)} fusion(bf16[64,64,16,64]{1,0,2,3:T(8,128)(2,1)} %copy.170, bf16[35,16,64,64]{3,0,1,2:T(8,128)(2,1)} %copy-done.2), kind=kOutput, calls=%fused_computation.31 | convolution fusion | flops 268435456 | bytes 25690112 | tf_op jit(solution)/shard_map/while/body/eval_jaxpr/ijeb,rebj->rbi/dot_general | solution.py:171
  336.1 3.6 all-to-all-start
  340.0 3.6 gather_fusion.3
  348.2 33.6 %multiply_reduce_fusion.1 = f32[64,64,16,64]{3,2,1,0:T(8,128)} fusion(f32[3,64,16,64]{3,2,1,0:T(8,128)S(1)} %copy.144, f32[3,64,64]{2,1,0:T(8,128)S(1)} %convert_element_type.117), kind=kLoop, calls=%fused_computation.8 | loop fusion | flops 33554432 | bytes 17612800 | tf_op jit(solution)/shard_map/while/body/eval_jaxpr/reduce_sum | solution.py:34
  381.7 18.3 %multiply_convert_fusion.1 = bf16[64,64,16,64]{3,2,1,0:T(8,128)(2,1)} fusion(f32[64,64,16,64]{3,2,1,0:T(8,128)} %multiply_reduce_fusion.1), kind=kLoop, calls=%fused_computation.10 | loop fusion | flops 12582912 | bytes 25165824 | tf_op jit(solution)/shard_map/while/body/eval_jaxpr/convert_element_type | solution.py:35
  400.0 22.0 %copy.145 = bf16[64,64,16,64]{1,0,3,2:T(8,128)(2,1)} copy(bf16[64,64,16,64]{3,2,1,0:T(8,128)(2,1)} %multiply_convert_fusion.1) | data formatting | bytes 16777216 | tf_op jit(solution)/shard_map/while/body/eval_jaxpr/convert_element_type | solution.py:35
  426.6 9.9 %gather_fusion.1 = bf16[1024,32,64]{2,1,0:T(8,128)(2,1)} fusion(bf16[32,64,192]{1,0,2:T(8,128)(2,1)S(1)} %pad_maximum_fusion, s32[1024]{0:T(1024)S(1)} %broadcast_clamp_fusion.1), kind=kCustom, calls=%fused_computation.1 | custom fusion | bytes 8392704 | tf_op jit(solution)/shard_map/while/body/eval_jaxpr/jit(_take)/gather | solution.py:156
  436.5 11.8 %fusion.10 = f32[64,32,64]{2,1,0:T(8,128)} fusion(bf16[64,64,16,64]{1,0,3,2:T(8,128)(2,1)} %copy.145, bf16[16,64,32,64]{3,2,1,0:T(8,128)(2,1)} %bitcast.130, pred[16,64]{1,0:T(8,128)(4,1)S(1)} %copy-done.8), kind=kOutput, calls=%fused_computation.27 | convolution fusion | flops 270532608 | bytes 13108224 | tf_op jit(solution)/shard_map/while/body/eval_jaxpr/kjeb,rjeb->rkb/dot_general | solution.py:159
  448.3 3.9 fusion.13
  (103 shorter events, 68.2 us)
Async XLA Ops:
  0.0 205.0 %copy-start = (bf16[64,64,8]{1,2,0:T(8,128)(2,1)S(1)}, bf16[64,64,8]{1,2,0:T(8,128)(2,1)}, u32[]{:S(2)}) copy-start(bf16[64,64,8]{1,2,0:T(8,128)(2,1)} %param.24) | copy-start | bytes 196612
  1.8 0.8 copy-start.5
  3.2 211.2 %collective-permute-start.1 = (bf16[35,256]{1,0:T(8,128)(2,1)}, bf16[35,256]{1,0:T(8,128)(2,1)}, u32[]{:S(2)}, u32[]{:S(2)}) collective-permute-start(bf16[35,256]{1,0:T(8,128)(2,1)} %get-tuple-element.32), channel_id=1, source_target_pairs={{1,0},{2,1},{3,2},{4,3},{5,4},{6,5},{7,6},{8,7},{9,8},{10,9},{11,1... | collective-permute-start | bytes 53768 | tf_op jit(solution)/shard_map/ppermute | solution.py:25
  4.5 209.9 %collective-permute-start = (bf16[35,256]{1,0:T(8,128)(2,1)}, bf16[35,256]{1,0:T(8,128)(2,1)}, u32[]{:S(2)}, u32[]{:S(2)}) collective-permute-start(bf16[35,256]{1,0:T(8,128)(2,1)} %get-tuple-element.31), channel_id=1, source_target_pairs={{0,1},{1,2},{2,3},{3,4},{4,5},{5,6},{6,7},{7,8},{8,9},{9,10},{10,1... | collective-permute-start | bytes 53768 | tf_op jit(solution)/shard_map/ppermute | solution.py:23
  16.4 319.7 %all-to-all-start.1 = ((bf16[32,2,384]{2,1,0:T(2,128)(2,1)}), bf16[32,2,384]{2,1,0:T(2,128)(2,1)S(1)}, u32[]{:S(2)}, u32[]{:S(2)}) async-start(bf16[32,2,384]{2,1,0:T(2,128)(2,1)} %reshape.203), calls=%async_computation.1 | async-start | bytes 98304 | tf_op jit(solution)/shard_map/all_to_all | solution.py:99
  29.4 61.2 %copy-start.9 = (pred[16,8]{0,1:T(8,128)(4,1)}, pred[16,8]{0,1:T(8,128)(4,1)S(1)}, u32[]{:S(2)}) copy-start(pred[16,8]{0,1:T(8,128)(4,1)S(1)} %compare_and_fusion.2) | copy-start | bytes 388
  129.6 77.3 %copy-start.7 = (bf16[3,4096]{1,0:T(4,128)(2,1)S(1)}, bf16[3,4096]{1,0:T(4,128)(2,1)}, u32[]{:S(2)}) copy-start(bf16[3,4096]{1,0:T(4,128)(2,1)} %param.18) | copy-start | bytes 73732
  129.6 77.4 %copy-start.6 = (bf16[3,64,64]{2,1,0:T(8,128)(2,1)S(1)}, bf16[3,64,64]{2,1,0:T(8,128)(2,1)}, u32[]{:S(2)}) copy-start(bf16[3,64,64]{2,1,0:T(8,128)(2,1)} %param.26) | copy-start | bytes 73732
  233.0 3.9 copy-start.2
  324.6 19.0 %copy-start.8 = (pred[16,64]{1,0:T(8,128)(4,1)S(1)}, pred[16,64]{1,0:T(8,128)(4,1)}, u32[]{:S(2)}) copy-start(pred[16,64]{1,0:T(8,128)(4,1)} %compare_and_fusion.1) | copy-start | bytes 3076
  336.1 85.9 %all-to-all-start = ((bf16[32,2,4096]{2,1,0:T(2,128)(2,1)}), bf16[32,2,4096]{2,1,0:T(2,128)(2,1)}, u32[]{:S(2)}, u32[]{:S(2)}) async-start(bf16[32,2,4096]{2,1,0:T(2,128)(2,1)} %reshape.205), calls=%async_computation | async-start | bytes 1048576 | tf_op jit(solution)/shard_map/all_to_all | solution.py:92
  436.5 11.8 %copy-start.3 = (f32[64,32,64]{2,1,0:T(8,128)S(1)}, f32[64,32,64]{2,1,0:T(8,128)}, u32[]{:S(2)}) copy-start(f32[64,32,64]{2,1,0:T(8,128)} %fusion.14) | copy-start | bytes 1572868
  436.5 11.8 %copy-start.4 = (bf16[64,64,64]{1,0,2:T(8,128)(2,1)S(1)}, bf16[64,64,64]{1,0,2:T(8,128)(2,1)}, u32[]{:S(2)}) copy-start(bf16[64,64,64]{1,0,2:T(8,128)(2,1)} %copy.162) | copy-start | bytes 1572868
  436.5 18.7 %copy-start.1 = (bf16[64,64,8]{1,2,0:T(8,128)(2,1)S(1)}, bf16[64,64,8]{1,2,0:T(8,128)(2,1)}, u32[]{:S(2)}) copy-start(bf16[64,64,8]{1,2,0:T(8,128)(2,1)} %param.24) | copy-start | bytes 196612
where the time goes:
time: 457 us; the launch traced here: 455 us
  blocking collectives  150 us (33%)
  other arithmetic  134 us (29%)
  local copies, waits for them, and re-layouts  118 us (26%)
  matrix products  34.5 us (8%)
  starting transfers between devices  19.1 us (4%)
    reduce_sum x5, other arithmetic, kernel_block(): square = jnp.sum(delta * delta, axis=0)  70.6 us
    convert_element_type x2, local copies, waits for them, and re-layouts, kernel_block(): return (INV_FOUR_PI * lax.rsqrt(square + SOFTEN)).astype(jnp.bfloat16)  53.7 us
    convert_element_type x3, other arithmetic, kernel_block(): return (INV_FOUR_PI * lax.rsqrt(square + SOFTEN)).astype(jnp.bfloat16)  38.5 us
    all_gather x1, blocking collectives, on_device(): lax.all_gather(m_branch, 'dev', axis=2, tiled=True)  31.2 us
    all_gather x1, blocking collectives, on_device(): lax.all_gather(up_device, 'dev', axis=2, tiled=True)  30.7 us
    all_gather x1, blocking collectives, on_device(): lax.all_gather(m_device, 'dev', axis=2, tiled=True)  30.5 us
    all_gather x1, blocking collectives, on_device(): lax.all_gather(proxy_branch, 'dev', axis=2, tiled=True)  26.6 us
    all_gather x1, blocking collectives, on_device(): lax.all_gather(proxy_device, 'dev', axis=2, tiled=True)  19 us
  transfers between devices with their start and end apart: 4, of which 0 were waited for; matrix products, arithmetic and copies ran while one was open for 54% of the time, Pallas kernels for 0%

commit v1 on v0

v1 whole, which is shorter than its diff:
```python
import functools
import math

import jax
import jax.numpy as jnp
from jax import lax
from jax.experimental import pallas as pl
from jax.experimental.pallas import tpu as pltpu
from jax.sharding import PartitionSpec as P

REACH = 4
FAN = 8

INV_FOUR_PI = 1.0 / (4.0 * math.pi)
SOFTEN = 0.25
FEATURES = 16

BF16 = jnp.bfloat16
F32 = jnp.float32


def dot(a, b):
    return jnp.dot(a, b, preferred_element_type=F32)


def dot_t(a, b):
    return lax.dot_general(a, b, (((1,), (1,)), ((), ())), preferred_element_type=F32)


def dot_0(a, b):
    return lax.dot_general(a, b, (((0,), (0,)), ((), ())), preferred_element_type=F32)


def low_half(shape):
    width = shape[-1]
    return lax.broadcasted_iota(jnp.int32, shape, len(shape) - 1) < width // 2


def pair(low, first, second):
    return jnp.where(low, first, second)


def swap(tile):
    half = tile.shape[-1] // 2
    return jnp.concatenate([tile[..., half:], tile[..., :half]], axis=-1)


def twice(tile):
    return jnp.concatenate([tile, tile], axis=-1)


def three(value):
    first = value.astype(BF16).astype(F32)
    rest = value - first
    second = rest.astype(BF16).astype(F32)
    return first, second, rest - second


def source_rows(x, y, z):
    one = jnp.ones_like(x)
    return (-2.0 * x, -2.0 * y, -2.0 * z, one, one, one) + three(x * x + y * y + z * z)


def target_rows(x, y, z):
    one = jnp.ones_like(x)
    return (x, y, z) + three(x * x + y * y + z * z + SOFTEN) + (one, one, one)


def put_rows(ref, rows, start, count, step):
    for f in range(FEATURES):
        value = rows[f] if f < len(rows) else jnp.zeros_like(rows[0])
        ref[pl.ds(start * FEATURES + f, count, stride=step * FEATURES), :] = value


def kern_of(square):
    return (INV_FOUR_PI * lax.rsqrt(square)).astype(BF16)


def interact(target, slots, source_ref, moment_ref):
    rank2 = source_ref.shape[-1]
    low_s = low_half((FEATURES, rank2))
    low_m = low_half(moment_ref.shape[1:])
    sources, moments = [], []
    for first, second in zip(slots[0::2], slots[1::2]):
        sources.append(pair(low_s, source_ref[first], source_ref[second]))
        moments.append(pair(low_m, moment_ref[first], moment_ref[second]))
    square = dot_0(target, jnp.concatenate(sources, axis=1))
    return dot_t(jnp.concatenate(moments, axis=1), kern_of(square))


def listed_kernel(send_ref, charges_ref, basis_ref, proxy_ref, moment_ref, own_ref, out_ref, tile_ref):
    slots, devices = send_ref.shape
    leaves, rhs, rank2 = moment_ref.shape
    rank = rank2 // 2
    low = low_half((rhs, rank2))
    tile_ref[...] = jnp.zeros_like(tile_ref)
    for c in range(3):
        spread = twice(jnp.transpose(proxy_ref[c].astype(F32)))
        own_ref[c] = spread
        tile_ref[pl.ds(c, leaves, stride=8), :] = spread
        tile_ref[pl.ds(c + 4, leaves, stride=8), :] = spread

    def leaf_pair(i, carry):
        columns = pl.ds(pl.multiple_of(i * rank2, rank2), rank2)
        q = charges_ref[:, columns]
        u = basis_ref[:, columns]
        zero = jnp.zeros_like(q)
        stacked = jnp.concatenate([jnp.where(low, q, zero), jnp.where(low, zero, q)], axis=0)
        product = dot_t(stacked, jnp.concatenate([u, u], axis=0)).astype(BF16)
        moment_ref[2 * i] = product[:rhs]
        moment_ref[2 * i + 1] = product[rhs:]
        return carry

    lax.fori_loop(0, leaves // 2, leaf_pair, 0, unroll=8)

    low8 = low_half((8, rank2))
    top8 = lax.broadcasted_iota(jnp.int32, (8, rank2), 0) < 4

    def pack(p, carry):
        s = [send_ref[t, p] for t in range(slots)]
        tiles = []
        for q in range(slots // 2):
            out_ref[p, q * rhs : (q + 1) * rhs, :] = pair(low, moment_ref[s[2 * q]], moment_ref[s[2 * q + 1]])
            a = tile_ref[pl.ds(pl.multiple_of(s[2 * q] * 8, 8), 8), :]
            b = tile_ref[pl.ds(pl.multiple_of(s[2 * q + 1] * 8, 8), 8), :]
            tiles.append(pair(low8, a, b))
        out_ref[p, slots // 2 * rhs :, :] = jnp.where(top8, tiles[0], tiles[1]).astype(BF16)
        return carry

    lax.fori_loop(0, devices, pack, 0, unroll=4)


def relayout(x_ref, scratch_ref):
    rank, _, leaves = x_ref.shape
    half = rank // 2
    eye = (
        lax.broadcasted_iota(jnp.int32, (leaves, leaves), 0)
        == lax.broadcasted_iota(jnp.int32, (leaves, leaves), 1)
    ).astype(BF16)
    for k in range(0, half, 2):
        block = jnp.concatenate(
            [x_ref[k], x_ref[k + half], x_ref[k + 1], x_ref[k + 1 + half]], axis=0
        )
        turned = dot_t(eye, block)
        for n in range(2):
            scratch_ref[pl.ds(k + n, leaves, stride=half), :] = turned[:, n * 2 * rank : (n + 1) * 2 * rank]


def spread_rows(block, low):
    zero = jnp.zeros_like(block)
    return jnp.concatenate([jnp.where(low, block, zero), jnp.where(low, zero, block)], axis=0)


def upward_kernel(
    moment_ref, up_leaf_ref, up_branch_ref, up_device_ref, pbranch_ref, pdevice_ref, out_ref, scratch_ref, branch_ref
):
    leaves, rhs, rank2 = moment_ref.shape
    rank = rank2 // 2
    half = rank // 2
    branches = leaves // FAN
    relayout(up_leaf_ref, scratch_ref)
    low = low_half((half, rank2))
    low_m = low_half((rhs, rank2))
    wide = up_branch_ref[...].astype(F32).reshape(rank * branches, rank)
    branch_ref[...] = twice(wide)
    m_device = jnp.zeros((rhs, rank), F32)
    previous = None
    for c in range(branches):
        blocks, moments = [], []
        for b in range(c * FAN, (c + 1) * FAN):
            block = scratch_ref[b * half : (b + 1) * half, :].astype(BF16)
            blocks.append(spread_rows(block, low))
            moments.append(moment_ref[b])
        m_branch = dot_t(jnp.concatenate(moments, axis=1), jnp.concatenate(blocks, axis=1)).astype(BF16)
        matrix = branch_ref[pl.ds(c, rank, stride=branches), :][:, :rank].astype(BF16)
        m_device = m_device + dot_t(m_branch, matrix)
        spread = twice(m_branch)
        if c % 2 == 1:
            out_ref[(c // 2) * rhs : (c // 2 + 1) * rhs, :] = pair(low_m, previous, spread)
        previous = spread
    m_device = m_device.astype(BF16)
    base = branches // 2 * rhs
    proxies = jnp.concatenate(
        [
            pdevice_ref[...].astype(F32),
            jnp.zeros((5, rank), F32),
            pbranch_ref[...].astype(F32).reshape(3 * branches, rank),
        ],
        axis=0,
    )
    out_ref[base : base + rhs, :] = jnp.concatenate([m_device.astype(F32), proxies], axis=1).astype(BF16)
    share = dot_t(m_device, up_device_ref[...])
    high = share.astype(BF16).astype(F32)
    out_ref[base + rhs : base + 2 * rhs, :] = jnp.concatenate([high, share - high], axis=1).astype(BF16)


def near_kernel(
    near_ref, charges_ref, points_ref, left_ref, right_ref, down_leaf_ref, out_ref, down_ref,
    wide_ref, source_ref, target_ref, scratch_ref, count_ref, weight_ref,
):
    rhs, total = charges_ref.shape
    entries, leaves = near_ref.shape
    size = total // leaves
    halo = REACH * size
    span = 2 * REACH + 1
    reach = (span + 1) * size
    relayout(down_leaf_ref, scratch_ref)
    down_ref[...] = scratch_ref[...].astype(BF16)

    wide_ref[:, :halo] = left_ref[:rhs, :]
    wide_ref[:, halo : halo + total] = charges_ref[...]
    wide_ref[:, halo + total :] = right_ref[:rhs, :]
    coords = [
        jnp.concatenate(
            [left_ref[rhs + c : rhs + c + 1, :], points_ref[c : c + 1, :], right_ref[rhs + c : rhs + c + 1, :]], axis=1
        ).astype(F32)
        for c in range(3)
    ]
    rows = source_rows(*coords)
    rows = rows + (jnp.zeros((FEATURES - len(rows), coords[0].shape[1]), F32),)
    source_ref[...] = jnp.concatenate(rows, axis=0).astype(BF16)
    rows = target_rows(*[c[:, halo : halo + total] for c in coords])
    rows = rows + (jnp.zeros((FEATURES - len(rows), total), F32),)
    target_ref[...] = jnp.concatenate(rows, axis=0).astype(BF16)

    near = near_ref[...]
    counts = [jnp.sum((near == o - REACH).astype(F32), axis=0, keepdims=True) for o in range(span)]
    counts = jnp.concatenate(counts + [jnp.zeros((FEATURES - span, leaves), F32)], axis=0).astype(BF16)
    offset = lax.broadcasted_iota(jnp.int32, (FEATURES, reach), 0)
    block = lax.broadcasted_iota(jnp.int32, (FEATURES, reach), 1) // size
    for h in range(2):
        weight_ref[h] = dot_0(counts, (block == offset + h).astype(BF16))

    low = low_half((rhs, 2 * size))

    def leaf_pair(i, carry):
        start = pl.multiple_of(i * 2 * size, 2 * size)
        square = dot_0(target_ref[:, pl.ds(start, 2 * size)], source_ref[:, pl.ds(start, reach)])
        kern = kern_of(square)
        x = wide_ref[:, pl.ds(start, reach)].astype(F32)
        parts = []
        for h in range(2):
            scaled = x * weight_ref[h, pl.ds(2 * i + h, 1), :]
            high = scaled.astype(BF16)
            parts += [high, (scaled - high.astype(F32)).astype(BF16)]
        product = dot_t(jnp.concatenate(parts, axis=0), kern)
        first = product[:rhs] + product[rhs : 2 * rhs]
        second = product[2 * rhs : 3 * rhs] + product[3 * rhs :]
        out_ref[:, pl.ds(start, 2 * size)] = pair(low, first, second)
        return carry

    lax.fori_loop(0, leaves // 2, leaf_pair, 0, unroll=2)


def group_kernel(*refs, members):
    far_ref, pgroup_ref = refs[:2]
    parts = refs[2 : 2 + members]
    fb_ref, ld_ref, out_ref = refs[2 + members : 5 + members]
    moment_ref, coord_ref, rows_ref, source_ref, dev_m_ref, dev_coord_ref, dev_rows_ref, dev_source_ref = refs[5 + members :]
    entries, branches = far_ref.shape
    rhs, rank2 = moment_ref.shape[1:]
    rank = rank2 // 2
    base = branches // 2 * rhs
    me = lax.axis_index("dev")
    low = low_half((rhs, rank2))
    m_group = jnp.zeros((rhs, rank), F32)
    for s, part in enumerate(parts):
        owner = lax.rem(me - s + members, members)
        for q in range(branches // 2):
            tile = part[q * rhs : (q + 1) * rhs, :]
            other = swap(tile)
            moment_ref[owner * branches + 2 * q] = pair(low, tile, other)
            moment_ref[owner * branches + 2 * q + 1] = pair(low, other, tile)
        mixed = part[base : base + rhs, :].astype(F32)
        turned = pltpu.roll(mixed, rank, 1)
        keep = (jnp.abs(owner - me) >= 2).astype(F32)
        dev_m_ref[owner] = (pair(low, mixed, turned) * keep).astype(BF16)
        spread = pair(low, turned, mixed)
        for c in range(3):
            rows = pl.ds(pl.multiple_of(owner * branches, branches), branches)
            coord_ref[c, rows, :] = spread[8 + c * branches : 8 + (c + 1) * branches, :]
            dev_coord_ref[c, pl.ds(owner, 1), :] = spread[c : c + 1, :]
        share = part[base + rhs : base + 2 * rhs, :].astype(F32)
        m_group = m_group + (share + pltpu.roll(share, rank, 1))[:, :rank]
    group_proxies = jnp.concatenate([pgroup_ref[...].astype(F32), jnp.zeros((rhs - 3, rank), F32)], axis=0)
    out_ref[...] = jnp.concatenate([m_group.astype(BF16).astype(F32), group_proxies], axis=1).astype(BF16)

    count = members * branches
    put_rows(rows_ref, source_rows(*[coord_ref[c] for c in range(3)]), 0, count, 1)
    source_ref[...] = rows_ref[...].astype(BF16).reshape(source_ref.shape)
    put_rows(dev_rows_ref, source_rows(*[dev_coord_ref[c] for c in range(3)]), 0, members, 1)
    dev_source_ref[...] = dev_rows_ref[...].astype(BF16).reshape(dev_source_ref.shape)

    def targets(x, y, z):
        rows = target_rows(x, y, z)
        rows = rows + (jnp.zeros((FEATURES - len(rows), rank), F32),)
        return jnp.concatenate(rows, axis=0).astype(BF16)

    mixed = parts[0][base : base + rhs, :].astype(F32)[:, rank:]
    for c in range(branches):
        target = targets(*[mixed[8 + a * branches + c : 9 + a * branches + c, :] for a in range(3)])
        fb_ref[c] = interact(target, [far_ref[e, c] for e in range(entries)], source_ref, moment_ref)
    target = targets(*[mixed[a : a + 1, :] for a in range(3)])
    ld_ref[...] = interact(target, list(range(members)), dev_source_ref, dev_m_ref)


def downward_kernel(*refs, groups):
    far_ref = refs[0]
    tiles = refs[1 : 1 + groups]
    (
        fb_ref, ld_ref, down_device_ref, down_branch_ref, down_ref, own_ref, own_m_ref, recv_ref, basis_ref, near_ref,
        out_ref, moment_ref, rows_ref, source_ref, trows_ref, target_ref, coord_ref, grp_m_ref, grp_coord_ref,
        grp_rows_ref, grp_source_ref, branch_ref, parent_ref,
    ) = refs[1 + groups :]
    entries, leaves = far_ref.shape
    rhs, rank2 = moment_ref.shape[1:]
    rank = rank2 // 2
    half = rank // 2
    branches = leaves // FAN
    devices = recv_ref.shape[0]
    slots = (moment_ref.shape[0] - leaves) // devices
    me = lax.axis_index("grp")
    low = low_half((rhs, rank2))

    for s, tile_ref in enumerate(tiles):
        owner = lax.rem(me - s + groups, groups)
        mixed = tile_ref[...].astype(F32)
        turned = pltpu.roll(mixed, rank, 1)
        keep = (jnp.abs(owner - me) >= 2).astype(F32)
        grp_m_ref[owner] = (pair(low, mixed, turned) * keep).astype(BF16)
        spread = pair(low, turned, mixed)
        for c in range(3):
            grp_coord_ref[c, pl.ds(owner, 1), :] = spread[c : c + 1, :]
    put_rows(grp_rows_ref, source_rows(*[grp_coord_ref[c] for c in range(3)]), 0, groups, 1)
    grp_source_ref[...] = grp_rows_ref[...].astype(BF16).reshape(grp_source_ref.shape)
    mixed = tiles[0][...].astype(F32)[:, rank:]
    rows = target_rows(*[mixed[a : a + 1, :] for a in range(3)])
    rows = rows + (jnp.zeros((FEATURES - len(rows), rank), F32),)
    target = jnp.concatenate(rows, axis=0).astype(BF16)
    l_group = interact(target, list(range(groups)), grp_source_ref, grp_m_ref).astype(BF16)
    l_device = (ld_ref[...] + dot_t(l_group, down_device_ref[...])).astype(BF16)
    branch_ref[...] = twice(down_branch_ref[...].astype(F32).reshape(rank * branches, rank))
    for c in range(branches):
        matrix = branch_ref[pl.ds(c, rank, stride=branches), :][:, :rank].astype(BF16)
        parent_ref[c] = twice((fb_ref[c] + dot_t(l_device, matrix)).astype(BF16))

    moment_ref[:leaves] = own_m_ref[...]

    def unpack(p, carry):
        for q in range(slots // 2):
            tile = recv_ref[p, q * rhs : (q + 1) * rhs, :]
            other = swap(tile)
            moment_ref[leaves + p * slots + 2 * q] = pair(low, tile, other)
            moment_ref[leaves + p * slots + 2 * q + 1] = pair(low, other, tile)
        coord_ref[pl.ds(pl.multiple_of(p * 8, 8), 8), :] = recv_ref[p, slots // 2 * rhs :, :].astype(F32)
        return carry

    lax.fori_loop(0, devices, unpack, 0, unroll=4)
    own = [own_ref[c] for c in range(3)]
    put_rows(rows_ref, source_rows(*own), 0, leaves, 1)
    put_rows(trows_ref, target_rows(*own), 0, leaves, 1)
    target_ref[...] = trows_ref[...].astype(BF16).reshape(target_ref.shape)
    low_p = low_half((devices, rank2))
    for q in range(slots // 2):
        found = [coord_ref[pl.ds(q * 4 + c, devices, stride=8), :] for c in range(3)]
        other = [pltpu.roll(v, rank, 1) for v in found]
        put_rows(rows_ref, source_rows(*[pair(low_p, v, o) for v, o in zip(found, other)]), leaves + 2 * q, devices, slots)
        put_rows(rows_ref, source_rows(*[pair(low_p, o, v) for v, o in zip(found, other)]), leaves + 2 * q + 1, devices, slots)
    source_ref[...] = rows_ref[...].astype(BF16).reshape(source_ref.shape)

    low_d = low_half((half, rank2))

    def leaf_pair(i, carry):
        sums = []
        for h in range(2):
            b = 2 * i + h
            far = interact(target_ref[b][:, :rank], [far_ref[e, b] for e in range(entries)], source_ref, moment_ref)
            rows = down_ref[pl.ds(pl.multiple_of(b * half, half), half), :]
            parent = parent_ref[b // FAN]
            sums.append((far + dot_t(parent, spread_rows(rows, low_d))).astype(BF16))
        columns = pl.ds(pl.multiple_of(i * rank2, rank2), rank2)
        product = dot(jnp.concatenate(sums, axis=0), basis_ref[:, columns])
        out_ref[:, columns] = near_ref[:, columns] + pair(low, product[:rhs], product[rhs:])
        return carry

    lax.fori_loop(0, leaves // 2, leaf_pair, 0)


VMEM = functools.partial(pl.BlockSpec, memory_space=pltpu.VMEM)
SMEM = functools.partial(pl.BlockSpec, memory_space=pltpu.SMEM)


def struct(shape, dtype):
    return jax.ShapeDtypeStruct(shape, dtype)


def on_device(
    charges, points, basis, up_leaf, up_branch, up_device, down_leaf, down_branch, down_device,
    proxy_leaf, proxy_branch, proxy_device, proxy_group, far_leaf, send_leaf, far_branch, near_leaf,
):
    rhs, total = charges.shape
    rank = basis.shape[0]
    leaves = up_leaf.shape[2]
    size = total // leaves
    branches = leaves // FAN
    slots = send_leaf.shape[0]
    groups = lax.axis_size("grp")
    members = lax.axis_size("dev")
    devices = groups * members
    rank2 = 2 * rank
    half = rank // 2
    halo = REACH * size
    assert rank == size and slots == 4 and rhs == 3 * branches + 8

    moments, own, listed = pl.pallas_call(
        listed_kernel,
        out_shape=(
            struct((leaves, rhs, rank2), BF16),
            struct((3, leaves, rank2), F32),
            struct((devices, slots // 2 * rhs + 8, rank2), BF16),
        ),
        in_specs=[SMEM(), VMEM(), VMEM(), VMEM()],
        out_specs=(VMEM(), VMEM(), VMEM()),
        scratch_shapes=[pltpu.VMEM((leaves * 8, rank2), F32)],
        name="listed",
    )(send_leaf, charges, basis, proxy_leaf)
    received = lax.all_to_all(listed, ("grp", "dev"), split_axis=0, concat_axis=0, tiled=True)

    stacked = jnp.concatenate([charges, points], axis=0)
    last = devices - 1
    left = lax.ppermute(stacked[:, total - halo :], ("grp", "dev"), [(i, i + 1) for i in range(last)])
    right = lax.ppermute(stacked[:, :halo], ("grp", "dev"), [(i + 1, i) for i in range(last)])

    shared = pl.pallas_call(
        upward_kernel,
        out_shape=struct((branches // 2 * rhs + 2 * rhs, rank2), BF16),
        in_specs=[VMEM()] * 6,
        out_specs=VMEM(),
        scratch_shapes=[pltpu.VMEM((leaves * half, rank2), F32), pltpu.VMEM((rank * branches, rank2), F32)],
        name="upward",
    )(
        moments,
        up_leaf,
        jnp.transpose(up_branch, (0, 2, 1)),
        up_device[:, :, 0],
        jnp.transpose(proxy_branch, (0, 2, 1)),
        proxy_device[:, :, 0],
    )
    parts = [shared] + [
        lax.ppermute(shared, "dev", [(i, (i + s) % members) for i in range(members)]) for s in range(1, members)
    ]

    reach = (2 * REACH + 2) * size
    near, down = pl.pallas_call(
        near_kernel,
        out_shape=(struct((rhs, total), F32), struct((leaves * half, rank2), BF16)),
        in_specs=[VMEM()] * 6,
        out_specs=(VMEM(), VMEM()),
        scratch_shapes=[
            pltpu.VMEM((rhs, total + 2 * halo), BF16),
            pltpu.VMEM((FEATURES, total + 2 * halo), BF16),
            pltpu.VMEM((FEATURES, total), BF16),
            pltpu.VMEM((leaves * half, rank2), F32),
            pltpu.VMEM((8, 128), F32),
            pltpu.VMEM((2, leaves, reach), F32),
        ],
        name="near",
    )(near_leaf, charges, points, left, right, down_leaf)

    far_b, part_d, tile = pl.pallas_call(
        functools.partial(group_kernel, members=members),
        out_shape=(struct((branches, rhs, rank), F32), struct((rhs, rank), F32), struct((rhs, rank2), BF16)),
        in_specs=[SMEM(), VMEM()] + [VMEM()] * members,
        out_specs=(VMEM(), VMEM(), VMEM()),
        scratch_shapes=[
            pltpu.VMEM((members * branches, rhs, rank2), BF16),
            pltpu.VMEM((3, members * branches, rank2), F32),
            pltpu.VMEM((members * branches * FEATURES, rank2), F32),
            pltpu.VMEM((members * branches, FEATURES, rank2), BF16),
            pltpu.VMEM((members, rhs, rank2), BF16),
            pltpu.VMEM((3, members, rank2), F32),
            pltpu.VMEM((members * FEATURES, rank2), F32),
            pltpu.VMEM((members, FEATURES, rank2), BF16),
        ],
        name="group",
    )(far_branch, proxy_group[:, :, 0], *parts)
    tiles = [tile] + [
        lax.ppermute(tile, "grp", [(i, (i + s) % groups) for i in range(groups)]) for s in range(1, groups)
    ]

    table = leaves + devices * slots
    return pl.pallas_call(
        functools.partial(downward_kernel, groups=groups),
        out_shape=struct((rhs, total), F32),
        in_specs=[SMEM()] + [VMEM()] * (groups + 10),
        out_specs=VMEM(),
        scratch_shapes=[
            pltpu.VMEM((table, rhs, rank2), BF16),
            pltpu.VMEM((table * FEATURES, rank2), F32),
            pltpu.VMEM((table, FEATURES, rank2), BF16),
            pltpu.VMEM((leaves * FEATURES, rank2), F32),
            pltpu.VMEM((leaves, FEATURES, rank2), BF16),
            pltpu.VMEM((devices * 8, rank2), F32),
            pltpu.VMEM((groups, rhs, rank2), BF16),
            pltpu.VMEM((3, groups, rank2), F32),
            pltpu.VMEM((groups * FEATURES, rank2), F32),
            pltpu.VMEM((groups, FEATURES, rank2), BF16),
            pltpu.VMEM((rank * branches, rank2), F32),
            pltpu.VMEM((branches, rhs, rank2), BF16),
        ],
        name="downward",
    )(
        far_leaf, *tiles, far_b, part_d, down_device[:, :, 0], jnp.transpose(down_branch, (0, 2, 1)), down, own,
        moments, received, basis, near,
    )


def solution(mesh):
    points = P(None, ("grp", "dev"))
    blocks = P(None, None, ("grp", "dev"))
    placed = (points,) * 3 + (blocks,) * 9 + (P(None, None, "grp"),) + (points,) * 4
    return jax.shard_map(on_device, mesh=mesh, in_specs=placed, out_specs=points, check_vma=False)
```

time: 457 us -> 88.7 us (0.19)
  blocking collectives: 150 us -> 0 us
  other arithmetic: 134 us -> 0 us
  local copies, waits for them, and re-layouts: 118 us -> 4.81 us
  Pallas kernels: 0 us -> 50.6 us
  matrix products: 34.5 us -> 0 us
  starting transfers between devices: 19.1 us -> 26.3 us
  waiting for transfers between devices: 0.01 us -> 5.85 us
    all_gather x7 -> x0, blocking collectives: 150 us -> none  [the longest x1 31.2 us: on_device(): lax.all_gather(m_branch, 'dev', axis=2, tiled=True)]
    reduce_sum x5 -> x0, other arithmetic: 70.6 us -> none  [kernel_block(): square = jnp.sum(delta * delta, axis=0)]
    convert_element_type x9 -> x0, local copies, waits for them, and re-layouts: 59 us -> none  [the longest x2 53.7 us: kernel_block(): return (INV_FOUR_PI * lax.rsqrt(square + SOFTEN)).astype(jnp.bfloat16)]
    pallas_call x0 -> x5, Pallas kernels: none -> 50.6 us  [the longest x1 26.5 us: on_device(): pl.pallas_call(functools.partial(downward_kernel, groups=groups), out_sha...]
    convert_element_type x11 -> x0, other arithmetic: 43.9 us -> none  [the longest x3 38.5 us: kernel_block(): return (INV_FOUR_PI * lax.rsqrt(square + SOFTEN)).astype(jnp.bfloat16)]
    dot_general x11 -> x0, matrix products: 34.5 us -> none  [the longest x1 11.8 us: leaf_step(): jnp.einsum('kjeb,rjeb->rkb', kern, src_m, preferred_element_type=jnp.floa...]
    gather x8 -> x0, local copies, waits for them, and re-layouts: 27.5 us -> none  [the longest x1 11 us: leaf_step(): source = jnp.take(wide, rows, axis=1)]
    ppermute x2 -> x12, starting transfers between devices: 7.41 us -> 20.3 us  [the longest x7 12.7 us: on_device(): lax.ppermute(shared, 'dev', [(i, (i + s) % members) for i in range(member...]
  transfers between devices with their start and end apart: 4 -> 13, of which waited for: 0 -> 2; matrix products, arithmetic and copies ran while one was open for 54% -> 1% of each run, Pallas kernels for 0% -> 19%
where the time goes in v1:
time: 88.7 us; the launch traced here: 87.8 us
  Pallas kernels  50.6 us (57%)
  starting transfers between devices  26.3 us (30%)
  waiting for transfers between devices  5.85 us (7%)
  local copies, waits for them, and re-layouts  4.81 us (5%)
    pallas_call x1, Pallas kernels, on_device(): pl.pallas_call(functools.partial(downward_kernel, groups=groups), out_sha...  26.5 us
    pallas_call x1, Pallas kernels, on_device(): pl.pallas_call(near_kernel, out_shape=(struct((rhs, total), F32), struct(...  13.6 us
    ppermute x7, starting transfers between devices, on_device(): lax.ppermute(shared, 'dev', [(i, (i + s) % members) for i in range(member...  12.7 us
    all_to_all x1, starting transfers between devices, on_device(): lax.all_to_all(listed, ('grp', 'dev'), split_axis=0, concat_axis=0, tiled...  6.07 us
    ppermute x7, waiting for transfers between devices, on_device(): lax.ppermute(shared, 'dev', [(i, (i + s) % members) for i in range(member...  5.84 us
    unnamed x36, local copies, waits for them, and re-layouts  4.78 us
    ppermute x1, starting transfers between devices, on_device(): lax.ppermute(stacked[:, total - halo:], ('grp', 'dev'), [(i, i + 1) for i...  4.55 us
    pallas_call x1, Pallas kernels, on_device(): pl.pallas_call(upward_kernel, out_shape=struct((branches // 2 * rhs + 2 *...  3.84 us
  transfers between devices with their start and end apart: 13, of which 2 were waited for; matrix products, arithmetic and copies ran while one was open for 1% of the time, Pallas kernels for 19%

profile of v1, /device:TPU:0, one launch (start us, length us, event | category | flops | bytes accessed | tf_op | source)
XLA Modules:
  0.0 87.8 jit_solution(13230558997909540785)
XLA Ops:
  0.0 3.8 %listed.1 = (bf16[64,32,128]{2,1,0:T(8,128)(2,1)}, f32[3,64,128]{2,1,0:T(8,128)}, bf16[32,72,128]{2,1,0:T(8,128)(2,1)}) custom-call(s32[4,32]{1,0:T(4,128)} %send_ref.1, bf16[32,4096]{1,0:T(8,128)(2,1)} %charges_ref.3, bf16[64,4096]{1,0:T(8,128)(2,1)} %refs_13_.1, bf16[3,64,64]{2,1,0:T(8,128)(2,1)} %proxy_ref.1), custom_call_target="tpu_custom_call" | custom-call | tf_op jit(solution)/shard_map/listed/pallas_call | solution.py:415
  3.8 3.8 %upward.1.refs_2_ = bf16[192,128]{1,0:T(8,128)(2,1)} custom-call(bf16[64,32,128]{2,1,0:T(8,128)(2,1)} %get-tuple-element.13.moment_ref.refs_11_, bf16[64,64,64]{2,1,0:T(8,128)(2,1)} %up_leaf_ref.1, bf16[64,8,64]{2,1,0:T(8,128)(2,1)} %bitcast.8, bf16[64,64]{1,0:T(8,128)(2,1)} %bitcast.9, bf16[3,8,64]{2,1,0:T(8,128)(2,1)} %bitcast.11, bf16[3,64]{1,0:T(4,128)(2,1)} %bitcast.12), custom_call_target="tpu_custom_call" | custom-call | tf_op jit(solution)/shard_map/upward/pallas_call | solution.py:434
  7.7 6.0 %collective-permute-start.6 = (bf16[192,128]{1,0:T(8,128)(2,1)}, bf16[192,128]{1,0:T(8,128)(2,1)S(1)}, u32[]{:S(2)}, u32[]{:S(2)}) collective-permute-start(bf16[192,128]{1,0:T(8,128)(2,1)} %upward.1.refs_2_), channel_id=1, source_target_pairs={{0,7},{1,0},{2,1},{3,2},{4,3},{5,4},{6,5},{7,6},{8,15},{9,8},{10,9... | collective-permute-start | bytes 147464 | tf_op jit(solution)/shard_map/ppermute | solution.py:450
  13.7 0.5 collective-permute-start.5
  14.2 3.0 %collective-permute-start.3 = (bf16[192,128]{1,0:T(8,128)(2,1)}, bf16[192,128]{1,0:T(8,128)(2,1)S(1)}, u32[]{:S(2)}, u32[]{:S(2)}) collective-permute-start(bf16[192,128]{1,0:T(8,128)(2,1)} %upward.1.refs_2_), channel_id=1, source_target_pairs={{0,4},{1,5},{2,6},{3,7},{4,0},{5,1},{6,2},{7,3},{8,12},{9,13},{10,... | collective-permute-start | bytes 147464 | tf_op jit(solution)/shard_map/ppermute | solution.py:450
  17.1 6.1 %all-to-all-start = ((bf16[32,72,128]{2,1,0:T(8,128)(2,1)}), bf16[32,72,128]{2,1,0:T(8,128)(2,1)S(1)}, u32[]{:S(2)}, u32[]{:S(2)}) async-start(bf16[32,72,128]{2,1,0:T(8,128)(2,1)} %get-tuple-element.19), calls=%async_computation | async-start | bytes 1179648 | tf_op jit(solution)/shard_map/all_to_all | solution.py:427
  23.3 0.7 copy-done.3
  24.0 0.8 copy-done.2
  24.8 1.8 %collective-permute-start.1 = (bf16[192,128]{1,0:T(8,128)(2,1)S(1)}, bf16[192,128]{1,0:T(8,128)(2,1)S(1)}, u32[]{:S(2)}, u32[]{:S(2)}) collective-permute-start(bf16[192,128]{1,0:T(8,128)(2,1)S(1)} %copy-done.2), channel_id=1, source_target_pairs={{0,2},{1,3},{2,4},{3,5},{4,6},{5,7},{6,0},{7,1},{8,10},{9,11},{10,... | collective-permute-start | bytes 147464 | tf_op jit(solution)/shard_map/ppermute | solution.py:450
  26.6 1.5 %collective-permute-start = (bf16[192,128]{1,0:T(8,128)(2,1)S(1)}, bf16[192,128]{1,0:T(8,128)(2,1)S(1)}, u32[]{:S(2)}, u32[]{:S(2)}) collective-permute-start(bf16[192,128]{1,0:T(8,128)(2,1)S(1)} %copy-done.2), channel_id=1, source_target_pairs={{0,1},{1,2},{2,3},{3,4},{4,5},{5,6},{6,7},{7,0},{8,9},{9,10},{10,1... | collective-permute-start | bytes 147464 | tf_op jit(solution)/shard_map/ppermute | solution.py:450
  28.1 1.3 %collective-permute-start.11 = (bf16[35,256]{1,0:T(8,128)(2,1)S(1)}, bf16[35,256]{1,0:T(8,128)(2,1)S(1)}, u32[]{:S(2)}, u32[]{:S(2)}) collective-permute-start(bf16[35,256]{1,0:T(8,128)(2,1)S(1)} %get-tuple-element.21), channel_id=1, source_target_pairs={{1,0},{2,1},{3,2},{4,3},{5,4},{6,5},{7,6},{8,7},{9,8},{10,9},{11,1... | collective-permute-start | bytes 53768 | tf_op jit(solution)/shard_map/ppermute | solution.py:432
  29.4 4.5 %collective-permute-start.10 = (bf16[35,256]{1,0:T(8,128)(2,1)S(1)}, bf16[35,256]{1,0:T(8,128)(2,1)S(1)}, u32[]{:S(2)}, u32[]{:S(2)}) collective-permute-start(bf16[35,256]{1,0:T(8,128)(2,1)S(1)} %get-tuple-element.22), channel_id=1, source_target_pairs={{0,1},{1,2},{2,3},{3,4},{4,5},{5,6},{6,7},{7,8},{8,9},{9,10},{10,1... | collective-permute-start | bytes 53768 | tf_op jit(solution)/shard_map/ppermute | solution.py:431
  34.0 0.7 copy.18.refs_0_
  34.6 4.1 %collective-permute-done.1.refs_4_ = bf16[192,128]{1,0:T(8,128)(2,1)S(1)} collective-permute-done((bf16[192,128]{1,0:T(8,128)(2,1)S(1)}, bf16[192,128]{1,0:T(8,128)(2,1)S(1)}, u32[]{:S(2)}, u32[]{:S(2)}) %collective-permute-start.1) | collective-permute-done | bytes 49184 | tf_op jit(solution)/shard_map/ppermute | solution.py:450
  38.7 1.8 %collective-permute-done.refs_3_ = bf16[192,128]{1,0:T(8,128)(2,1)S(1)} collective-permute-done((bf16[192,128]{1,0:T(8,128)(2,1)S(1)}, bf16[192,128]{1,0:T(8,128)(2,1)S(1)}, u32[]{:S(2)}, u32[]{:S(2)}) %collective-permute-start) | collective-permute-done | bytes 49184 | tf_op jit(solution)/shard_map/ppermute | solution.py:450
  40.5 0.6 copy-done.10
  41.1 2.9 %group.1 = (f32[8,32,64]{2,1,0:T(8,128)}, f32[32,64]{1,0:T(8,128)}, bf16[32,128]{1,0:T(8,128)(2,1)}) custom-call(s32[16,8]{1,0:T(8,128)} %copy.18.refs_0_, bf16[3,64]{1,0:T(4,128)(2,1)} %bitcast.13, bf16[192,128]{1,0:T(8,128)(2,1)} %upward.1.refs_2_, bf16[192,128]{1,0:T(8,128)(2,1)} %copy-done.10, bf16[192,128]{1,0:T(8,128)(2,1)} %copy-done.9, ...), custom_call_target="tpu_custom_call" | custom-call | tf_op jit(solution)/shard_map/group/pallas_call | solution.py:470
  43.9 0.3 collective-permute-start.9
  44.3 1.2 %collective-permute-start.8 = (bf16[32,128]{1,0:T(8,128)(2,1)}, bf16[32,128]{1,0:T(8,128)(2,1)S(1)}, u32[]{:S(2)}, u32[]{:S(2)}) collective-permute-start(bf16[32,128]{1,0:T(8,128)(2,1)} %get-tuple-element.14.refs_1_), channel_id=1, source_target_pairs={{0,16},{8,24},{16,0},{24,8},{1,17},{9,25},{17,1},{25,9},{2,18},{10... | collective-permute-start | bytes 24584 | tf_op jit(solution)/shard_map/ppermute | solution.py:488
  45.6 0.6 copy-done.11
  46.2 0.6 copy-done.12
  46.8 13.6 %near.1 = (f32[32,4096]{1,0:T(8,128)}, bf16[2048,128]{1,0:T(8,128)(2,1)}) custom-call(s32[16,64]{1,0:T(8,128)} %near_ref.1, bf16[32,4096]{1,0:T(8,128)(2,1)} %charges_ref.3, bf16[3,4096]{1,0:T(4,128)(2,1)} %points_ref.1, bf16[35,256]{1,0:T(8,128)(2,1)} %copy-done.12, bf16[35,256]{1,0:T(8,128)(2,1)} %copy-done.11, bf16[64,64,64]{2,1,0:T(8,128)(2,1)} %down_leaf_ref.1), custom_call_target="tpu_custom_call" | custom-call | tf_op jit(solution)/shard_map/near/pallas_call | solution.py:454
  60.5 0.5 copy-done.13
  61.3 26.5 %downward.1 = f32[32,4096]{1,0:T(8,128)} custom-call(s32[16,64]{1,0:T(8,128)} %refs_0_.2, bf16[32,128]{1,0:T(8,128)(2,1)} %get-tuple-element.14.refs_1_, bf16[32,128]{1,0:T(8,128)(2,1)} %copy-done.15, bf16[32,128]{1,0:T(8,128)(2,1)} %copy-done.14, bf16[32,128]{1,0:T(8,128)(2,1)} %copy-done.13, f32[8,32,64]{2,1,0:T(8,128)} %get-tuple-element.15.refs_5_, ...), custom_call_target="tpu_custom_call" | custom-call | tf_op jit(solution)/shard_map/downward/pallas_call | solution.py:492
  (45 shorter events, 0.6 us)
Async XLA Ops:
  7.7 16.4 %collective-permute-start.6 = (bf16[192,128]{1,0:T(8,128)(2,1)}, bf16[192,128]{1,0:T(8,128)(2,1)S(1)}, u32[]{:S(2)}, u32[]{:S(2)}) collective-permute-start(bf16[192,128]{1,0:T(8,128)(2,1)} %upward.1.refs_2_), channel_id=1, source_target_pairs={{0,7},{1,0},{2,1},{3,2},{4,3},{5,4},{6,5},{7,6},{8,15},{9,8},{10,9... | collective-permute-start | bytes 147464 | tf_op jit(solution)/shard_map/ppermute | solution.py:450
  13.7 12.9 %collective-permute-start.5 = (bf16[192,128]{1,0:T(8,128)(2,1)}, bf16[192,128]{1,0:T(8,128)(2,1)S(1)}, u32[]{:S(2)}, u32[]{:S(2)}) collective-permute-start(bf16[192,128]{1,0:T(8,128)(2,1)} %upward.1.refs_2_), channel_id=1, source_target_pairs={{0,6},{1,7},{2,0},{3,1},{4,2},{5,3},{6,4},{7,5},{8,14},{9,15},{10,... | collective-permute-start | bytes 147464 | tf_op jit(solution)/shard_map/ppermute | solution.py:450
  14.2 13.9 %collective-permute-start.4 = (bf16[192,128]{1,0:T(8,128)(2,1)}, bf16[192,128]{1,0:T(8,128)(2,1)S(1)}, u32[]{:S(2)}, u32[]{:S(2)}) collective-permute-start(bf16[192,128]{1,0:T(8,128)(2,1)} %upward.1.refs_2_), channel_id=1, source_target_pairs={{0,5},{1,6},{2,7},{3,0},{4,1},{5,2},{6,3},{7,4},{8,13},{9,14},{10,... | collective-permute-start | bytes 147464 | tf_op jit(solution)/shard_map/ppermute | solution.py:450
  14.2 15.2 %collective-permute-start.3 = (bf16[192,128]{1,0:T(8,128)(2,1)}, bf16[192,128]{1,0:T(8,128)(2,1)S(1)}, u32[]{:S(2)}, u32[]{:S(2)}) collective-permute-start(bf16[192,128]{1,0:T(8,128)(2,1)} %upward.1.refs_2_), channel_id=1, source_target_pairs={{0,4},{1,5},{2,6},{3,7},{4,0},{5,1},{6,2},{7,3},{8,12},{9,13},{10,... | collective-permute-start | bytes 147464 | tf_op jit(solution)/shard_map/ppermute | solution.py:450
  17.1 17.5 %collective-permute-start.2 = (bf16[192,128]{1,0:T(8,128)(2,1)}, bf16[192,128]{1,0:T(8,128)(2,1)S(1)}, u32[]{:S(2)}, u32[]{:S(2)}) collective-permute-start(bf16[192,128]{1,0:T(8,128)(2,1)} %upward.1.refs_2_), channel_id=1, source_target_pairs={{0,3},{1,4},{2,5},{3,6},{4,7},{5,0},{6,1},{7,2},{8,11},{9,12},{10,... | collective-permute-start | bytes 147464 | tf_op jit(solution)/shard_map/ppermute | solution.py:450
  17.1 6.1 %copy-start.1 = (bf16[32,4096]{1,0:T(8,128)(2,1)S(1)}, bf16[32,4096]{1,0:T(8,128)(2,1)}, u32[]{:S(2)}) copy-start(bf16[32,4096]{1,0:T(8,128)(2,1)} %charges_ref.3) | copy-start | bytes 786436
  17.1 43.3 %all-to-all-start = ((bf16[32,72,128]{2,1,0:T(8,128)(2,1)}), bf16[32,72,128]{2,1,0:T(8,128)(2,1)S(1)}, u32[]{:S(2)}, u32[]{:S(2)}) async-start(bf16[32,72,128]{2,1,0:T(8,128)(2,1)} %get-tuple-element.19), calls=%async_computation | async-start | bytes 1179648 | tf_op jit(solution)/shard_map/all_to_all | solution.py:427
  23.2 0.8 copy-start.3
  24.0 0.8 copy-start.2
  24.8 15.6 %copy-start.4 = (bf16[192,128]{1,0:T(8,128)(2,1)}, bf16[192,128]{1,0:T(8,128)(2,1)S(1)}, u32[]{:S(2)}) copy-start(bf16[192,128]{1,0:T(8,128)(2,1)S(1)} %collective-permute-done.6.refs_9_) | copy-start | bytes 147460
  24.8 13.9 %collective-permute-start.1 = (bf16[192,128]{1,0:T(8,128)(2,1)S(1)}, bf16[192,128]{1,0:T(8,128)(2,1)S(1)}, u32[]{:S(2)}, u32[]{:S(2)}) collective-permute-start(bf16[192,128]{1,0:T(8,128)(2,1)S(1)} %copy-done.2), channel_id=1, source_target_pairs={{0,2},{1,3},{2,4},{3,5},{4,6},{5,7},{6,0},{7,1},{8,10},{9,11},{10,... | collective-permute-start | bytes 147464 | tf_op jit(solution)/shard_map/ppermute | solution.py:450
  26.6 13.9 %copy-start.5 = (bf16[192,128]{1,0:T(8,128)(2,1)}, bf16[192,128]{1,0:T(8,128)(2,1)S(1)}, u32[]{:S(2)}) copy-start(bf16[192,128]{1,0:T(8,128)(2,1)S(1)} %collective-permute-done.5.refs_8_) | copy-start | bytes 147460
  26.6 13.9 %collective-permute-start = (bf16[192,128]{1,0:T(8,128)(2,1)S(1)}, bf16[192,128]{1,0:T(8,128)(2,1)S(1)}, u32[]{:S(2)}, u32[]{:S(2)}) collective-permute-start(bf16[192,128]{1,0:T(8,128)(2,1)S(1)} %copy-done.2), channel_id=1, source_target_pairs={{0,1},{1,2},{2,3},{3,4},{4,5},{5,6},{6,7},{7,0},{8,9},{9,10},{10,1... | collective-permute-start | bytes 147464 | tf_op jit(solution)/shard_map/ppermute | solution.py:450
  28.0 5.9 %copy-start.16 = (s32[16,8]{0,1:T(8,128)S(1)}, s32[16,8]{0,1:T(8,128)}, u32[]{:S(2)}) copy-start(s32[16,8]{0,1:T(8,128)} %param.32) | copy-start | bytes 1540
  28.1 12.4 %copy-start.6 = (bf16[192,128]{1,0:T(8,128)(2,1)}, bf16[192,128]{1,0:T(8,128)(2,1)S(1)}, u32[]{:S(2)}) copy-start(bf16[192,128]{1,0:T(8,128)(2,1)S(1)} %collective-permute-done.4.refs_7_) | copy-start | bytes 147460
  28.1 17.6 %collective-permute-start.11 = (bf16[35,256]{1,0:T(8,128)(2,1)S(1)}, bf16[35,256]{1,0:T(8,128)(2,1)S(1)}, u32[]{:S(2)}, u32[]{:S(2)}) collective-permute-start(bf16[35,256]{1,0:T(8,128)(2,1)S(1)} %get-tuple-element.21), channel_id=1, source_target_pairs={{1,0},{2,1},{3,2},{4,3},{5,4},{6,5},{7,6},{8,7},{9,8},{10,9},{11,1... | collective-permute-start | bytes 53768 | tf_op jit(solution)/shard_map/ppermute | solution.py:432
  29.4 11.1 %copy-start.7 = (bf16[192,128]{1,0:T(8,128)(2,1)}, bf16[192,128]{1,0:T(8,128)(2,1)S(1)}, u32[]{:S(2)}) copy-start(bf16[192,128]{1,0:T(8,128)(2,1)S(1)} %collective-permute-done.3.refs_6_) | copy-start | bytes 147460
  29.4 16.3 %collective-permute-start.10 = (bf16[35,256]{1,0:T(8,128)(2,1)S(1)}, bf16[35,256]{1,0:T(8,128)(2,1)S(1)}, u32[]{:S(2)}, u32[]{:S(2)}) collective-permute-start(bf16[35,256]{1,0:T(8,128)(2,1)S(1)} %get-tuple-element.22), channel_id=1, source_target_pairs={{0,1},{1,2},{2,3},{3,4},{4,5},{5,6},{6,7},{7,8},{8,9},{9,10},{10,1... | collective-permute-start | bytes 53768 | tf_op jit(solution)/shard_map/ppermute | solution.py:431
  34.6 5.9 %copy-start.8 = (bf16[192,128]{1,0:T(8,128)(2,1)}, bf16[192,128]{1,0:T(8,128)(2,1)S(1)}, u32[]{:S(2)}) copy-start(bf16[192,128]{1,0:T(8,128)(2,1)S(1)} %collective-permute-done.2.refs_5_) | copy-start | bytes 147460
  38.7 1.8 %copy-start.9 = (bf16[192,128]{1,0:T(8,128)(2,1)}, bf16[192,128]{1,0:T(8,128)(2,1)S(1)}, u32[]{:S(2)}) copy-start(bf16[192,128]{1,0:T(8,128)(2,1)S(1)} %collective-permute-done.1.refs_4_) | copy-start | bytes 147460
  43.9 16.5 %collective-permute-start.9 = (bf16[32,128]{1,0:T(8,128)(2,1)}, bf16[32,128]{1,0:T(8,128)(2,1)S(1)}, u32[]{:S(2)}, u32[]{:S(2)}) collective-permute-start(bf16[32,128]{1,0:T(8,128)(2,1)} %get-tuple-element.14.refs_1_), channel_id=1, source_target_pairs={{0,24},{8,0},{16,8},{24,16},{1,25},{9,1},{17,9},{25,17},{2,26},{10... | collective-permute-start | bytes 24584 | tf_op jit(solution)/shard_map/ppermute | solution.py:488
  44.3 16.1 %collective-permute-start.8 = (bf16[32,128]{1,0:T(8,128)(2,1)}, bf16[32,128]{1,0:T(8,128)(2,1)S(1)}, u32[]{:S(2)}, u32[]{:S(2)}) collective-permute-start(bf16[32,128]{1,0:T(8,128)(2,1)} %get-tuple-element.14.refs_1_), channel_id=1, source_target_pairs={{0,16},{8,24},{16,0},{24,8},{1,17},{9,25},{17,1},{25,9},{2,18},{10... | collective-permute-start | bytes 24584 | tf_op jit(solution)/shard_map/ppermute | solution.py:488
  45.5 15.0 %collective-permute-start.7 = (bf16[32,128]{1,0:T(8,128)(2,1)}, bf16[32,128]{1,0:T(8,128)(2,1)S(1)}, u32[]{:S(2)}, u32[]{:S(2)}) collective-permute-start(bf16[32,128]{1,0:T(8,128)(2,1)} %get-tuple-element.14.refs_1_), channel_id=1, source_target_pairs={{0,8},{8,16},{16,24},{24,0},{1,9},{9,17},{17,25},{25,1},{2,10},{10... | collective-permute-start | bytes 24584 | tf_op jit(solution)/shard_map/ppermute | solution.py:488
  60.5 0.8 copy-start
  (6 other events, 3.6 us)

commit v2 on v1

v2 whole, which is shorter than its diff:
```python
import functools
import math

import jax
import jax.numpy as jnp
from jax import lax
from jax.experimental import pallas as pl
from jax.experimental.pallas import tpu as pltpu
from jax.sharding import PartitionSpec as P

REACH = 4
FAN = 8

INV_FOUR_PI = 1.0 / (4.0 * math.pi)
SOFTEN = 0.25
ROWS = 8

BF16 = jnp.bfloat16
F32 = jnp.float32


def dot(a, b):
    return jnp.dot(a, b, preferred_element_type=F32)


def dot_t(a, b):
    return lax.dot_general(a, b, (((1,), (1,)), ((), ())), preferred_element_type=F32)


def dot_0(a, b):
    return lax.dot_general(a, b, (((0,), (0,)), ((), ())), preferred_element_type=F32)


def low_half(shape):
    width = shape[-1]
    return lax.broadcasted_iota(jnp.int32, shape, len(shape) - 1) < width // 2


def pair(low, first, second):
    return jnp.where(low, first, second)


def swap(tile):
    half = tile.shape[-1] // 2
    return jnp.concatenate([tile[..., half:], tile[..., :half]], axis=-1)


def twice(tile):
    return jnp.concatenate([tile, tile], axis=-1)


def three(value):
    first = value.astype(BF16).astype(F32)
    rest = value - first
    second = rest.astype(BF16).astype(F32)
    return first, second, rest - second


def source_rows(x, y, z):
    return (-2.0 * x, -2.0 * y, -2.0 * z) + three(x * x + y * y + z * z)


def row_mask(shape, rows):
    row = lax.broadcasted_iota(jnp.int32, shape, 0)
    found = row == rows[0]
    for r in rows[1:]:
        found = found | (row == r)
    return found.astype(F32)


def source_tail(width):
    return row_mask((ROWS, width), (3, 4, 5, 6)).astype(BF16)


def target_of(rows):
    rows = rows.astype(F32)
    shape = rows.shape
    squares = row_mask(shape, (3, 4, 5))
    upper = rows * (-0.5 * row_mask(shape, (0, 1, 2))) + squares
    lower = rows * squares + SOFTEN * row_mask(shape, (6,))
    return jnp.concatenate([upper, lower], axis=0).astype(BF16)


def put_rows(ref, rows, count):
    for f in range(ROWS):
        value = rows[f] if f < len(rows) else jnp.zeros_like(rows[0])
        ref[pl.ds(f, count, stride=ROWS), :] = value


def stack_rows(rows):
    n = rows[0].shape[1]
    return jnp.concatenate(tuple(rows) + (jnp.zeros((ROWS - len(rows), n), F32),), axis=0)


def couplings(target, slots, source_ref, tail):
    low = low_half(source_ref.shape[1:])
    tiles = [
        jnp.concatenate([pair(low, source_ref[first], source_ref[second]), tail], axis=0)
        for first, second in zip(slots[0::2], slots[1::2])
    ]
    square = dot_0(target, jnp.concatenate(tiles, axis=1))
    return lax.rsqrt(square.astype(BF16))


def gathered(slots, moment_ref):
    low = low_half(moment_ref.shape[1:])
    tiles = [pair(low, moment_ref[first], moment_ref[second]) for first, second in zip(slots[0::2], slots[1::2])]
    return jnp.concatenate(tiles, axis=1)


def interact(target, slots, source_ref, tail, moment_ref):
    kern = couplings(target, slots, source_ref, tail)
    return INV_FOUR_PI * dot_t(gathered(slots, moment_ref), kern)


def listed_kernel(send_ref, charges_ref, basis_ref, proxy_ref, moment_ref, own_ref, out_ref, tile_ref):
    slots, devices = send_ref.shape
    leaves, rhs, rank2 = moment_ref.shape
    low = low_half((rhs, rank2))
    put_rows(tile_ref, source_rows(*[twice(jnp.transpose(proxy_ref[c].astype(F32))) for c in range(3)]), leaves)
    own_ref[...] = tile_ref[...].astype(BF16).reshape(own_ref.shape)

    def leaf_pair(i, carry):
        columns = pl.ds(pl.multiple_of(i * rank2, rank2), rank2)
        q = charges_ref[:, columns]
        u = basis_ref[:, columns]
        zero = jnp.zeros_like(q)
        stacked = jnp.concatenate([jnp.where(low, q, zero), jnp.where(low, zero, q)], axis=0)
        product = dot_t(stacked, jnp.concatenate([u, u], axis=0)).astype(BF16)
        moment_ref[2 * i] = product[:rhs]
        moment_ref[2 * i + 1] = product[rhs:]
        return carry

    lax.fori_loop(0, leaves // 2, leaf_pair, 0, unroll=8)
    low8 = low_half((ROWS, rank2))
    base = slots // 2 * rhs

    def pack(p, carry):
        s = [send_ref[t, p] for t in range(slots)]
        for q in range(slots // 2):
            first, second = s[2 * q], s[2 * q + 1]
            out_ref[p, q * rhs : (q + 1) * rhs, :] = pair(low, moment_ref[first], moment_ref[second])
            out_ref[p, base + q * ROWS : base + (q + 1) * ROWS, :] = pair(low8, own_ref[first], own_ref[second])
        return carry

    lax.fori_loop(0, devices, pack, 0, unroll=4)


def relayout(x_ref, scratch_ref):
    rank, _, leaves = x_ref.shape
    half = rank // 2
    eye = (
        lax.broadcasted_iota(jnp.int32, (leaves, leaves), 0)
        == lax.broadcasted_iota(jnp.int32, (leaves, leaves), 1)
    ).astype(BF16)
    for k in range(0, half, 2):
        block = jnp.concatenate(
            [x_ref[k], x_ref[k + half], x_ref[k + 1], x_ref[k + 1 + half]], axis=0
        )
        turned = dot_t(eye, block)
        for n in range(2):
            scratch_ref[pl.ds(k + n, leaves, stride=half), :] = turned[:, n * 2 * rank : (n + 1) * 2 * rank]


def spread_rows(block, low):
    zero = jnp.zeros_like(block)
    return jnp.concatenate([jnp.where(low, block, zero), jnp.where(low, zero, block)], axis=0)


def upward_kernel(
    moment_ref, up_leaf_ref, up_branch_ref, up_device_ref, pbranch_ref, pdevice_ref, out_ref, scratch_ref, branch_ref
):
    leaves, rhs, rank2 = moment_ref.shape
    rank = rank2 // 2
    half = rank // 2
    branches = leaves // FAN
    relayout(up_leaf_ref, scratch_ref)
    low = low_half((half, rank2))
    low_m = low_half((rhs, rank2))
    low_r = low_half((ROWS, rank2))
    wide = up_branch_ref[...].astype(F32).reshape(rank * branches, rank)
    branch_ref[...] = twice(wide)
    rows = source_rows(*[twice(pbranch_ref[c].astype(F32)) for c in range(3)])
    m_device = jnp.zeros((rhs, rank), F32)
    previous = None
    base = branches // 2 * rhs
    for c in range(branches):
        blocks, moments = [], []
        for b in range(c * FAN, (c + 1) * FAN):
            block = scratch_ref[b * half : (b + 1) * half, :].astype(BF16)
            blocks.append(spread_rows(block, low))
            moments.append(moment_ref[b])
        m_branch = dot_t(jnp.concatenate(moments, axis=1), jnp.concatenate(blocks, axis=1)).astype(BF16)
        matrix = branch_ref[pl.ds(c, rank, stride=branches), :][:, :rank].astype(BF16)
        m_device = m_device + dot_t(m_branch, matrix)
        spread = twice(m_branch)
        source = stack_rows([r[c : c + 1, :] for r in rows]).astype(BF16)
        if c % 2 == 1:
            q = c // 2
            out_ref[q * rhs : (q + 1) * rhs, :] = pair(low_m, previous[0], spread)
            out_ref[base + q * ROWS : base + (q + 1) * ROWS, :] = pair(low_r, previous[1], source)
        previous = spread, source
    base = base + branches // 2 * ROWS
    m_device = m_device.astype(BF16)
    share = dot_t(m_device, up_device_ref[...]).astype(BF16)
    out_ref[base : base + rhs, :] = jnp.concatenate([m_device, share], axis=1)
    rows = source_rows(*[twice(pdevice_ref[c : c + 1, :].astype(F32)) for c in range(3)])
    out_ref[base + rhs :, :] = stack_rows(rows).astype(BF16)


def near_kernel(
    near_ref, charges_ref, points_ref, left_ref, right_ref, down_leaf_ref, out_ref, down_ref,
    wide_ref, source_ref, target_ref, scratch_ref, weight_ref, kern_a_ref, kern_b_ref,
):
    rhs, total = charges_ref.shape
    entries, leaves = near_ref.shape
    size = total // leaves
    halo = REACH * size
    span = 2 * REACH + 1
    reach = (span + 1) * size
    pairs = leaves // 2
    relayout(down_leaf_ref, scratch_ref)
    down_ref[...] = scratch_ref[...].astype(BF16)

    wide_ref[:, :halo] = left_ref[:rhs, :]
    wide_ref[:, halo : halo + total] = charges_ref[...]
    wide_ref[:, halo + total :] = right_ref[:rhs, :]
    coords = [
        jnp.concatenate(
            [left_ref[rhs + c : rhs + c + 1, :], points_ref[c : c + 1, :], right_ref[rhs + c : rhs + c + 1, :]], axis=1
        ).astype(F32)
        for c in range(3)
    ]
    rows = stack_rows(source_rows(*coords))
    source_ref[...] = jnp.concatenate([rows.astype(BF16), source_tail(total + 2 * halo)], axis=0)
    target_ref[...] = target_of(rows[:, halo : halo + total])

    near = near_ref[...]
    counts = [jnp.sum((near == o - REACH).astype(F32), axis=0, keepdims=True) for o in range(span)]
    counts = jnp.concatenate(counts + [jnp.zeros((2 * ROWS - span, leaves), F32)], axis=0).astype(BF16)
    offset = lax.broadcasted_iota(jnp.int32, (2 * ROWS, reach), 0)
    block = lax.broadcasted_iota(jnp.int32, (2 * ROWS, reach), 1) // size
    for h in range(2):
        weight_ref[h] = dot_0(counts, (block == offset + h).astype(BF16))

    def evaluate(i, kern_ref):
        start = pl.multiple_of(i * 2 * size, 2 * size)
        square = dot_0(target_ref[:, pl.ds(start, 2 * size)], source_ref[:, pl.ds(start, reach)])
        kern = lax.rsqrt(square.astype(BF16))
        for h in range(2):
            weight = jnp.broadcast_to(weight_ref[h, pl.ds(2 * i + h, 1), :], (2 * ROWS, reach)).astype(BF16)
            for s in range(h * size, (h + 1) * size, 2 * ROWS):
                kern_ref[s : s + 2 * ROWS, :] = kern[s : s + 2 * ROWS, :] * weight

    def apply(i, kern_ref):
        start = pl.multiple_of(i * 2 * size, 2 * size)
        out_ref[:, pl.ds(start, 2 * size)] = INV_FOUR_PI * dot_t(wide_ref[:, pl.ds(start, reach)], kern_ref[...])

    evaluate(0, kern_a_ref)

    def step(t, carry):
        apply(2 * t, kern_a_ref)
        evaluate(2 * t + 1, kern_b_ref)
        evaluate(jnp.minimum(2 * t + 2, pairs - 1), kern_a_ref)
        apply(2 * t + 1, kern_b_ref)
        return carry

    lax.fori_loop(0, pairs // 2, step, 0)


def put_pair(moment_ref, slot, tile):
    low = low_half(tile.shape)
    other = swap(tile)
    moment_ref[slot] = pair(low, tile, other)
    moment_ref[slot + 1] = pair(low, other, tile)


def group_kernel(*refs, members):
    far_ref, pgroup_ref = refs[:2]
    parts = refs[2 : 2 + members]
    fb_ref, ld_ref, out_ref = refs[2 + members : 5 + members]
    moment_ref, source_ref, dev_m_ref, dev_source_ref = refs[5 + members :]
    entries, branches = far_ref.shape
    rhs, rank2 = moment_ref.shape[1:]
    rank = rank2 // 2
    me = lax.axis_index("dev")
    low = low_half((rhs, rank2))
    tail = source_tail(rank2)
    first = branches // 2 * rhs
    base = first + branches // 2 * ROWS
    m_group = jnp.zeros((rhs, rank2), F32)
    for s, part in enumerate(parts):
        owner = lax.rem(me - s + members, members)
        for q in range(branches // 2):
            put_pair(moment_ref, owner * branches + 2 * q, part[q * rhs : (q + 1) * rhs, :])
            put_pair(source_ref, owner * branches + 2 * q, part[first + q * ROWS : first + (q + 1) * ROWS, :])
        mixed = part[base : base + rhs, :].astype(F32)
        m_group = m_group + mixed
        keep = (jnp.abs(owner - me) >= 2).astype(F32)
        dev_m_ref[owner] = (pair(low, mixed, pltpu.roll(mixed, rank, 1)) * keep).astype(BF16)
        dev_source_ref[owner] = part[base + rhs :, :]
    out_ref[:rhs, :] = twice(m_group[:, rank:]).astype(BF16)
    rows = source_rows(*[twice(pgroup_ref[c : c + 1, :].astype(F32)) for c in range(3)])
    out_ref[rhs:, :] = stack_rows(rows).astype(BF16)

    for c in range(branches):
        target = target_of(source_ref[me * branches + c][:, :rank])
        fb_ref[c] = interact(target, [far_ref[e, c] for e in range(entries)], source_ref, tail, moment_ref)
    target = target_of(dev_source_ref[me][:, :rank])
    ld_ref[...] = interact(target, list(range(members)), dev_source_ref, tail, dev_m_ref)


def downward_kernel(*refs, groups):
    far_ref = refs[0]
    tiles = refs[1 : 1 + groups]
    (
        fb_ref, ld_ref, down_device_ref, down_branch_ref, down_ref, own_ref, own_m_ref, recv_ref, basis_ref, near_ref,
        out_ref, moment_ref, source_ref, grp_m_ref, grp_source_ref, branch_ref, parent_ref, kern_a_ref, kern_b_ref,
    ) = refs[1 + groups :]
    entries, leaves = far_ref.shape
    rhs, rank2 = moment_ref.shape[1:]
    rank = rank2 // 2
    half = rank // 2
    branches = leaves // FAN
    devices = recv_ref.shape[0]
    slots = (moment_ref.shape[0] - leaves) // devices
    pairs = leaves // 2
    me = lax.axis_index("grp")
    low = low_half((rhs, rank2))
    tail = source_tail(rank2)

    for s, tile_ref in enumerate(tiles):
        owner = lax.rem(me - s + groups, groups)
        keep = (jnp.abs(owner - me) >= 2).astype(F32)
        grp_m_ref[owner] = (tile_ref[:rhs, :].astype(F32) * keep).astype(BF16)
        grp_source_ref[owner] = tile_ref[rhs:, :]
    target = target_of(tiles[0][rhs:, :rank])
    l_group = interact(target, list(range(groups)), grp_source_ref, tail, grp_m_ref).astype(BF16)
    l_device = (ld_ref[...] + dot_t(l_group, down_device_ref[...])).astype(BF16)
    branch_ref[...] = twice(down_branch_ref[...].astype(F32).reshape(rank * branches, rank))
    for c in range(branches):
        matrix = branch_ref[pl.ds(c, rank, stride=branches), :][:, :rank].astype(BF16)
        parent_ref[c] = twice((fb_ref[c] + dot_t(l_device, matrix)).astype(BF16))

    moment_ref[:leaves] = own_m_ref[...]
    source_ref[:leaves] = own_ref[...]
    base = slots // 2 * rhs

    def unpack(p, carry):
        for q in range(slots // 2):
            slot = leaves + p * slots + 2 * q
            put_pair(moment_ref, slot, recv_ref[p, q * rhs : (q + 1) * rhs, :])
            put_pair(source_ref, slot, recv_ref[p, base + q * ROWS : base + (q + 1) * ROWS, :])
        return carry

    lax.fori_loop(0, devices, unpack, 0, unroll=4)
    low_d = low_half((half, rank2))

    def named(b):
        return [far_ref[e, b] for e in range(entries)]

    def evaluate(i, kern_ref):
        for h in range(2):
            b = 2 * i + h
            kern_ref[h] = couplings(target_of(source_ref[b][:, :rank]), named(b), source_ref, tail)

    def apply(i, kern_ref):
        sums = []
        for h in range(2):
            b = 2 * i + h
            far = INV_FOUR_PI * dot_t(gathered(named(b), moment_ref), kern_ref[h])
            rows = down_ref[pl.ds(pl.multiple_of(b * half, half), half), :]
            sums.append((far + dot_t(parent_ref[b // FAN], spread_rows(rows, low_d))).astype(BF16))
        return jnp.concatenate(sums, axis=0)

    def finish(i, sums):
        columns = pl.ds(pl.multiple_of(i * rank2, rank2), rank2)
        product = dot(sums, basis_ref[:, columns])
        out_ref[:, columns] = near_ref[:, columns] + pair(low, product[:rhs], product[rhs:])

    evaluate(0, kern_a_ref)

    def step(t, sums):
        finish(jnp.maximum(2 * t - 1, 0), sums)
        sums = apply(2 * t, kern_a_ref)
        evaluate(2 * t + 1, kern_b_ref)
        finish(2 * t, sums)
        evaluate(jnp.minimum(2 * t + 2, pairs - 1), kern_a_ref)
        return apply(2 * t + 1, kern_b_ref)

    finish(pairs - 1, lax.fori_loop(0, pairs // 2, step, jnp.zeros((2 * rhs, rank), BF16)))


VMEM = functools.partial(pl.BlockSpec, memory_space=pltpu.VMEM)
SMEM = functools.partial(pl.BlockSpec, memory_space=pltpu.SMEM)


def struct(shape, dtype):
    return jax.ShapeDtypeStruct(shape, dtype)


def on_device(
    charges, points, basis, up_leaf, up_branch, up_device, down_leaf, down_branch, down_device,
    proxy_leaf, proxy_branch, proxy_device, proxy_group, far_leaf, send_leaf, far_branch, near_leaf,
):
    rhs, total = charges.shape
    rank = basis.shape[0]
    leaves = up_leaf.shape[2]
    size = total // leaves
    branches = leaves // FAN
    slots = send_leaf.shape[0]
    groups = lax.axis_size("grp")
    members = lax.axis_size("dev")
    devices = groups * members
    rank2 = 2 * rank
    half = rank // 2
    halo = REACH * size
    assert rank == size and slots % 2 == 0 and branches % 2 == 0

    moments, own, listed = pl.pallas_call(
        listed_kernel,
        out_shape=(
            struct((leaves, rhs, rank2), BF16),
            struct((leaves, ROWS, rank2), BF16),
            struct((devices, slots // 2 * (rhs + ROWS), rank2), BF16),
        ),
        in_specs=[SMEM(), VMEM(), VMEM(), VMEM()],
        out_specs=(VMEM(), VMEM(), VMEM()),
        scratch_shapes=[pltpu.VMEM((leaves * ROWS, rank2), F32)],
        name="listed",
    )(send_leaf, charges, basis, proxy_leaf)
    received = lax.all_to_all(listed, ("grp", "dev"), split_axis=0, concat_axis=0, tiled=True)

    stacked = jnp.concatenate([charges, points], axis=0)
    last = devices - 1
    left = lax.ppermute(stacked[:, total - halo :], ("grp", "dev"), [(i, i + 1) for i in range(last)])
    right = lax.ppermute(stacked[:, :halo], ("grp", "dev"), [(i + 1, i) for i in range(last)])

    shared = pl.pallas_call(
        upward_kernel,
        out_shape=struct(((branches // 2 + 1) * (rhs + ROWS), rank2), BF16),
        in_specs=[VMEM()] * 6,
        out_specs=VMEM(),
        scratch_shapes=[pltpu.VMEM((leaves * half, rank2), F32), pltpu.VMEM((rank * branches, rank2), F32)],
        name="upward",
    )(
        moments,
        up_leaf,
        jnp.transpose(up_branch, (0, 2, 1)),
        up_device[:, :, 0],
        jnp.transpose(proxy_branch, (0, 2, 1)),
        proxy_device[:, :, 0],
    )
    parts = [shared] + [
        lax.ppermute(shared, "dev", [(i, (i + s) % members) for i in range(members)]) for s in range(1, members)
    ]

    reach = (2 * REACH + 2) * size
    near, down = pl.pallas_call(
        near_kernel,
        out_shape=(struct((rhs, total), F32), struct((leaves * half, rank2), BF16)),
        in_specs=[VMEM()] * 6,
        out_specs=(VMEM(), VMEM()),
        scratch_shapes=[
            pltpu.VMEM((rhs, total + 2 * halo), BF16),
            pltpu.VMEM((2 * ROWS, total + 2 * halo), BF16),
            pltpu.VMEM((2 * ROWS, total), BF16),
            pltpu.VMEM((leaves * half, rank2), F32),
            pltpu.VMEM((2, leaves, reach), F32),
            pltpu.VMEM((2 * size, reach), BF16),
            pltpu.VMEM((2 * size, reach), BF16),
        ],
        name="near",
    )(near_leaf, charges, points, left, right, down_leaf)

    far_b, part_d, tile = pl.pallas_call(
        functools.partial(group_kernel, members=members),
        out_shape=(struct((branches, rhs, rank), F32), struct((rhs, rank), F32), struct((rhs + ROWS, rank2), BF16)),
        in_specs=[SMEM(), VMEM()] + [VMEM()] * members,
        out_specs=(VMEM(), VMEM(), VMEM()),
        scratch_shapes=[
            pltpu.VMEM((members * branches, rhs, rank2), BF16),
            pltpu.VMEM((members * branches, ROWS, rank2), BF16),
            pltpu.VMEM((members, rhs, rank2), BF16),
            pltpu.VMEM((members, ROWS, rank2), BF16),
        ],
        name="group",
    )(far_branch, proxy_group[:, :, 0], *parts)
    tiles = [tile] + [
        lax.ppermute(tile, "grp", [(i, (i + s) % groups) for i in range(groups)]) for s in range(1, groups)
    ]

    table = leaves + devices * slots
    return pl.pallas_call(
        functools.partial(downward_kernel, groups=groups),
        out_shape=struct((rhs, total), F32),
        in_specs=[SMEM()] + [VMEM()] * (groups + 10),
        out_specs=VMEM(),
        scratch_shapes=[
            pltpu.VMEM((table, rhs, rank2), BF16),
            pltpu.VMEM((table, ROWS, rank2), BF16),
            pltpu.VMEM((groups, rhs, rank2), BF16),
            pltpu.VMEM((groups, ROWS, rank2), BF16),
            pltpu.VMEM((rank * branches, rank2), F32),
            pltpu.VMEM((branches, rhs, rank2), BF16),
            pltpu.VMEM((2, rank, far_leaf.shape[0] * rank), BF16),
            pltpu.VMEM((2, rank, far_leaf.shape[0] * rank), BF16),
        ],
        name="downward",
    )(
        far_leaf, *tiles, far_b, part_d, down_device[:, :, 0], jnp.transpose(down_branch, (0, 2, 1)), down, own,
        moments, received, basis, near,
    )


def solution(mesh):
    points = P(None, ("grp", "dev"))
    blocks = P(None, None, ("grp", "dev"))
    placed = (points,) * 3 + (blocks,) * 9 + (P(None, None, "grp"),) + (points,) * 4
    return jax.shard_map(on_device, mesh=mesh, in_specs=placed, out_specs=points, check_vma=False)
```

time: 88.7 us -> 74.1 us (0.84)
  Pallas kernels: 50.6 us -> 33.1 us
  starting transfers between devices: 26.3 us -> 36 us
  waiting for transfers between devices: 5.85 us -> 0.82 us
  local copies, waits for them, and re-layouts: 4.81 us -> 3.38 us
    pallas_call x1, Pallas kernels: 26.5 us -> 12.7 us  [on_device(): pl.pallas_call(functools.partial(downward_kernel, groups=groups), out_sha...]
    ppermute x7, starting transfers between devices: 12.7 us -> 21.1 us  [on_device(): lax.ppermute(shared, 'dev', [(i, (i + s) % members) for i in range(member...]
    ppermute x7, waiting for transfers between devices: 5.84 us -> 0.81 us  [on_device(): lax.ppermute(shared, 'dev', [(i, (i + s) % members) for i in range(member...]
    pallas_call x1, Pallas kernels: 13.6 us -> 9.95 us  [on_device(): pl.pallas_call(near_kernel, out_shape=(struct((rhs, total), F32), struct(...]
    unnamed x36, local copies, waits for them, and re-layouts: 4.78 us -> 3.35 us
    all_to_all x1, starting transfers between devices: 6.07 us -> 7.33 us  [on_device(): lax.all_to_all(listed, ('grp', 'dev'), split_axis=0, concat_axis=0, tiled...]
  transfers between devices with their start and end apart: 13 -> 13, of which waited for: 2 -> 1; matrix products, arithmetic and copies ran while one was open for 1% -> 1% of each run, Pallas kernels for 19% -> 22%
where the time goes in v2:
time: 74.1 us; the launch traced here: 73.4 us
  starting transfers between devices  36 us (49%)
  Pallas kernels  33.1 us (45%)
  local copies, waits for them, and re-layouts  3.38 us (5%)
  waiting for transfers between devices  0.82 us (1%)
    ppermute x7, starting transfers between devices, on_device(): lax.ppermute(shared, 'dev', [(i, (i + s) % members) for i in range(member...  21.1 us
    pallas_call x1, Pallas kernels, on_device(): pl.pallas_call(functools.partial(downward_kernel, groups=groups), out_sha...  12.7 us
    pallas_call x1, Pallas kernels, on_device(): pl.pallas_call(near_kernel, out_shape=(struct((rhs, total), F32), struct(...  9.95 us
    all_to_all x1, starting transfers between devices, on_device(): lax.all_to_all(listed, ('grp', 'dev'), split_axis=0, concat_axis=0, tiled...  7.33 us
    ppermute x1, starting transfers between devices, on_device(): lax.ppermute(stacked[:, total - halo:], ('grp', 'dev'), [(i, i + 1) for i...  4.55 us
    pallas_call x1, Pallas kernels, on_device(): pl.pallas_call(upward_kernel, out_shape=struct(((branches // 2 + 1) * (rh...  3.89 us
    pallas_call x1, Pallas kernels, on_device(): pl.pallas_call(listed_kernel, out_shape=(struct((leaves, rhs, rank2), BF1...  3.88 us
    unnamed x36, local copies, waits for them, and re-layouts  3.35 us
  transfers between devices with their start and end apart: 13, of which 1 were waited for; matrix products, arithmetic and copies ran while one was open for 1% of the time, Pallas kernels for 22%

profile of v2, /device:TPU:0, one launch (start us, length us, event | category | flops | bytes accessed | tf_op | source)
XLA Modules:
  0.0 73.4 jit_solution(11643653169356761154)
XLA Ops:
  0.0 3.9 %listed.1 = (bf16[64,32,128]{2,1,0:T(8,128)(2,1)}, bf16[64,8,128]{2,1,0:T(8,128)(2,1)}, bf16[32,80,128]{2,1,0:T(8,128)(2,1)}) custom-call(s32[4,32]{1,0:T(4,128)} %send_ref.1, bf16[32,4096]{1,0:T(8,128)(2,1)} %charges_ref.3, bf16[64,4096]{1,0:T(8,128)(2,1)} %refs_13_.1, bf16[3,64,64]{2,1,0:T(8,128)(2,1)} %proxy_ref.1), custom_call_target="tpu_custom_call" | custom-call | tf_op jit(solution)/shard_map/listed/pallas_call | solution.py:420
  3.9 7.3 %all-to-all-start = ((bf16[32,80,128]{2,1,0:T(8,128)(2,1)}), bf16[32,80,128]{2,1,0:T(8,128)(2,1)S(1)}, u32[]{:S(2)}, u32[]{:S(2)}) async-start(bf16[32,80,128]{2,1,0:T(8,128)(2,1)} %get-tuple-element.19), calls=%async_computation | async-start | bytes 1310720 | tf_op jit(solution)/shard_map/all_to_all | solution.py:432
  11.2 3.9 %upward.1.refs_2_ = bf16[200,128]{1,0:T(8,128)(2,1)} custom-call(bf16[64,32,128]{2,1,0:T(8,128)(2,1)} %get-tuple-element.13.moment_ref.refs_11_, bf16[64,64,64]{2,1,0:T(8,128)(2,1)} %up_leaf_ref.1, bf16[64,8,64]{2,1,0:T(8,128)(2,1)} %bitcast.7, bf16[64,64]{1,0:T(8,128)(2,1)} %bitcast.9, bf16[3,8,64]{2,1,0:T(8,128)(2,1)} %bitcast.11, bf16[3,64]{1,0:T(4,128)(2,1)} %bitcast.12), custom_call_target="tpu_custom_call" | custom-call | tf_op jit(solution)/shard_map/upward/pallas_call | solution.py:439
  15.1 4.6 %collective-permute-start.6 = (bf16[200,128]{1,0:T(8,128)(2,1)}, bf16[200,128]{1,0:T(8,128)(2,1)S(1)}, u32[]{:S(2)}, u32[]{:S(2)}) collective-permute-start(bf16[200,128]{1,0:T(8,128)(2,1)} %upward.1.refs_2_), channel_id=1, source_target_pairs={{0,7},{1,0},{2,1},{3,2},{4,3},{5,4},{6,5},{7,6},{8,15},{9,8},{10,9... | collective-permute-start | bytes 153608 | tf_op jit(solution)/shard_map/ppermute | solution.py:455
  19.7 0.5 collective-permute-start.5
  20.2 3.0 %collective-permute-start.3 = (bf16[200,128]{1,0:T(8,128)(2,1)}, bf16[200,128]{1,0:T(8,128)(2,1)S(1)}, u32[]{:S(2)}, u32[]{:S(2)}) collective-permute-start(bf16[200,128]{1,0:T(8,128)(2,1)} %upward.1.refs_2_), channel_id=1, source_target_pairs={{0,4},{1,5},{2,6},{3,7},{4,0},{5,1},{6,2},{7,3},{8,12},{9,13},{10,... | collective-permute-start | bytes 153608 | tf_op jit(solution)/shard_map/ppermute | solution.py:455
  23.2 0.8 %collective-permute-done.6.refs_9_ = bf16[200,128]{1,0:T(8,128)(2,1)S(1)} collective-permute-done((bf16[200,128]{1,0:T(8,128)(2,1)}, bf16[200,128]{1,0:T(8,128)(2,1)S(1)}, u32[]{:S(2)}, u32[]{:S(2)}) %collective-permute-start.6) | collective-permute-done | bytes 51232 | tf_op jit(solution)/shard_map/ppermute | solution.py:455
  24.0 2.0 %collective-permute-start.1 = (bf16[200,128]{1,0:T(8,128)(2,1)S(1)}, bf16[200,128]{1,0:T(8,128)(2,1)S(1)}, u32[]{:S(2)}, u32[]{:S(2)}) collective-permute-start(bf16[200,128]{1,0:T(8,128)(2,1)S(1)} %copy-done.2), channel_id=1, source_target_pairs={{0,2},{1,3},{2,4},{3,5},{4,6},{5,7},{6,0},{7,1},{8,10},{9,11},{10,... | collective-permute-start | bytes 153608 | tf_op jit(solution)/shard_map/ppermute | solution.py:455
  26.0 11.1 %collective-permute-start = (bf16[200,128]{1,0:T(8,128)(2,1)S(1)}, bf16[200,128]{1,0:T(8,128)(2,1)S(1)}, u32[]{:S(2)}, u32[]{:S(2)}) collective-permute-start(bf16[200,128]{1,0:T(8,128)(2,1)S(1)} %copy-done.2), channel_id=1, source_target_pairs={{0,1},{1,2},{2,3},{3,4},{4,5},{5,6},{6,7},{7,0},{8,9},{9,10},{10,1... | collective-permute-start | bytes 153608 | tf_op jit(solution)/shard_map/ppermute | solution.py:455
  37.1 1.3 %collective-permute-start.11 = (bf16[35,256]{1,0:T(8,128)(2,1)S(1)}, bf16[35,256]{1,0:T(8,128)(2,1)S(1)}, u32[]{:S(2)}, u32[]{:S(2)}) collective-permute-start(bf16[35,256]{1,0:T(8,128)(2,1)S(1)} %get-tuple-element.21), channel_id=1, source_target_pairs={{1,0},{2,1},{3,2},{4,3},{5,4},{6,5},{7,6},{8,7},{9,8},{10,9},{11,1... | collective-permute-start | bytes 53768 | tf_op jit(solution)/shard_map/ppermute | solution.py:437
  38.4 4.5 %collective-permute-start.10 = (bf16[35,256]{1,0:T(8,128)(2,1)S(1)}, bf16[35,256]{1,0:T(8,128)(2,1)S(1)}, u32[]{:S(2)}, u32[]{:S(2)}) collective-permute-start(bf16[35,256]{1,0:T(8,128)(2,1)S(1)} %get-tuple-element.22), channel_id=1, source_target_pairs={{0,1},{1,2},{2,3},{3,4},{4,5},{5,6},{6,7},{7,8},{8,9},{9,10},{10,1... | collective-permute-start | bytes 53768 | tf_op jit(solution)/shard_map/ppermute | solution.py:436
  43.0 0.7 copy.18.refs_0_
  43.7 0.5 copy-done.8
  44.3 0.0 copy-done.9
  44.3 0.0 copy-done.10
  44.3 2.7 %group.1 = (f32[8,32,64]{2,1,0:T(8,128)}, f32[32,64]{1,0:T(8,128)}, bf16[40,128]{1,0:T(8,128)(2,1)}) custom-call(s32[16,8]{1,0:T(8,128)} %copy.18.refs_0_, bf16[3,64]{1,0:T(4,128)(2,1)} %bitcast.13, bf16[200,128]{1,0:T(8,128)(2,1)} %upward.1.refs_2_, bf16[200,128]{1,0:T(8,128)(2,1)} %copy-done.10, bf16[200,128]{1,0:T(8,128)(2,1)} %copy-done.9, ...), custom_call_target="tpu_custom_call" | custom-call | tf_op jit(solution)/shard_map/group/pallas_call | solution.py:476
  47.0 1.5 %collective-permute-start.8 = (bf16[40,128]{1,0:T(8,128)(2,1)}, bf16[40,128]{1,0:T(8,128)(2,1)S(1)}, u32[]{:S(2)}, u32[]{:S(2)}) collective-permute-start(bf16[40,128]{1,0:T(8,128)(2,1)} %get-tuple-element.14.refs_1_), channel_id=1, source_target_pairs={{0,16},{8,24},{16,0},{24,8},{1,17},{9,25},{17,1},{25,9},{2,18},{10... | collective-permute-start | bytes 30728 | tf_op jit(solution)/shard_map/ppermute | solution.py:490
  48.5 0.2 collective-permute-start.7
  48.7 0.6 copy-done.11
  49.3 0.6 copy-done.12
  49.9 9.9 %near.1 = (f32[32,4096]{1,0:T(8,128)}, bf16[2048,128]{1,0:T(8,128)(2,1)}) custom-call(s32[16,64]{1,0:T(8,128)} %near_ref.1, bf16[32,4096]{1,0:T(8,128)(2,1)} %charges_ref.3, bf16[3,4096]{1,0:T(4,128)(2,1)} %points_ref.1, bf16[35,256]{1,0:T(8,128)(2,1)} %copy-done.12, bf16[35,256]{1,0:T(8,128)(2,1)} %copy-done.11, bf16[64,64,64]{2,1,0:T(8,128)(2,1)} %down_leaf_ref.1), custom_call_target="tpu_custom_call" | custom-call | tf_op jit(solution)/shard_map/near/pallas_call | solution.py:459
  60.0 0.5 copy-done.13
  60.5 0.3 copy-done
  60.8 12.7 %downward.1 = f32[32,4096]{1,0:T(8,128)} custom-call(s32[16,64]{1,0:T(8,128)} %refs_0_.2, bf16[40,128]{1,0:T(8,128)(2,1)} %get-tuple-element.14.refs_1_, bf16[40,128]{1,0:T(8,128)(2,1)} %copy-done.15, bf16[40,128]{1,0:T(8,128)(2,1)} %copy-done.14, bf16[40,128]{1,0:T(8,128)(2,1)} %copy-done.13, f32[8,32,64]{2,1,0:T(8,128)} %get-tuple-element.15.refs_5_, ...), custom_call_target="tpu_custom_call" | custom-call | tf_op jit(solution)/shard_map/downward/pallas_call | solution.py:494
  (45 shorter events, 0.2 us)
Async XLA Ops:
  3.9 56.1 %all-to-all-start = ((bf16[32,80,128]{2,1,0:T(8,128)(2,1)}), bf16[32,80,128]{2,1,0:T(8,128)(2,1)S(1)}, u32[]{:S(2)}, u32[]{:S(2)}) async-start(bf16[32,80,128]{2,1,0:T(8,128)(2,1)} %get-tuple-element.19), calls=%async_computation | async-start | bytes 1310720 | tf_op jit(solution)/shard_map/all_to_all | solution.py:432
  11.2 11.9 %copy-start.1 = (bf16[32,4096]{1,0:T(8,128)(2,1)S(1)}, bf16[32,4096]{1,0:T(8,128)(2,1)}, u32[]{:S(2)}) copy-start(bf16[32,4096]{1,0:T(8,128)(2,1)} %charges_ref.3) | copy-start | bytes 786436
  15.1 8.0 %copy-start.3 = (bf16[3,4096]{1,0:T(4,128)(2,1)S(1)}, bf16[3,4096]{1,0:T(4,128)(2,1)}, u32[]{:S(2)}) copy-start(bf16[3,4096]{1,0:T(4,128)(2,1)} %points_ref.1) | copy-start | bytes 73732
  15.1 8.9 %collective-permute-start.6 = (bf16[200,128]{1,0:T(8,128)(2,1)}, bf16[200,128]{1,0:T(8,128)(2,1)S(1)}, u32[]{:S(2)}, u32[]{:S(2)}) collective-permute-start(bf16[200,128]{1,0:T(8,128)(2,1)} %upward.1.refs_2_), channel_id=1, source_target_pairs={{0,7},{1,0},{2,1},{3,2},{4,3},{5,4},{6,5},{7,6},{8,15},{9,8},{10,9... | collective-permute-start | bytes 153608 | tf_op jit(solution)/shard_map/ppermute | solution.py:455
  19.7 6.3 %collective-permute-start.5 = (bf16[200,128]{1,0:T(8,128)(2,1)}, bf16[200,128]{1,0:T(8,128)(2,1)S(1)}, u32[]{:S(2)}, u32[]{:S(2)}) collective-permute-start(bf16[200,128]{1,0:T(8,128)(2,1)} %upward.1.refs_2_), channel_id=1, source_target_pairs={{0,6},{1,7},{2,0},{3,1},{4,2},{5,3},{6,4},{7,5},{8,14},{9,15},{10,... | collective-permute-start | bytes 153608 | tf_op jit(solution)/shard_map/ppermute | solution.py:455
  20.2 16.9 %collective-permute-start.4 = (bf16[200,128]{1,0:T(8,128)(2,1)}, bf16[200,128]{1,0:T(8,128)(2,1)S(1)}, u32[]{:S(2)}, u32[]{:S(2)}) collective-permute-start(bf16[200,128]{1,0:T(8,128)(2,1)} %upward.1.refs_2_), channel_id=1, source_target_pairs={{0,5},{1,6},{2,7},{3,0},{4,1},{5,2},{6,3},{7,4},{8,13},{9,14},{10,... | collective-permute-start | bytes 153608 | tf_op jit(solution)/shard_map/ppermute | solution.py:455
  20.2 18.2 %collective-permute-start.3 = (bf16[200,128]{1,0:T(8,128)(2,1)}, bf16[200,128]{1,0:T(8,128)(2,1)S(1)}, u32[]{:S(2)}, u32[]{:S(2)}) collective-permute-start(bf16[200,128]{1,0:T(8,128)(2,1)} %upward.1.refs_2_), channel_id=1, source_target_pairs={{0,4},{1,5},{2,6},{3,7},{4,0},{5,1},{6,2},{7,3},{8,12},{9,13},{10,... | collective-permute-start | bytes 153608 | tf_op jit(solution)/shard_map/ppermute | solution.py:455
  23.1 20.5 %collective-permute-start.2 = (bf16[200,128]{1,0:T(8,128)(2,1)}, bf16[200,128]{1,0:T(8,128)(2,1)S(1)}, u32[]{:S(2)}, u32[]{:S(2)}) collective-permute-start(bf16[200,128]{1,0:T(8,128)(2,1)} %upward.1.refs_2_), channel_id=1, source_target_pairs={{0,3},{1,4},{2,5},{3,6},{4,7},{5,0},{6,1},{7,2},{8,11},{9,12},{10,... | collective-permute-start | bytes 153608 | tf_op jit(solution)/shard_map/ppermute | solution.py:455
  23.2 0.8 %copy-start.2 = (bf16[200,128]{1,0:T(8,128)(2,1)S(1)}, bf16[200,128]{1,0:T(8,128)(2,1)}, u32[]{:S(2)}) copy-start(bf16[200,128]{1,0:T(8,128)(2,1)} %upward.1.refs_2_) | copy-start | bytes 153604
  24.0 19.7 %copy-start.4 = (bf16[200,128]{1,0:T(8,128)(2,1)}, bf16[200,128]{1,0:T(8,128)(2,1)S(1)}, u32[]{:S(2)}) copy-start(bf16[200,128]{1,0:T(8,128)(2,1)S(1)} %collective-permute-done.6.refs_9_) | copy-start | bytes 153604
  24.0 19.7 %collective-permute-start.1 = (bf16[200,128]{1,0:T(8,128)(2,1)S(1)}, bf16[200,128]{1,0:T(8,128)(2,1)S(1)}, u32[]{:S(2)}, u32[]{:S(2)}) collective-permute-start(bf16[200,128]{1,0:T(8,128)(2,1)S(1)} %copy-done.2), channel_id=1, source_target_pairs={{0,2},{1,3},{2,4},{3,5},{4,6},{5,7},{6,0},{7,1},{8,10},{9,11},{10,... | collective-permute-start | bytes 153608 | tf_op jit(solution)/shard_map/ppermute | solution.py:455
  26.0 17.7 %copy-start.5 = (bf16[200,128]{1,0:T(8,128)(2,1)}, bf16[200,128]{1,0:T(8,128)(2,1)S(1)}, u32[]{:S(2)}) copy-start(bf16[200,128]{1,0:T(8,128)(2,1)S(1)} %collective-permute-done.5.refs_8_) | copy-start | bytes 153604
  26.0 17.7 %collective-permute-start = (bf16[200,128]{1,0:T(8,128)(2,1)S(1)}, bf16[200,128]{1,0:T(8,128)(2,1)S(1)}, u32[]{:S(2)}, u32[]{:S(2)}) collective-permute-start(bf16[200,128]{1,0:T(8,128)(2,1)S(1)} %copy-done.2), channel_id=1, source_target_pairs={{0,1},{1,2},{2,3},{3,4},{4,5},{5,6},{6,7},{7,0},{8,9},{9,10},{10,1... | collective-permute-start | bytes 153608 | tf_op jit(solution)/shard_map/ppermute | solution.py:455
  37.1 5.9 %copy-start.16 = (s32[16,8]{0,1:T(8,128)S(1)}, s32[16,8]{0,1:T(8,128)}, u32[]{:S(2)}) copy-start(s32[16,8]{0,1:T(8,128)} %param.32) | copy-start | bytes 1540
  37.1 6.6 %copy-start.6 = (bf16[200,128]{1,0:T(8,128)(2,1)}, bf16[200,128]{1,0:T(8,128)(2,1)S(1)}, u32[]{:S(2)}) copy-start(bf16[200,128]{1,0:T(8,128)(2,1)S(1)} %collective-permute-done.4.refs_7_) | copy-start | bytes 153604
  37.1 11.6 %collective-permute-start.11 = (bf16[35,256]{1,0:T(8,128)(2,1)S(1)}, bf16[35,256]{1,0:T(8,128)(2,1)S(1)}, u32[]{:S(2)}, u32[]{:S(2)}) collective-permute-start(bf16[35,256]{1,0:T(8,128)(2,1)S(1)} %get-tuple-element.21), channel_id=1, source_target_pairs={{1,0},{2,1},{3,2},{4,3},{5,4},{6,5},{7,6},{8,7},{9,8},{10,9},{11,1... | collective-permute-start | bytes 53768 | tf_op jit(solution)/shard_map/ppermute | solution.py:437
  38.4 5.3 %copy-start.7 = (bf16[200,128]{1,0:T(8,128)(2,1)}, bf16[200,128]{1,0:T(8,128)(2,1)S(1)}, u32[]{:S(2)}) copy-start(bf16[200,128]{1,0:T(8,128)(2,1)S(1)} %collective-permute-done.3.refs_6_) | copy-start | bytes 153604
  38.4 10.3 %collective-permute-start.10 = (bf16[35,256]{1,0:T(8,128)(2,1)S(1)}, bf16[35,256]{1,0:T(8,128)(2,1)S(1)}, u32[]{:S(2)}, u32[]{:S(2)}) collective-permute-start(bf16[35,256]{1,0:T(8,128)(2,1)S(1)} %get-tuple-element.22), channel_id=1, source_target_pairs={{0,1},{1,2},{2,3},{3,4},{4,5},{5,6},{6,7},{7,8},{8,9},{9,10},{10,1... | collective-permute-start | bytes 53768 | tf_op jit(solution)/shard_map/ppermute | solution.py:436
  43.7 0.6 copy-start.9
  43.7 0.6 copy-start.10
  47.0 12.9 %collective-permute-start.9 = (bf16[40,128]{1,0:T(8,128)(2,1)}, bf16[40,128]{1,0:T(8,128)(2,1)S(1)}, u32[]{:S(2)}, u32[]{:S(2)}) collective-permute-start(bf16[40,128]{1,0:T(8,128)(2,1)} %get-tuple-element.14.refs_1_), channel_id=1, source_target_pairs={{0,24},{8,0},{16,8},{24,16},{1,25},{9,1},{17,9},{25,17},{2,26},{10... | collective-permute-start | bytes 30728 | tf_op jit(solution)/shard_map/ppermute | solution.py:490
  47.0 12.9 %collective-permute-start.8 = (bf16[40,128]{1,0:T(8,128)(2,1)}, bf16[40,128]{1,0:T(8,128)(2,1)S(1)}, u32[]{:S(2)}, u32[]{:S(2)}) collective-permute-start(bf16[40,128]{1,0:T(8,128)(2,1)} %get-tuple-element.14.refs_1_), channel_id=1, source_target_pairs={{0,16},{8,24},{16,0},{24,8},{1,17},{9,25},{17,1},{25,9},{2,18},{10... | collective-permute-start | bytes 30728 | tf_op jit(solution)/shard_map/ppermute | solution.py:490
  48.5 11.4 %collective-permute-start.7 = (bf16[40,128]{1,0:T(8,128)(2,1)}, bf16[40,128]{1,0:T(8,128)(2,1)S(1)}, u32[]{:S(2)}, u32[]{:S(2)}) collective-permute-start(bf16[40,128]{1,0:T(8,128)(2,1)} %get-tuple-element.14.refs_1_), channel_id=1, source_target_pairs={{0,8},{8,16},{16,24},{24,0},{1,9},{9,17},{17,25},{25,1},{2,10},{10... | collective-permute-start | bytes 30728 | tf_op jit(solution)/shard_map/ppermute | solution.py:490
  59.9 0.8 %copy-start = (bf16[32,80,128]{2,1,0:T(8,128)(2,1)}, bf16[32,80,128]{2,1,0:T(8,128)(2,1)S(1)}, u32[]{:S(2)}) copy-start(bf16[32,80,128]{2,1,0:T(8,128)(2,1)S(1)} %all-to-all-done.refs_12_) | copy-start | bytes 1966084
  (6 other events, 3.6 us)

commit v3 on v2

--- a/solution.py
+++ b/solution.py
@@ -98,8 +98,11 @@
         jnp.concatenate([pair(low, source_ref[first], source_ref[second]), tail], axis=0)
         for first, second in zip(slots[0::2], slots[1::2])
     ]
-    square = dot_0(target, jnp.concatenate(tiles, axis=1))
-    return lax.rsqrt(square.astype(BF16))
+    return kern_of(dot_0(target, jnp.concatenate(tiles, axis=1)))
+
+
+def kern_of(square):
+    return (INV_FOUR_PI * lax.rsqrt(square)).astype(BF16)
 
 
 def gathered(slots, moment_ref):
@@ -109,11 +112,12 @@
 
 
 def interact(target, slots, source_ref, tail, moment_ref):
-    kern = couplings(target, slots, source_ref, tail)
-    return INV_FOUR_PI * dot_t(gathered(slots, moment_ref), kern)
-
-
-def listed_kernel(send_ref, charges_ref, basis_ref, proxy_ref, moment_ref, own_ref, out_ref, tile_ref):
+    return dot_t(gathered(slots, moment_ref), couplings(target, slots, source_ref, tail))
+
+
+def listed_kernel(
+    send_ref, charges_ref, points_ref, basis_ref, proxy_ref, moment_ref, own_ref, out_ref, head_ref, last_ref, tile_ref
+):
     slots, devices = send_ref.shape
     leaves, rhs, rank2 = moment_ref.shape
     low = low_half((rhs, rank2))
@@ -144,6 +148,12 @@
         return carry
 
     lax.fori_loop(0, devices, pack, 0, unroll=4)
+    total = charges_ref.shape[1]
+    halo = head_ref.shape[1]
+    for ref, start in ((head_ref, 0), (last_ref, total - halo)):
+        ref[:rhs, :] = charges_ref[:, start : start + halo]
+        ref[rhs:, :] = jnp.zeros((ROWS, halo), BF16)
+        ref[rhs : rhs + 3, :] = points_ref[:, start : start + halo]
 
 
 def relayout(x_ref, scratch_ref):
@@ -208,20 +218,22 @@
     out_ref[base + rhs :, :] = stack_rows(rows).astype(BF16)
 
 
+def turn_kernel(down_leaf_ref, _, down_ref, scratch_ref):
+    relayout(down_leaf_ref, scratch_ref)
+    down_ref[...] = scratch_ref[...].astype(BF16)
+
+
 def near_kernel(
-    near_ref, charges_ref, points_ref, left_ref, right_ref, down_leaf_ref, out_ref, down_ref,
-    wide_ref, source_ref, target_ref, scratch_ref, weight_ref, kern_a_ref, kern_b_ref,
+    near_ref, charges_ref, points_ref, left_ref, right_ref, _, out_ref,
+    wide_ref, source_ref, target_ref, weight_ref, kern_a_ref, kern_b_ref,
 ):
     rhs, total = charges_ref.shape
-    entries, leaves = near_ref.shape
+    _, leaves = near_ref.shape
     size = total // leaves
     halo = REACH * size
     span = 2 * REACH + 1
     reach = (span + 1) * size
     pairs = leaves // 2
-    relayout(down_leaf_ref, scratch_ref)
-    down_ref[...] = scratch_ref[...].astype(BF16)
-
     wide_ref[:, :halo] = left_ref[:rhs, :]
     wide_ref[:, halo : halo + total] = charges_ref[...]
     wide_ref[:, halo + total :] = right_ref[:rhs, :]
@@ -246,7 +258,7 @@
     def evaluate(i, kern_ref):
         start = pl.multiple_of(i * 2 * size, 2 * size)
         square = dot_0(target_ref[:, pl.ds(start, 2 * size)], source_ref[:, pl.ds(start, reach)])
-        kern = lax.rsqrt(square.astype(BF16))
+        kern = kern_of(square)
         for h in range(2):
             weight = jnp.broadcast_to(weight_ref[h, pl.ds(2 * i + h, 1), :], (2 * ROWS, reach)).astype(BF16)
             for s in range(h * size, (h + 1) * size, 2 * ROWS):
@@ -254,7 +266,7 @@
 
     def apply(i, kern_ref):
         start = pl.multiple_of(i * 2 * size, 2 * size)
-        out_ref[:, pl.ds(start, 2 * size)] = INV_FOUR_PI * dot_t(wide_ref[:, pl.ds(start, reach)], kern_ref[...])
+        out_ref[:, pl.ds(start, 2 * size)] = dot_t(wide_ref[:, pl.ds(start, reach)], kern_ref[...])
 
     evaluate(0, kern_a_ref)
 
@@ -275,12 +287,34 @@
     moment_ref[slot + 1] = pair(low, other, tile)
 
 
+def part_of(parts, s, members):
+    length = parts[0].shape[0] // 2
+    owner = lax.rem(lax.axis_index("dev") - s // 2 * 2 + members, members)
+    owner = owner + s % 2 * (1 - 2 * lax.rem(owner, 2))
+    return parts[s // 2].at[s % 2 * length : (s % 2 + 1) * length], owner
+
+
+def top_kernel(*refs, members):
+    _, pgroup_ref, *parts, out_ref = refs
+    rhs = out_ref.shape[0] - ROWS
+    rank2 = out_ref.shape[1]
+    m_group = jnp.zeros((rhs, rank2), F32)
+    for s in range(members):
+        part, _ = part_of(parts, s, members)
+        base = part.shape[0] - rhs - ROWS
+        m_group = m_group + part[base : base + rhs, :].astype(F32)
+    out_ref[:rhs, :] = twice(m_group[:, rank2 // 2 :]).astype(BF16)
+    rows = source_rows(*[twice(pgroup_ref[c : c + 1, :].astype(F32)) for c in range(3)])
+    out_ref[rhs:, :] = stack_rows(rows).astype(BF16)
+
+
 def group_kernel(*refs, members):
-    far_ref, pgroup_ref = refs[:2]
-    parts = refs[2 : 2 + members]
-    fb_ref, ld_ref, out_ref = refs[2 + members : 5 + members]
-    moment_ref, source_ref, dev_m_ref, dev_source_ref = refs[5 + members :]
-    entries, branches = far_ref.shape
+    far_ref, _ = refs[:2]
+    count = members // 2
+    parts = refs[2 : 2 + count]
+    fb_ref, ld_ref = refs[2 + count : 4 + count]
+    moment_ref, source_ref, dev_m_ref, dev_source_ref = refs[4 + count :]
+    branches, entries = far_ref.shape
     rhs, rank2 = moment_ref.shape[1:]
     rank = rank2 // 2
     me = lax.axis_index("dev")
@@ -288,24 +322,18 @@
     tail = source_tail(rank2)
     first = branches // 2 * rhs
     base = first + branches // 2 * ROWS
-    m_group = jnp.zeros((rhs, rank2), F32)
-    for s, part in enumerate(parts):
-        owner = lax.rem(me - s + members, members)
+    for s in range(members):
+        part, owner = part_of(parts, s, members)
         for q in range(branches // 2):
             put_pair(moment_ref, owner * branches + 2 * q, part[q * rhs : (q + 1) * rhs, :])
             put_pair(source_ref, owner * branches + 2 * q, part[first + q * ROWS : first + (q + 1) * ROWS, :])
         mixed = part[base : base + rhs, :].astype(F32)
-        m_group = m_group + mixed
         keep = (jnp.abs(owner - me) >= 2).astype(F32)
         dev_m_ref[owner] = (pair(low, mixed, pltpu.roll(mixed, rank, 1)) * keep).astype(BF16)
         dev_source_ref[owner] = part[base + rhs :, :]
-    out_ref[:rhs, :] = twice(m_group[:, rank:]).astype(BF16)
-    rows = source_rows(*[twice(pgroup_ref[c : c + 1, :].astype(F32)) for c in range(3)])
-    out_ref[rhs:, :] = stack_rows(rows).astype(BF16)
-
     for c in range(branches):
         target = target_of(source_ref[me * branches + c][:, :rank])
-        fb_ref[c] = interact(target, [far_ref[e, c] for e in range(entries)], source_ref, tail, moment_ref)
+        fb_ref[c] = interact(target, [far_ref[c, e] for e in range(entries)], source_ref, tail, moment_ref)
     target = target_of(dev_source_ref[me][:, :rank])
     ld_ref[...] = interact(target, list(range(members)), dev_source_ref, tail, dev_m_ref)
 
@@ -368,7 +396,7 @@
         sums = []
         for h in range(2):
             b = 2 * i + h
-            far = INV_FOUR_PI * dot_t(gathered(named(b), moment_ref), kern_ref[h])
+            far = dot_t(gathered(named(b), moment_ref), kern_ref[h])
             rows = down_ref[pl.ds(pl.multiple_of(b * half, half), half), :]
             sums.append((far + dot_t(parent_ref[b // FAN], spread_rows(rows, low_d))).astype(BF16))
         return jnp.concatenate(sums, axis=0)
@@ -393,10 +421,16 @@
 
 VMEM = functools.partial(pl.BlockSpec, memory_space=pltpu.VMEM)
 SMEM = functools.partial(pl.BlockSpec, memory_space=pltpu.SMEM)
-
-
-def struct(shape, dtype):
+ANY = functools.partial(pl.BlockSpec, memory_space=pl.ANY)
+PARAMS = pltpu.CompilerParams()
+
+
+def hbm(shape, dtype):
     return jax.ShapeDtypeStruct(shape, dtype)
+
+
+def vmem(*arrays):
+    return [pltpu.with_memory_space_constraint(a, pltpu.VMEM) if a.size <= 1 << 19 else a for a in arrays]
 
 
 def on_device(
@@ -415,33 +449,37 @@
     rank2 = 2 * rank
     half = rank // 2
     halo = REACH * size
-    assert rank == size and slots % 2 == 0 and branches % 2 == 0
-
-    moments, own, listed = pl.pallas_call(
+    assert rank == size and slots % 2 == 0 and branches % 2 == 0 and members % 2 == 0
+
+    moments, own, listed, head, tail = pl.pallas_call(
         listed_kernel,
         out_shape=(
-            struct((leaves, rhs, rank2), BF16),
-            struct((leaves, ROWS, rank2), BF16),
-            struct((devices, slots // 2 * (rhs + ROWS), rank2), BF16),
+            pltpu.VMEM((leaves, rhs, rank2), BF16),
+            hbm((leaves, ROWS, rank2), BF16),
+            hbm((devices, slots // 2 * (rhs + ROWS), rank2), BF16),
+            hbm((rhs + ROWS, halo), BF16),
+            hbm((rhs + ROWS, halo), BF16),
         ),
-        in_specs=[SMEM(), VMEM(), VMEM(), VMEM()],
-        out_specs=(VMEM(), VMEM(), VMEM()),
+        in_specs=[SMEM()] + [VMEM()] * 4,
+        out_specs=(VMEM(),) * 5,
         scratch_shapes=[pltpu.VMEM((leaves * ROWS, rank2), F32)],
+        compiler_params=PARAMS,
         name="listed",
-    )(send_leaf, charges, basis, proxy_leaf)
+    )(send_leaf, charges, points, basis, proxy_leaf)
+    (moments,) = vmem(moments)
     received = lax.all_to_all(listed, ("grp", "dev"), split_axis=0, concat_axis=0, tiled=True)
 
-    stacked = jnp.concatenate([charges, points], axis=0)
     last = devices - 1
-    left = lax.ppermute(stacked[:, total - halo :], ("grp", "dev"), [(i, i + 1) for i in range(last)])
-    right = lax.ppermute(stacked[:, :halo], ("grp", "dev"), [(i + 1, i) for i in range(last)])
+    left = lax.ppermute(tail, ("grp", "dev"), [(i, i + 1) for i in range(last)])
+    right = lax.ppermute(head, ("grp", "dev"), [(i + 1, i) for i in range(last)])
 
     shared = pl.pallas_call(
         upward_kernel,
-        out_shape=struct(((branches // 2 + 1) * (rhs + ROWS), rank2), BF16),
+        out_shape=hbm(((branches // 2 + 1) * (rhs + ROWS), rank2), BF16),
         in_specs=[VMEM()] * 6,
         out_specs=VMEM(),
         scratch_shapes=[pltpu.VMEM((leaves * half, rank2), F32), pltpu.VMEM((rank * branches, rank2), F32)],
+        compiler_params=PARAMS,
         name="upward",
     )(
         moments,
@@ -451,49 +489,71 @@
         jnp.transpose(proxy_branch, (0, 2, 1)),
         proxy_device[:, :, 0],
     )
-    parts = [shared] + [
-        lax.ppermute(shared, "dev", [(i, (i + s) % members) for i in range(members)]) for s in range(1, members)
+    partner = lax.ppermute(shared, "dev", [(i, i ^ 1) for i in range(members)])
+    down = pl.pallas_call(
+        turn_kernel,
+        out_shape=hbm((leaves * half, rank2), BF16),
+        in_specs=[VMEM(), ANY()],
+        out_specs=VMEM(),
+        scratch_shapes=[pltpu.VMEM((leaves * half, rank2), F32)],
+        compiler_params=PARAMS,
+        name="turn",
+    )(down_leaf, shared)
+    partner, down = lax.optimization_barrier((partner, down))
+    both = jnp.concatenate([shared, partner], axis=0)
+    parts = [both] + [
+        lax.ppermute(both, "dev", [(i, (i + s) % members) for i in range(members)]) for s in range(2, members, 2)
     ]
 
     reach = (2 * REACH + 2) * size
-    near, down = pl.pallas_call(
+    near = pl.pallas_call(
         near_kernel,
-        out_shape=(struct((rhs, total), F32), struct((leaves * half, rank2), BF16)),
+        out_shape=pltpu.VMEM((rhs, total), F32),
         in_specs=[VMEM()] * 6,
-        out_specs=(VMEM(), VMEM()),
+        out_specs=VMEM(),
         scratch_shapes=[
             pltpu.VMEM((rhs, total + 2 * halo), BF16),
             pltpu.VMEM((2 * ROWS, total + 2 * halo), BF16),
             pltpu.VMEM((2 * ROWS, total), BF16),
-            pltpu.VMEM((leaves * half, rank2), F32),
             pltpu.VMEM((2, leaves, reach), F32),
             pltpu.VMEM((2 * size, reach), BF16),
             pltpu.VMEM((2 * size, reach), BF16),
         ],
+        compiler_params=PARAMS,
         name="near",
-    )(near_leaf, charges, points, left, right, down_leaf)
-
-    far_b, part_d, tile = pl.pallas_call(
+    )(near_leaf, charges, points, *vmem(left, right, both))
+
+    parts = vmem(*parts)
+    tile = pl.pallas_call(
+        functools.partial(top_kernel, members=members),
+        out_shape=hbm((rhs + ROWS, rank2), BF16),
+        in_specs=[VMEM()] * (2 + len(parts)),
+        out_specs=VMEM(),
+        compiler_params=PARAMS,
+        name="top",
+    )(*vmem(near), proxy_group[:, :, 0], *parts)
+    tiles = [tile] + [
+        lax.ppermute(tile, "grp", [(i, (i + s) % groups) for i in range(groups)]) for s in range(1, groups)
+    ]
+    far_b, part_d = pl.pallas_call(
         functools.partial(group_kernel, members=members),
-        out_shape=(struct((branches, rhs, rank), F32), struct((rhs, rank), F32), struct((rhs + ROWS, rank2), BF16)),
-        in_specs=[SMEM(), VMEM()] + [VMEM()] * members,
-        out_specs=(VMEM(), VMEM(), VMEM()),
+        out_shape=(hbm((branches, rhs, rank), F32), hbm((rhs, rank), F32)),
+        in_specs=[SMEM(), ANY()] + [VMEM()] * len(parts),
+        out_specs=(VMEM(), VMEM()),
         scratch_shapes=[
             pltpu.VMEM((members * branches, rhs, rank2), BF16),
             pltpu.VMEM((members * branches, ROWS, rank2), BF16),
             pltpu.VMEM((members, rhs, rank2), BF16),
             pltpu.VMEM((members, ROWS, rank2), BF16),
         ],
+        compiler_params=PARAMS,
         name="group",
-    )(far_branch, proxy_group[:, :, 0], *parts)
-    tiles = [tile] + [
-        lax.ppermute(tile, "grp", [(i, (i + s) % groups) for i in range(groups)]) for s in range(1, groups)
-    ]
+    )(jnp.transpose(far_branch), tile, *parts)
 
     table = leaves + devices * slots
     return pl.pallas_call(
         functools.partial(downward_kernel, groups=groups),
-        out_shape=struct((rhs, total), F32),
+        out_shape=hbm((rhs, total), F32),
         in_specs=[SMEM()] + [VMEM()] * (groups + 10),
         out_specs=VMEM(),
         scratch_shapes=[
@@ -506,10 +566,22 @@
             pltpu.VMEM((2, rank, far_leaf.shape[0] * rank), BF16),
             pltpu.VMEM((2, rank, far_leaf.shape[0] * rank), BF16),
         ],
+        compiler_params=PARAMS,
         name="downward",
     )(
-        far_leaf, *tiles, far_b, part_d, down_device[:, :, 0], jnp.transpose(down_branch, (0, 2, 1)), down, own,
-        moments, received, basis, near,
+        far_leaf,
+        tile,
+        *vmem(*tiles[1:]),
+        far_b,
+        part_d,
+        down_device[:, :, 0],
+        jnp.transpose(down_branch, (0, 2, 1)),
+        down,
+        own,
+        moments,
+        *vmem(received),
+        basis,
+        *vmem(near),
     )
 
 
@@ -517,4 +589,5 @@
     points = P(None, ("grp", "dev"))
     blocks = P(None, None, ("grp", "dev"))
     placed = (points,) * 3 + (blocks,) * 9 + (P(None, None, "grp"),) + (points,) * 4
+
     return jax.shard_map(on_device, mesh=mesh, in_specs=placed, out_specs=points, check_vma=False)

time: 74.1 us -> 63.9 us (0.86)
  the two profiles are of different devices: /device:TPU:0 before, /device:TPU:17 now
where the time goes in v3:
time: 63.9 us; the launch traced here: 63.5 us
  Pallas kernels  34.9 us (55%)
  starting transfers between devices  21.4 us (33%)
  waiting for transfers between devices  7.07 us (11%)
    pallas_call x1, Pallas kernels, on_device(): pl.pallas_call(functools.partial(downward_kernel, groups=groups), out_sha...  12.8 us
    pallas_call x1, Pallas kernels, on_device(): pl.pallas_call(near_kernel, out_shape=pltpu.VMEM((rhs, total), F32), in_s...  7.99 us
    ppermute x1, waiting for transfers between devices, on_device(): left = lax.ppermute(tail, ('grp', 'dev'), [(i, i + 1) for i in range(last)])  7.04 us
    all_to_all x1, starting transfers between devices, on_device(): lax.all_to_all(listed, ('grp', 'dev'), split_axis=0, concat_axis=0, tiled...  6.22 us
    ppermute x3, starting transfers between devices, on_device(): lax.ppermute(both, 'dev', [(i, (i + s) % members) for i in range(members)])  4.58 us
    ppermute x1, starting transfers between devices, on_device(): lax.ppermute(head, ('grp', 'dev'), [(i + 1, i) for i in range(last)])  4.26 us
    pallas_call x1, Pallas kernels, on_device(): pl.pallas_call(upward_kernel, out_shape=hbm(((branches // 2 + 1) * (rhs +...  3.77 us
    pallas_call x1, Pallas kernels, on_device(): pl.pallas_call(listed_kernel, out_shape=(pltpu.VMEM((leaves, rhs, rank2),...  3.76 us
  transfers between devices with their start and end apart: 10, of which 1 were waited for; matrix products, arithmetic and copies ran while one was open for 0% of the time, Pallas kernels for 29%

profile of v3, /device:TPU:17, one launch (start us, length us, event | category | flops | bytes accessed | tf_op | source)
XLA Modules:
  0.0 63.5 jit_solution(9815745055916458699)
XLA Ops:
  0.0 3.8 %listed.1 = (bf16[64,32,128]{2,1,0:T(8,128)(2,1)S(1)}, bf16[64,8,128]{2,1,0:T(8,128)(2,1)}, bf16[32,80,128]{2,1,0:T(8,128)(2,1)}, bf16[40,256]{1,0:T(8,128)(2,1)}, bf16[40,256]{1,0:T(8,128)(2,1)}) custom-call(s32[4,32]{1,0:T(4,128)} %send_ref.1, bf16[32,4096]{1,0:T(8,128)(2,1)} %charges_ref.3, bf16[3,4096]{1,0:T(4,128)(2,1)} %points_ref.3, ...), custom_call_target="tpu_custom_call" | custom-call | tf_op jit(solution)/shard_map/listed/pallas_call | solution.py:454
  3.8 6.2 %all-to-all-start = ((bf16[32,80,128]{2,1,0:T(8,128)(2,1)}), bf16[32,80,128]{2,1,0:T(8,128)(2,1)S(1)}, u32[]{:S(2)}, u32[]{:S(2)}) async-start(bf16[32,80,128]{2,1,0:T(8,128)(2,1)} %get-tuple-element.22), calls=%async_computation | async-start | bytes 1310720 | tf_op jit(solution)/shard_map/all_to_all | solution.py:470
  10.0 3.8 %upward.1._ = bf16[200,128]{1,0:T(8,128)(2,1)} custom-call(bf16[64,32,128]{2,1,0:T(8,128)(2,1)S(1)} %get-tuple-element.16.moment_ref.refs_11_, bf16[64,64,64]{2,1,0:T(8,128)(2,1)} %up_leaf_ref.1, bf16[64,8,64]{2,1,0:T(8,128)(2,1)} %bitcast.8, bf16[64,64]{1,0:T(8,128)(2,1)} %bitcast.10, bf16[3,8,64]{2,1,0:T(8,128)(2,1)} %bitcast.12, bf16[3,64]{1,0:T(4,128)(2,1)} %bitcast.14), custom_call_target="tpu_custom_call" | custom-call | tf_op jit(solution)/shard_map/upward/pallas_call | solution.py:476
  13.8 1.2 %collective-permute-start.2 = (bf16[200,128]{1,0:T(8,128)(2,1)}, bf16[200,128]{1,0:T(8,128)(2,1)S(1)}, u32[]{:S(2)}, u32[]{:S(2)}) collective-permute-start(bf16[200,128]{1,0:T(8,128)(2,1)} %upward.1._), channel_id=1, source_target_pairs={{0,1},{1,0},{2,3},{3,2},{4,5},{5,4},{6,7},{7,6},{8,9},{9,8},{10,11... | collective-permute-start | bytes 153608 | tf_op jit(solution)/shard_map/ppermute | solution.py:492
  15.0 2.9 %turn.1.refs_9_ = bf16[2048,128]{1,0:T(8,128)(2,1)} custom-call(bf16[64,64,64]{2,1,0:T(8,128)(2,1)} %down_leaf_ref.1, bf16[200,128]{1,0:T(8,128)(2,1)} %upward.1._), custom_call_target="tpu_custom_call" | custom-call | tf_op jit(solution)/shard_map/turn/pallas_call | solution.py:493
  17.9 0.0 collective-permute-done.2
  17.9 1.2 %collective-permute-start.5 = (bf16[400,128]{1,0:T(8,128)(2,1)S(1)}, bf16[400,128]{1,0:T(8,128)(2,1)S(1)}, u32[]{:S(2)}, u32[]{:S(2)}) collective-permute-start(bf16[400,128]{1,0:T(8,128)(2,1)S(1)} %pad_maximum_fusion._.refs_2_), channel_id=1, source_target_pairs={{0,6},{1,7},{2,0},{3,1},{4,2},{5,3},{6,4},{7,5},{8,14},{9,15},{10,... | collective-permute-start | bytes 307208 | tf_op jit(solution)/shard_map/ppermute | solution.py:505
  19.1 2.4 %collective-permute-start.4 = (bf16[400,128]{1,0:T(8,128)(2,1)S(1)}, bf16[400,128]{1,0:T(8,128)(2,1)S(1)}, u32[]{:S(2)}, u32[]{:S(2)}) collective-permute-start(bf16[400,128]{1,0:T(8,128)(2,1)S(1)} %pad_maximum_fusion._.refs_2_), channel_id=1, source_target_pairs={{0,4},{1,5},{2,6},{3,7},{4,0},{5,1},{6,2},{7,3},{8,12},{9,13},{10,... | collective-permute-start | bytes 307208 | tf_op jit(solution)/shard_map/ppermute | solution.py:505
  21.6 0.9 %collective-permute-start.3 = (bf16[400,128]{1,0:T(8,128)(2,1)S(1)}, bf16[400,128]{1,0:T(8,128)(2,1)S(1)}, u32[]{:S(2)}, u32[]{:S(2)}) collective-permute-start(bf16[400,128]{1,0:T(8,128)(2,1)S(1)} %pad_maximum_fusion._.refs_2_), channel_id=1, source_target_pairs={{0,2},{1,3},{2,4},{3,5},{4,6},{5,7},{6,0},{7,1},{8,10},{9,11},{10,... | collective-permute-start | bytes 307208 | tf_op jit(solution)/shard_map/ppermute | solution.py:505
  22.5 1.9 %collective-permute-start = (bf16[40,256]{1,0:T(8,128)(2,1)S(1)}, bf16[40,256]{1,0:T(8,128)(2,1)S(1)}, u32[]{:S(2)}, u32[]{:S(2)}) collective-permute-start(bf16[40,256]{1,0:T(8,128)(2,1)S(1)} %copy-done.2), channel_id=1, source_target_pairs={{0,1},{1,2},{2,3},{3,4},{4,5},{5,6},{6,7},{7,8},{8,9},{9,10},{10,1... | collective-permute-start | bytes 61448 | tf_op jit(solution)/shard_map/ppermute | solution.py:473
  24.4 4.3 %collective-permute-start.1 = (bf16[40,256]{1,0:T(8,128)(2,1)S(1)}, bf16[40,256]{1,0:T(8,128)(2,1)S(1)}, u32[]{:S(2)}, u32[]{:S(2)}) collective-permute-start(bf16[40,256]{1,0:T(8,128)(2,1)S(1)} %copy-done.1), channel_id=1, source_target_pairs={{1,0},{2,1},{3,2},{4,3},{5,4},{6,5},{7,6},{8,7},{9,8},{10,9},{11,1... | collective-permute-start | bytes 61448 | tf_op jit(solution)/shard_map/ppermute | solution.py:474
  28.7 7.0 %collective-permute-done.left_ref = bf16[40,256]{1,0:T(8,128)(2,1)S(1)} collective-permute-done((bf16[40,256]{1,0:T(8,128)(2,1)S(1)}, bf16[40,256]{1,0:T(8,128)(2,1)S(1)}, u32[]{:S(2)}, u32[]{:S(2)}) %collective-permute-start) | collective-permute-done | bytes 20512 | tf_op jit(solution)/shard_map/ppermute | solution.py:473
  35.7 0.0 collective-permute-done.1.right_ref
  35.7 8.0 %near.1.refs_0_.refs_14_ = f32[32,4096]{1,0:T(8,128)S(1)} custom-call(s32[16,64]{1,0:T(8,128)} %near_ref.1, bf16[32,4096]{1,0:T(8,128)(2,1)} %charges_ref.3, bf16[3,4096]{1,0:T(4,128)(2,1)} %points_ref.3, bf16[40,256]{1,0:T(8,128)(2,1)S(1)} %collective-permute-done.left_ref, bf16[40,256]{1,0:T(8,128)(2,1)S(1)} %collective-permute-done.1.right_ref, ...), custom_call_target="tpu_custom_call" | custom-call | tf_op jit(solution)/shard_map/near/pallas_call | solution.py:509
  43.7 0.0 collective-permute-done.5.refs_5_
  43.7 0.0 collective-permute-done.4.refs_4_
  43.7 1.4 %top.1.refs_1_ = bf16[40,128]{1,0:T(8,128)(2,1)} custom-call(f32[32,4096]{1,0:T(8,128)S(1)} %near.1.refs_0_.refs_14_, bf16[3,64]{1,0:T(4,128)(2,1)} %bitcast.15, bf16[400,128]{1,0:T(8,128)(2,1)S(1)} %pad_maximum_fusion._.refs_2_, bf16[400,128]{1,0:T(8,128)(2,1)S(1)} %collective-permute-done.3.refs_3_, bf16[400,128]{1,0:T(8,128)(2,1)S(1)} %collective-permute-done.4.refs_4_, ...), custom_call_target="tpu_custom_call" | custom-call | tf_op jit(solution)/shard_map/top/pallas_call | solution.py:527
  45.1 0.4 collective-permute-start.8
  45.6 1.2 %collective-permute-start.7 = (bf16[40,128]{1,0:T(8,128)(2,1)}, bf16[40,128]{1,0:T(8,128)(2,1)S(1)}, u32[]{:S(2)}, u32[]{:S(2)}) collective-permute-start(bf16[40,128]{1,0:T(8,128)(2,1)} %top.1.refs_1_), channel_id=1, source_target_pairs={{0,16},{8,24},{16,0},{24,8},{1,17},{9,25},{17,1},{25,9},{2,18},{10... | collective-permute-start | bytes 30728 | tf_op jit(solution)/shard_map/ppermute | solution.py:536
  46.7 1.6 %collective-permute-start.6 = (bf16[40,128]{1,0:T(8,128)(2,1)}, bf16[40,128]{1,0:T(8,128)(2,1)S(1)}, u32[]{:S(2)}, u32[]{:S(2)}) collective-permute-start(bf16[40,128]{1,0:T(8,128)(2,1)} %top.1.refs_1_), channel_id=1, source_target_pairs={{0,8},{8,16},{16,24},{24,0},{1,9},{9,17},{17,25},{25,1},{2,10},{10... | collective-permute-start | bytes 30728 | tf_op jit(solution)/shard_map/ppermute | solution.py:536
  48.3 2.4 %group.1 = (f32[8,32,64]{2,1,0:T(8,128)}, f32[32,64]{1,0:T(8,128)}) custom-call(s32[8,16]{1,0:T(8,128)} %bitcast.13, bf16[40,128]{1,0:T(8,128)(2,1)} %top.1.refs_1_, bf16[400,128]{1,0:T(8,128)(2,1)S(1)} %pad_maximum_fusion._.refs_2_, bf16[400,128]{1,0:T(8,128)(2,1)S(1)} %collective-permute-done.3.refs_3_, ...), custom_call_target="tpu_custom_call" | custom-call | tf_op jit(solution)/shard_map/group/pallas_call | solution.py:538
  50.7 0.0 collective-permute-done.8.refs_4_
  50.7 0.0 collective-permute-done.7.refs_3_
  50.7 12.8 %downward.1 = f32[32,4096]{1,0:T(8,128)} custom-call(s32[16,64]{1,0:T(8,128)} %refs_0_.1, bf16[40,128]{1,0:T(8,128)(2,1)} %top.1.refs_1_, bf16[40,128]{1,0:T(8,128)(2,1)S(1)} %collective-permute-done.6.refs_2_, bf16[40,128]{1,0:T(8,128)(2,1)S(1)} %collective-permute-done.7.refs_3_, bf16[40,128]{1,0:T(8,128)(2,1)S(1)} %collective-permute-done.8.refs_4_, ...), custom_call_target="tpu_custom_call" | custom-call | tf_op jit(solution)/shard_map/downward/pallas_call | solution.py:554
  (10 shorter events, 0.0 us)
Async XLA Ops:
  3.8 46.9 %all-to-all-start = ((bf16[32,80,128]{2,1,0:T(8,128)(2,1)}), bf16[32,80,128]{2,1,0:T(8,128)(2,1)S(1)}, u32[]{:S(2)}, u32[]{:S(2)}) async-start(bf16[32,80,128]{2,1,0:T(8,128)(2,1)} %get-tuple-element.22), calls=%async_computation | async-start | bytes 1310720 | tf_op jit(solution)/shard_map/all_to_all | solution.py:470
  13.8 4.1 %copy-start = (bf16[200,128]{1,0:T(8,128)(2,1)S(1)}, bf16[200,128]{1,0:T(8,128)(2,1)}, u32[]{:S(2)}) copy-start(bf16[200,128]{1,0:T(8,128)(2,1)} %upward.1._) | copy-start | bytes 153604
  13.8 4.1 %collective-permute-start.2 = (bf16[200,128]{1,0:T(8,128)(2,1)}, bf16[200,128]{1,0:T(8,128)(2,1)S(1)}, u32[]{:S(2)}, u32[]{:S(2)}) collective-permute-start(bf16[200,128]{1,0:T(8,128)(2,1)} %upward.1._), channel_id=1, source_target_pairs={{0,1},{1,0},{2,3},{3,2},{4,5},{5,4},{6,7},{7,6},{8,9},{9,8},{10,11... | collective-permute-start | bytes 153608 | tf_op jit(solution)/shard_map/ppermute | solution.py:492
  17.9 4.6 %copy-start.2 = (bf16[40,256]{1,0:T(8,128)(2,1)S(1)}, bf16[40,256]{1,0:T(8,128)(2,1)}, u32[]{:S(2)}) copy-start(bf16[40,256]{1,0:T(8,128)(2,1)} %get-tuple-element.14) | copy-start | bytes 61444
  17.9 6.5 %copy-start.1 = (bf16[40,256]{1,0:T(8,128)(2,1)S(1)}, bf16[40,256]{1,0:T(8,128)(2,1)}, u32[]{:S(2)}) copy-start(bf16[40,256]{1,0:T(8,128)(2,1)} %get-tuple-element.15) | copy-start | bytes 61444
  17.9 25.8 %collective-permute-start.5 = (bf16[400,128]{1,0:T(8,128)(2,1)S(1)}, bf16[400,128]{1,0:T(8,128)(2,1)S(1)}, u32[]{:S(2)}, u32[]{:S(2)}) collective-permute-start(bf16[400,128]{1,0:T(8,128)(2,1)S(1)} %pad_maximum_fusion._.refs_2_), channel_id=1, source_target_pairs={{0,6},{1,7},{2,0},{3,1},{4,2},{5,3},{6,4},{7,5},{8,14},{9,15},{10,... | collective-permute-start | bytes 307208 | tf_op jit(solution)/shard_map/ppermute | solution.py:505
  19.1 24.6 %collective-permute-start.4 = (bf16[400,128]{1,0:T(8,128)(2,1)S(1)}, bf16[400,128]{1,0:T(8,128)(2,1)S(1)}, u32[]{:S(2)}, u32[]{:S(2)}) collective-permute-start(bf16[400,128]{1,0:T(8,128)(2,1)S(1)} %pad_maximum_fusion._.refs_2_), channel_id=1, source_target_pairs={{0,4},{1,5},{2,6},{3,7},{4,0},{5,1},{6,2},{7,3},{8,12},{9,13},{10,... | collective-permute-start | bytes 307208 | tf_op jit(solution)/shard_map/ppermute | solution.py:505
  21.6 22.2 %collective-permute-start.3 = (bf16[400,128]{1,0:T(8,128)(2,1)S(1)}, bf16[400,128]{1,0:T(8,128)(2,1)S(1)}, u32[]{:S(2)}, u32[]{:S(2)}) collective-permute-start(bf16[400,128]{1,0:T(8,128)(2,1)S(1)} %pad_maximum_fusion._.refs_2_), channel_id=1, source_target_pairs={{0,2},{1,3},{2,4},{3,5},{4,6},{5,7},{6,0},{7,1},{8,10},{9,11},{10,... | collective-permute-start | bytes 307208 | tf_op jit(solution)/shard_map/ppermute | solution.py:505
  22.5 13.2 %collective-permute-start = (bf16[40,256]{1,0:T(8,128)(2,1)S(1)}, bf16[40,256]{1,0:T(8,128)(2,1)S(1)}, u32[]{:S(2)}, u32[]{:S(2)}) collective-permute-start(bf16[40,256]{1,0:T(8,128)(2,1)S(1)} %copy-done.2), channel_id=1, source_target_pairs={{0,1},{1,2},{2,3},{3,4},{4,5},{5,6},{6,7},{7,8},{8,9},{9,10},{10,1... | collective-permute-start | bytes 61448 | tf_op jit(solution)/shard_map/ppermute | solution.py:473
  24.4 11.3 %collective-permute-start.1 = (bf16[40,256]{1,0:T(8,128)(2,1)S(1)}, bf16[40,256]{1,0:T(8,128)(2,1)S(1)}, u32[]{:S(2)}, u32[]{:S(2)}) collective-permute-start(bf16[40,256]{1,0:T(8,128)(2,1)S(1)} %copy-done.1), channel_id=1, source_target_pairs={{1,0},{2,1},{3,2},{4,3},{5,4},{6,5},{7,6},{8,7},{9,8},{10,9},{11,1... | collective-permute-start | bytes 61448 | tf_op jit(solution)/shard_map/ppermute | solution.py:474
  45.1 5.6 %collective-permute-start.8 = (bf16[40,128]{1,0:T(8,128)(2,1)}, bf16[40,128]{1,0:T(8,128)(2,1)S(1)}, u32[]{:S(2)}, u32[]{:S(2)}) collective-permute-start(bf16[40,128]{1,0:T(8,128)(2,1)} %top.1.refs_1_), channel_id=1, source_target_pairs={{0,24},{8,0},{16,8},{24,16},{1,25},{9,1},{17,9},{25,17},{2,26},{10... | collective-permute-start | bytes 30728 | tf_op jit(solution)/shard_map/ppermute | solution.py:536
  45.6 5.1 %collective-permute-start.7 = (bf16[40,128]{1,0:T(8,128)(2,1)}, bf16[40,128]{1,0:T(8,128)(2,1)S(1)}, u32[]{:S(2)}, u32[]{:S(2)}) collective-permute-start(bf16[40,128]{1,0:T(8,128)(2,1)} %top.1.refs_1_), channel_id=1, source_target_pairs={{0,16},{8,24},{16,0},{24,8},{1,17},{9,25},{17,1},{25,9},{2,18},{10... | collective-permute-start | bytes 30728 | tf_op jit(solution)/shard_map/ppermute | solution.py:536
  46.7 4.0 %collective-permute-start.6 = (bf16[40,128]{1,0:T(8,128)(2,1)}, bf16[40,128]{1,0:T(8,128)(2,1)S(1)}, u32[]{:S(2)}, u32[]{:S(2)}) collective-permute-start(bf16[40,128]{1,0:T(8,128)(2,1)} %top.1.refs_1_), channel_id=1, source_target_pairs={{0,8},{8,16},{16,24},{24,0},{1,9},{9,17},{17,25},{25,1},{2,10},{10... | collective-permute-start | bytes 30728 | tf_op jit(solution)/shard_map/ppermute | solution.py:536

commit v4 on v3

--- a/solution.py
+++ b/solution.py
@@ -10,6 +10,8 @@
 
 REACH = 4
 FAN = 8
+ROUND = 8
+PAIRS = 4
 
 INV_FOUR_PI = 1.0 / (4.0 * math.pi)
 SOFTEN = 0.25
@@ -116,7 +118,7 @@
 
 
 def listed_kernel(
-    send_ref, charges_ref, points_ref, basis_ref, proxy_ref, moment_ref, own_ref, out_ref, head_ref, last_ref, tile_ref
+    send_ref, charges_ref, points_ref, basis_ref, proxy_ref, moment_ref, own_ref, out_ref, inner_ref, outer_ref, tile_ref
 ):
     slots, devices = send_ref.shape
     leaves, rhs, rank2 = moment_ref.shape
@@ -149,11 +151,17 @@
 
     lax.fori_loop(0, devices, pack, 0, unroll=4)
     total = charges_ref.shape[1]
-    halo = head_ref.shape[1]
-    for ref, start in ((head_ref, 0), (last_ref, total - halo)):
-        ref[:rhs, :] = charges_ref[:, start : start + halo]
-        ref[rhs:, :] = jnp.zeros((ROWS, halo), BF16)
-        ref[rhs : rhs + 3, :] = points_ref[:, start : start + halo]
+    halo = inner_ref.shape[0] // (rhs + ROWS) * rank2
+    odd = lax.rem(lax.axis_index("dev"), 2) == 1
+    for ref, first in ((inner_ref, odd), (outer_ref, jnp.logical_not(odd))):
+        start = jnp.where(first, 0, total - halo)
+        for n in range(halo // rank2):
+            columns = pl.ds(pl.multiple_of(start + n * rank2, rank2), rank2)
+            base = n * (rhs + ROWS)
+            ref[base : base + rhs, :] = charges_ref[:, columns]
+            points = points_ref[:, columns].astype(F32)
+            rows = jnp.concatenate([points, jnp.zeros((ROWS - 3, rank2), F32)], axis=0)
+            ref[base + rhs : base + rhs + ROWS, :] = rows.astype(BF16)
 
 
 def relayout(x_ref, scratch_ref):
@@ -218,13 +226,14 @@
     out_ref[base + rhs :, :] = stack_rows(rows).astype(BF16)
 
 
-def turn_kernel(down_leaf_ref, _, down_ref, scratch_ref):
+def turn_kernel(down_leaf_ref, far_ref, _, down_ref, turned_ref, scratch_ref):
+    turned_ref[...] = jnp.transpose(far_ref[...].astype(F32)).astype(jnp.int32)
     relayout(down_leaf_ref, scratch_ref)
     down_ref[...] = scratch_ref[...].astype(BF16)
 
 
 def near_kernel(
-    near_ref, charges_ref, points_ref, left_ref, right_ref, _, out_ref,
+    near_ref, charges_ref, points_ref, inner_ref, outer_ref, _, out_ref,
     wide_ref, source_ref, target_ref, weight_ref, kern_a_ref, kern_b_ref,
 ):
     rhs, total = charges_ref.shape
@@ -233,14 +242,20 @@
     halo = REACH * size
     span = 2 * REACH + 1
     reach = (span + 1) * size
-    pairs = leaves // 2
-    wide_ref[:, :halo] = left_ref[:rhs, :]
+    odd = lax.rem(lax.axis_index("dev"), 2) == 1
     wide_ref[:, halo : halo + total] = charges_ref[...]
-    wide_ref[:, halo + total :] = right_ref[:rhs, :]
+    lanes = 2 * size
+    sides = [[], []]
+    for n in range(halo // lanes):
+        rows = slice(n * (rhs + ROWS), (n + 1) * (rhs + ROWS))
+        inner, outer = inner_ref[rows, :], outer_ref[rows, :]
+        for side, block in enumerate((jnp.where(odd, inner, outer), jnp.where(odd, outer, inner))):
+            start = side * (halo + total) + n * lanes
+            wide_ref[:, start : start + lanes] = block[:rhs, :]
+            sides[side].append(block[rhs:, :].astype(F32))
+    left, right = (jnp.concatenate(side, axis=1) for side in sides)
     coords = [
-        jnp.concatenate(
-            [left_ref[rhs + c : rhs + c + 1, :], points_ref[c : c + 1, :], right_ref[rhs + c : rhs + c + 1, :]], axis=1
-        ).astype(F32)
+        jnp.concatenate([left[c : c + 1, :], points_ref[c : c + 1, :].astype(F32), right[c : c + 1, :]], axis=1)
         for c in range(3)
     ]
     rows = stack_rows(source_rows(*coords))
@@ -256,41 +271,44 @@
         weight_ref[h] = dot_0(counts, (block == offset + h).astype(BF16))
 
     def evaluate(i, kern_ref):
-        start = pl.multiple_of(i * 2 * size, 2 * size)
-        square = dot_0(target_ref[:, pl.ds(start, 2 * size)], source_ref[:, pl.ds(start, reach)])
-        kern = kern_of(square)
-        for h in range(2):
-            weight = jnp.broadcast_to(weight_ref[h, pl.ds(2 * i + h, 1), :], (2 * ROWS, reach)).astype(BF16)
-            for s in range(h * size, (h + 1) * size, 2 * ROWS):
-                kern_ref[s : s + 2 * ROWS, :] = kern[s : s + 2 * ROWS, :] * weight
+        for n in range(width):
+            j = i * width + n
+            start = pl.multiple_of(j * 2 * size, 2 * size)
+            kern = kern_of(dot_0(target_ref[:, pl.ds(start, 2 * size)], source_ref[:, pl.ds(start, reach)]))
+            for h in range(2):
+                weight = jnp.broadcast_to(weight_ref[h, pl.ds(2 * j + h, 1), :], (2 * ROWS, reach)).astype(BF16)
+                for s in range(h * size, (h + 1) * size, 2 * ROWS):
+                    kern_ref[n, s : s + 2 * ROWS, :] = kern[s : s + 2 * ROWS, :] * weight
 
     def apply(i, kern_ref):
-        start = pl.multiple_of(i * 2 * size, 2 * size)
-        out_ref[:, pl.ds(start, 2 * size)] = dot_t(wide_ref[:, pl.ds(start, reach)], kern_ref[...])
-
+        for n in range(width):
+            start = pl.multiple_of((i * width + n) * 2 * size, 2 * size)
+            out_ref[:, pl.ds(start, 2 * size)] = dot_t(wide_ref[:, pl.ds(start, reach)], kern_ref[n])
+
+    width = kern_a_ref.shape[0]
+    rounds = leaves // 2 // width
     evaluate(0, kern_a_ref)
 
     def step(t, carry):
+        evaluate(2 * t + 1, kern_b_ref)
         apply(2 * t, kern_a_ref)
-        evaluate(2 * t + 1, kern_b_ref)
-        evaluate(jnp.minimum(2 * t + 2, pairs - 1), kern_a_ref)
+        evaluate(jnp.minimum(2 * t + 2, rounds - 1), kern_a_ref)
         apply(2 * t + 1, kern_b_ref)
         return carry
 
-    lax.fori_loop(0, pairs // 2, step, 0)
-
-
-def put_pair(moment_ref, slot, tile):
+    lax.fori_loop(0, rounds // 2, step, 0)
+
+
+def put_pair(ref, slot, tile, row=0):
     low = low_half(tile.shape)
     other = swap(tile)
-    moment_ref[slot] = pair(low, tile, other)
-    moment_ref[slot + 1] = pair(low, other, tile)
+    ref[slot, row : row + tile.shape[0], :] = pair(low, tile, other)
+    ref[slot + 1, row : row + tile.shape[0], :] = pair(low, other, tile)
 
 
 def part_of(parts, s, members):
     length = parts[0].shape[0] // 2
-    owner = lax.rem(lax.axis_index("dev") - s // 2 * 2 + members, members)
-    owner = owner + s % 2 * (1 - 2 * lax.rem(owner, 2))
+    owner = lax.axis_index("dev") ^ (s // 2 + s % 2 * (members // 2))
     return parts[s // 2].at[s % 2 * length : (s % 2 + 1) * length], owner
 
 
@@ -343,22 +361,21 @@
     tiles = refs[1 : 1 + groups]
     (
         fb_ref, ld_ref, down_device_ref, down_branch_ref, down_ref, own_ref, own_m_ref, recv_ref, basis_ref, near_ref,
-        out_ref, moment_ref, source_ref, grp_m_ref, grp_source_ref, branch_ref, parent_ref, kern_a_ref, kern_b_ref,
+        out_ref, table_ref, grp_m_ref, grp_source_ref, branch_ref, parent_ref, *buffers,
     ) = refs[1 + groups :]
-    entries, leaves = far_ref.shape
-    rhs, rank2 = moment_ref.shape[1:]
+    leaves, entries = far_ref.shape
+    rhs, rank2 = parent_ref.shape[1:]
     rank = rank2 // 2
     half = rank // 2
     branches = leaves // FAN
     devices = recv_ref.shape[0]
-    slots = (moment_ref.shape[0] - leaves) // devices
-    pairs = leaves // 2
+    slots = (table_ref.shape[0] - leaves) // devices
     me = lax.axis_index("grp")
     low = low_half((rhs, rank2))
     tail = source_tail(rank2)
 
     for s, tile_ref in enumerate(tiles):
-        owner = lax.rem(me - s + groups, groups)
+        owner = me ^ s
         keep = (jnp.abs(owner - me) >= 2).astype(F32)
         grp_m_ref[owner] = (tile_ref[:rhs, :].astype(F32) * keep).astype(BF16)
         grp_source_ref[owner] = tile_ref[rhs:, :]
@@ -370,53 +387,80 @@
         matrix = branch_ref[pl.ds(c, rank, stride=branches), :][:, :rank].astype(BF16)
         parent_ref[c] = twice((fb_ref[c] + dot_t(l_device, matrix)).astype(BF16))
 
-    moment_ref[:leaves] = own_m_ref[...]
-    source_ref[:leaves] = own_ref[...]
+    table_ref[:leaves, :rhs, :] = own_m_ref[...]
+    table_ref[:leaves, rhs:, :] = own_ref[...]
     base = slots // 2 * rhs
 
     def unpack(p, carry):
         for q in range(slots // 2):
             slot = leaves + p * slots + 2 * q
-            put_pair(moment_ref, slot, recv_ref[p, q * rhs : (q + 1) * rhs, :])
-            put_pair(source_ref, slot, recv_ref[p, base + q * ROWS : base + (q + 1) * ROWS, :])
+            put_pair(table_ref, slot, recv_ref[p, q * rhs : (q + 1) * rhs, :], 0)
+            put_pair(table_ref, slot, recv_ref[p, base + q * ROWS : base + (q + 1) * ROWS, :], rhs)
         return carry
 
     lax.fori_loop(0, devices, unpack, 0, unroll=4)
     low_d = low_half((half, rank2))
 
-    def named(b):
-        return [far_ref[e, b] for e in range(entries)]
-
-    def evaluate(i, kern_ref):
-        for h in range(2):
-            b = 2 * i + h
-            kern_ref[h] = couplings(target_of(source_ref[b][:, :rank]), named(b), source_ref, tail)
-
-    def apply(i, kern_ref):
+    width = buffers[0].shape[0]
+    rounds = leaves // width
+    low_s = low_half((ROWS, rank2))
+
+    def gather(b, low, rows, ref):
+        for e in range(0, entries, 2):
+            first, second = far_ref[b, e], far_ref[b, e + 1]
+            ref[:, e * rank : (e + 2) * rank] = pair(low, table_ref[first, rows, :], table_ref[second, rows, :])
+
+    def collect_sources(i, targets_ref, sources_ref):
+        for h in range(width):
+            b = width * i + h
+            targets_ref[h] = jnp.transpose(target_of(table_ref[b, rhs:, :rank]))
+            gather(b, low_s, slice(rhs, None), sources_ref.at[h])
+
+    def collect_moments(i, moments_ref):
+        for h in range(width):
+            gather(width * i + h, low, slice(None, rhs), moments_ref.at[h])
+
+    def evaluate(targets_ref, sources_ref, kern_ref):
+        for h in range(width):
+            sources = jnp.concatenate([sources_ref[h], source_tail(sources_ref.shape[2])], axis=0)
+            kern_ref[h] = kern_of(dot(targets_ref[h], sources))
+
+    def apply(i, moments_ref, kern_ref):
         sums = []
-        for h in range(2):
-            b = 2 * i + h
-            far = dot_t(gathered(named(b), moment_ref), kern_ref[h])
+        for h in range(width):
+            b = width * i + h
+            far = dot_t(moments_ref[h], kern_ref[h])
             rows = down_ref[pl.ds(pl.multiple_of(b * half, half), half), :]
             sums.append((far + dot_t(parent_ref[b // FAN], spread_rows(rows, low_d))).astype(BF16))
-        return jnp.concatenate(sums, axis=0)
+        return tuple(sums)
 
     def finish(i, sums):
-        columns = pl.ds(pl.multiple_of(i * rank2, rank2), rank2)
-        product = dot(sums, basis_ref[:, columns])
-        out_ref[:, columns] = near_ref[:, columns] + pair(low, product[:rhs], product[rhs:])
-
-    evaluate(0, kern_a_ref)
+        for h in range(0, width, 2):
+            columns = pl.ds(pl.multiple_of((width * i + h) * rank, rank2), rank2)
+            product = dot(jnp.concatenate(sums[h : h + 2], axis=0), basis_ref[:, columns])
+            out_ref[:, columns] = near_ref[:, columns] + pair(low, product[:rhs], product[rhs:])
+
+    def stage(i, sums, this, other):
+        finish(jnp.maximum(i - 2, 0), sums)
+        evaluate(this[0], this[1], this[3])
+        sums = apply(jnp.maximum(i - 1, 0), other[2], other[3])
+        collect_sources(jnp.minimum(i + 2, rounds - 1), this[0], this[1])
+        collect_moments(jnp.minimum(i + 1, rounds - 1), other[2])
+        return sums
+
+    even, odd = buffers[:4], buffers[4:]
+    collect_sources(0, *even[:2])
+    collect_sources(1, *odd[:2])
+    collect_moments(0, even[2])
+    odd[2][...] = jnp.zeros_like(odd[2])
+    odd[3][...] = jnp.zeros_like(odd[3])
 
     def step(t, sums):
-        finish(jnp.maximum(2 * t - 1, 0), sums)
-        sums = apply(2 * t, kern_a_ref)
-        evaluate(2 * t + 1, kern_b_ref)
-        finish(2 * t, sums)
-        evaluate(jnp.minimum(2 * t + 2, pairs - 1), kern_a_ref)
-        return apply(2 * t + 1, kern_b_ref)
-
-    finish(pairs - 1, lax.fori_loop(0, pairs // 2, step, jnp.zeros((2 * rhs, rank), BF16)))
+        return stage(2 * t + 1, stage(2 * t, sums, even, odd), odd, even)
+
+    sums = lax.fori_loop(0, rounds // 2, step, (jnp.zeros((rhs, rank), BF16),) * width)
+    finish(rounds - 2, sums)
+    finish(rounds - 1, apply(rounds - 1, odd[2], odd[3]))
 
 
 VMEM = functools.partial(pl.BlockSpec, memory_space=pltpu.VMEM)
@@ -451,14 +495,14 @@
     halo = REACH * size
     assert rank == size and slots % 2 == 0 and branches % 2 == 0 and members % 2 == 0
 
-    moments, own, listed, head, tail = pl.pallas_call(
+    moments, own, listed, inner, outer = pl.pallas_call(
         listed_kernel,
         out_shape=(
             pltpu.VMEM((leaves, rhs, rank2), BF16),
             hbm((leaves, ROWS, rank2), BF16),
             hbm((devices, slots // 2 * (rhs + ROWS), rank2), BF16),
-            hbm((rhs + ROWS, halo), BF16),
-            hbm((rhs + ROWS, halo), BF16),
+            pltpu.VMEM((halo // rank2 * (rhs + ROWS), rank2), BF16),
+            pltpu.VMEM((halo // rank2 * (rhs + ROWS), rank2), BF16),
         ),
         in_specs=[SMEM()] + [VMEM()] * 4,
         out_specs=(VMEM(),) * 5,
@@ -469,9 +513,9 @@
     (moments,) = vmem(moments)
     received = lax.all_to_all(listed, ("grp", "dev"), split_axis=0, concat_axis=0, tiled=True)
 
-    last = devices - 1
-    left = lax.ppermute(tail, ("grp", "dev"), [(i, i + 1) for i in range(last)])
-    right = lax.ppermute(head, ("grp", "dev"), [(i + 1, i) for i in range(last)])
+    swaps = [(i, i + 1 if i % 2 else i - 1) for i in range(1, devices - 1)]
+    outer = lax.ppermute(outer, ("grp", "dev"), swaps)
+    inner = lax.ppermute(inner, "dev", [(i, i ^ 1) for i in range(members)])
 
     shared = pl.pallas_call(
         upward_kernel,
@@ -489,20 +533,20 @@
         jnp.transpose(proxy_branch, (0, 2, 1)),
         proxy_device[:, :, 0],
     )
-    partner = lax.ppermute(shared, "dev", [(i, i ^ 1) for i in range(members)])
-    down = pl.pallas_call(
+    partner = lax.ppermute(shared, "dev", [(i, i ^ members // 2) for i in range(members)])
+    down, far_turned = pl.pallas_call(
         turn_kernel,
-        out_shape=hbm((leaves * half, rank2), BF16),
-        in_specs=[VMEM(), ANY()],
-        out_specs=VMEM(),
+        out_shape=(pltpu.VMEM((leaves * half, rank2), BF16), hbm(far_leaf.shape[::-1], jnp.int32)),
+        in_specs=[VMEM(), VMEM(), ANY()],
+        out_specs=(VMEM(), VMEM()),
         scratch_shapes=[pltpu.VMEM((leaves * half, rank2), F32)],
         compiler_params=PARAMS,
         name="turn",
-    )(down_leaf, shared)
+    )(down_leaf, far_leaf, shared)
     partner, down = lax.optimization_barrier((partner, down))
     both = jnp.concatenate([shared, partner], axis=0)
     parts = [both] + [
-        lax.ppermute(both, "dev", [(i, (i + s) % members) for i in range(members)]) for s in range(2, members, 2)
+        lax.ppermute(both, "dev", [(i, i ^ s) for i in range(members)]) for s in range(1, members // 2)
     ]
 
     reach = (2 * REACH + 2) * size
@@ -516,12 +560,12 @@
             pltpu.VMEM((2 * ROWS, total + 2 * halo), BF16),
             pltpu.VMEM((2 * ROWS, total), BF16),
             pltpu.VMEM((2, leaves, reach), F32),
-            pltpu.VMEM((2 * size, reach), BF16),
-            pltpu.VMEM((2 * size, reach), BF16),
+            pltpu.VMEM((PAIRS, 2 * size, reach), BF16),
+            pltpu.VMEM((PAIRS, 2 * size, reach), BF16),
         ],
         compiler_params=PARAMS,
         name="near",
-    )(near_leaf, charges, points, *vmem(left, right, both))
+    )(near_leaf, charges, points, *vmem(inner, outer, both))
 
     parts = vmem(*parts)
     tile = pl.pallas_call(
@@ -532,9 +576,8 @@
         compiler_params=PARAMS,
         name="top",
     )(*vmem(near), proxy_group[:, :, 0], *parts)
-    tiles = [tile] + [
-        lax.ppermute(tile, "grp", [(i, (i + s) % groups) for i in range(groups)]) for s in range(1, groups)
-    ]
+    assert groups & (groups - 1) == 0 and members & (members - 1) == 0
+    tiles = [tile] + [lax.ppermute(tile, "grp", [(i, i ^ s) for i in range(groups)]) for s in range(1, groups)]
     far_b, part_d = pl.pallas_call(
         functools.partial(group_kernel, members=members),
         out_shape=(hbm((branches, rhs, rank), F32), hbm((rhs, rank), F32)),
@@ -557,26 +600,30 @@
         in_specs=[SMEM()] + [VMEM()] * (groups + 10),
         out_specs=VMEM(),
         scratch_shapes=[
-            pltpu.VMEM((table, rhs, rank2), BF16),
-            pltpu.VMEM((table, ROWS, rank2), BF16),
+            pltpu.VMEM((table, rhs + ROWS, rank2), BF16),
             pltpu.VMEM((groups, rhs, rank2), BF16),
             pltpu.VMEM((groups, ROWS, rank2), BF16),
             pltpu.VMEM((rank * branches, rank2), F32),
             pltpu.VMEM((branches, rhs, rank2), BF16),
-            pltpu.VMEM((2, rank, far_leaf.shape[0] * rank), BF16),
-            pltpu.VMEM((2, rank, far_leaf.shape[0] * rank), BF16),
-        ],
+        ]
+        + [
+            pltpu.VMEM((ROUND, rank, 2 * ROWS), BF16),
+            pltpu.VMEM((ROUND, ROWS, far_leaf.shape[0] * rank), BF16),
+            pltpu.VMEM((ROUND, rhs, far_leaf.shape[0] * rank), BF16),
+            pltpu.VMEM((ROUND, rank, far_leaf.shape[0] * rank), BF16),
+        ]
+        * 2,
         compiler_params=PARAMS,
         name="downward",
     )(
-        far_leaf,
+        far_turned,
         tile,
         *vmem(*tiles[1:]),
         far_b,
         part_d,
         down_device[:, :, 0],
         jnp.transpose(down_branch, (0, 2, 1)),
-        down,
+        *vmem(down),
         own,
         moments,
         *vmem(received),

time: 63.9 us -> 67.3 us (1.053)
  the two profiles are of different devices: /device:TPU:17 before, /device:TPU:0 now
where the time goes in v4:
time: 67.3 us; the launch traced here: 66.9 us
  Pallas kernels  30.4 us (45%)
  starting transfers between devices  22.7 us (34%)
  waiting for transfers between devices  13.7 us (20%)
    pallas_call x1, Pallas kernels, on_device(): pl.pallas_call(functools.partial(downward_kernel, groups=groups), out_sha...  11.5 us
    ppermute x1, waiting for transfers between devices, on_device(): lax.ppermute(shared, 'dev', [(i, i ^ members // 2) for i in range(members)])  11.1 us
    all_to_all x1, starting transfers between devices, on_device(): lax.all_to_all(listed, ('grp', 'dev'), split_axis=0, concat_axis=0, tiled...  7.33 us
    ppermute x3, starting transfers between devices, on_device(): lax.ppermute(tile, 'grp', [(i, i ^ s) for i in range(groups)])  7.02 us
    pallas_call x1, Pallas kernels, on_device(): pl.pallas_call(near_kernel, out_shape=pltpu.VMEM((rhs, total), F32), in_s...  5.19 us
    pallas_call x1, Pallas kernels, on_device(): pl.pallas_call(upward_kernel, out_shape=hbm(((branches // 2 + 1) * (rhs +...  3.77 us
    pallas_call x1, Pallas kernels, on_device(): pl.pallas_call(listed_kernel, out_shape=(pltpu.VMEM((leaves, rhs, rank2),...  3.73 us
    ppermute x3, starting transfers between devices, on_device(): lax.ppermute(both, 'dev', [(i, i ^ s) for i in range(members)])  3.55 us
  transfers between devices with their start and end apart: 10, of which 2 were waited for; matrix products, arithmetic and copies ran while one was open for 0% of the time, Pallas kernels for 23%

profile of v4, /device:TPU:0, one launch (start us, length us, event | category | flops | bytes accessed | tf_op | source)
XLA Modules:
  0.0 66.9 jit_solution(18031704197036837699)
XLA Ops:
  0.0 3.7 %listed.1 = (bf16[64,32,128]{2,1,0:T(8,128)(2,1)S(1)}, bf16[64,8,128]{2,1,0:T(8,128)(2,1)}, bf16[32,80,128]{2,1,0:T(8,128)(2,1)}, bf16[80,128]{1,0:T(8,128)(2,1)S(1)}, bf16[80,128]{1,0:T(8,128)(2,1)S(1)}) custom-call(s32[4,32]{1,0:T(4,128)} %send_ref.1, bf16[32,4096]{1,0:T(8,128)(2,1)} %charges_ref.3, bf16[3,4096]{1,0:T(4,128)(2,1)} %points_ref.3, ...), custom_call_target="tpu_custom_call" | custom-call | tf_op jit(solution)/shard_map/listed/pallas_call | solution.py:498
  3.7 7.3 %all-to-all-start = ((bf16[32,80,128]{2,1,0:T(8,128)(2,1)}), bf16[32,80,128]{2,1,0:T(8,128)(2,1)S(1)}, u32[]{:S(2)}, u32[]{:S(2)}) async-start(bf16[32,80,128]{2,1,0:T(8,128)(2,1)} %get-tuple-element.26), calls=%async_computation | async-start | bytes 1310720 | tf_op jit(solution)/shard_map/all_to_all | solution.py:514
  11.1 3.8 %upward.1._ = bf16[200,128]{1,0:T(8,128)(2,1)} custom-call(bf16[64,32,128]{2,1,0:T(8,128)(2,1)S(1)} %get-tuple-element.16.moment_ref.refs_11_, bf16[64,64,64]{2,1,0:T(8,128)(2,1)} %up_leaf_ref.1, bf16[64,8,64]{2,1,0:T(8,128)(2,1)} %bitcast.8, bf16[64,64]{1,0:T(8,128)(2,1)} %bitcast.10, bf16[3,8,64]{2,1,0:T(8,128)(2,1)} %bitcast.12, bf16[3,64]{1,0:T(4,128)(2,1)} %bitcast.14), custom_call_target="tpu_custom_call" | custom-call | tf_op jit(solution)/shard_map/upward/pallas_call | solution.py:520
  14.8 2.7 %collective-permute-start.2 = (bf16[200,128]{1,0:T(8,128)(2,1)}, bf16[200,128]{1,0:T(8,128)(2,1)S(1)}, u32[]{:S(2)}, u32[]{:S(2)}) collective-permute-start(bf16[200,128]{1,0:T(8,128)(2,1)} %upward.1._), channel_id=1, source_target_pairs={{0,4},{1,5},{2,6},{3,7},{4,0},{5,1},{6,2},{7,3},{8,12},{9,13},{10,... | collective-permute-start | bytes 153608 | tf_op jit(solution)/shard_map/ppermute | solution.py:536
  17.5 2.5 %turn.1 = (bf16[2048,128]{1,0:T(8,128)(2,1)S(1)}, s32[64,16]{1,0:T(8,128)}) custom-call(bf16[64,64,64]{2,1,0:T(8,128)(2,1)} %down_leaf_ref.1, s32[16,64]{1,0:T(8,128)} %far_ref.1, bf16[200,128]{1,0:T(8,128)(2,1)} %upward.1._), custom_call_target="tpu_custom_call" | custom-call | tf_op jit(solution)/shard_map/turn/pallas_call | solution.py:537
  20.0 11.1 %collective-permute-done.2 = bf16[200,128]{1,0:T(8,128)(2,1)S(1)} collective-permute-done((bf16[200,128]{1,0:T(8,128)(2,1)}, bf16[200,128]{1,0:T(8,128)(2,1)S(1)}, u32[]{:S(2)}, u32[]{:S(2)}) %collective-permute-start.2) | collective-permute-done | bytes 51232 | tf_op jit(solution)/shard_map/ppermute | solution.py:536
  31.1 0.1 collective-permute-start.5
  31.1 2.9 %collective-permute-start.4 = (bf16[400,128]{1,0:T(8,128)(2,1)S(1)}, bf16[400,128]{1,0:T(8,128)(2,1)S(1)}, u32[]{:S(2)}, u32[]{:S(2)}) collective-permute-start(bf16[400,128]{1,0:T(8,128)(2,1)S(1)} %pad_maximum_fusion._.refs_2_), channel_id=1, source_target_pairs={{0,2},{1,3},{2,0},{3,1},{4,6},{5,7},{6,4},{7,5},{8,10},{9,11},{10,... | collective-permute-start | bytes 307208 | tf_op jit(solution)/shard_map/ppermute | solution.py:549
  34.1 0.5 collective-permute-start.3
  34.6 1.5 %collective-permute-start = (bf16[80,128]{1,0:T(8,128)(2,1)S(1)}, bf16[80,128]{1,0:T(8,128)(2,1)S(1)}, u32[]{:S(2)}, u32[]{:S(2)}) collective-permute-start(bf16[80,128]{1,0:T(8,128)(2,1)S(1)} %get-tuple-element.18), channel_id=1, source_target_pairs={{0,1},{1,0},{2,3},{3,2},{4,5},{5,4},{6,7},{7,6},{8,9},{9,8},{10,11... | collective-permute-start | bytes 61448 | tf_op jit(solution)/shard_map/ppermute | solution.py:518
  36.1 0.7 collective-permute-start.1
  36.8 2.6 %collective-permute-done.inner_ref = bf16[80,128]{1,0:T(8,128)(2,1)S(1)} collective-permute-done((bf16[80,128]{1,0:T(8,128)(2,1)S(1)}, bf16[80,128]{1,0:T(8,128)(2,1)S(1)}, u32[]{:S(2)}, u32[]{:S(2)}) %collective-permute-start) | collective-permute-done | bytes 20512 | tf_op jit(solution)/shard_map/ppermute | solution.py:518
  39.3 0.0 collective-permute-done.1.outer_ref
  39.3 5.2 %near.1.refs_0_.refs_14_ = f32[32,4096]{1,0:T(8,128)S(1)} custom-call(s32[16,64]{1,0:T(8,128)} %near_ref.1, bf16[32,4096]{1,0:T(8,128)(2,1)} %charges_ref.3, bf16[3,4096]{1,0:T(4,128)(2,1)} %points_ref.3, bf16[80,128]{1,0:T(8,128)(2,1)S(1)} %collective-permute-done.inner_ref, bf16[80,128]{1,0:T(8,128)(2,1)S(1)} %collective-permute-done.1.outer_ref, ...), custom_call_target="tpu_custom_call" | custom-call | tf_op jit(solution)/shard_map/near/pallas_call | solution.py:553
  44.5 0.0 collective-permute-done.5.refs_5_
  44.6 0.0 collective-permute-done.4.refs_4_
  44.6 1.4 %top.1.refs_1_ = bf16[40,128]{1,0:T(8,128)(2,1)} custom-call(f32[32,4096]{1,0:T(8,128)S(1)} %near.1.refs_0_.refs_14_, bf16[3,64]{1,0:T(4,128)(2,1)} %bitcast.15, bf16[400,128]{1,0:T(8,128)(2,1)S(1)} %pad_maximum_fusion._.refs_2_, bf16[400,128]{1,0:T(8,128)(2,1)S(1)} %collective-permute-done.3.refs_3_, bf16[400,128]{1,0:T(8,128)(2,1)S(1)} %collective-permute-done.4.refs_4_, ...), custom_call_target="tpu_custom_call" | custom-call | tf_op jit(solution)/shard_map/top/pallas_call | solution.py:571
  46.0 3.7 %collective-permute-start.8 = (bf16[40,128]{1,0:T(8,128)(2,1)}, bf16[40,128]{1,0:T(8,128)(2,1)S(1)}, u32[]{:S(2)}, u32[]{:S(2)}) collective-permute-start(bf16[40,128]{1,0:T(8,128)(2,1)} %top.1.refs_1_), channel_id=1, source_target_pairs={{0,24},{8,16},{16,8},{24,0},{1,25},{9,17},{17,9},{25,1},{2,26},{10... | collective-permute-start | bytes 30728 | tf_op jit(solution)/shard_map/ppermute | solution.py:580
  49.7 3.2 %collective-permute-start.7 = (bf16[40,128]{1,0:T(8,128)(2,1)}, bf16[40,128]{1,0:T(8,128)(2,1)S(1)}, u32[]{:S(2)}, u32[]{:S(2)}) collective-permute-start(bf16[40,128]{1,0:T(8,128)(2,1)} %top.1.refs_1_), channel_id=1, source_target_pairs={{0,16},{8,24},{16,0},{24,8},{1,17},{9,25},{17,1},{25,9},{2,18},{10... | collective-permute-start | bytes 30728 | tf_op jit(solution)/shard_map/ppermute | solution.py:580
  52.9 0.1 collective-permute-start.6
  53.0 2.4 %group.1 = (f32[8,32,64]{2,1,0:T(8,128)}, f32[32,64]{1,0:T(8,128)}) custom-call(s32[8,16]{1,0:T(8,128)} %bitcast.13, bf16[40,128]{1,0:T(8,128)(2,1)} %top.1.refs_1_, bf16[400,128]{1,0:T(8,128)(2,1)S(1)} %pad_maximum_fusion._.refs_2_, bf16[400,128]{1,0:T(8,128)(2,1)S(1)} %collective-permute-done.3.refs_3_, ...), custom_call_target="tpu_custom_call" | custom-call | tf_op jit(solution)/shard_map/group/pallas_call | solution.py:581
  55.3 0.0 collective-permute-done.8.refs_4_
  55.3 0.0 collective-permute-done.7.refs_3_
  55.4 11.5 %downward.1 = f32[32,4096]{1,0:T(8,128)} custom-call(s32[64,16]{1,0:T(8,128)} %get-tuple-element.17.refs_0_, bf16[40,128]{1,0:T(8,128)(2,1)} %top.1.refs_1_, bf16[40,128]{1,0:T(8,128)(2,1)S(1)} %collective-permute-done.6.refs_2_, bf16[40,128]{1,0:T(8,128)(2,1)S(1)} %collective-permute-done.7.refs_3_, bf16[40,128]{1,0:T(8,128)(2,1)S(1)} %collective-permute-done.8.refs_4_, ...), custom_call_target="tpu_custom_call" | custom-call | tf_op jit(solution)/shard_map/downward/pallas_call | solution.py:597
  (6 shorter events, 0.0 us)
Async XLA Ops:
  3.7 51.6 %all-to-all-start = ((bf16[32,80,128]{2,1,0:T(8,128)(2,1)}), bf16[32,80,128]{2,1,0:T(8,128)(2,1)S(1)}, u32[]{:S(2)}, u32[]{:S(2)}) async-start(bf16[32,80,128]{2,1,0:T(8,128)(2,1)} %get-tuple-element.26), calls=%async_computation | async-start | bytes 1310720 | tf_op jit(solution)/shard_map/all_to_all | solution.py:514
  14.8 16.2 %copy-start = (bf16[200,128]{1,0:T(8,128)(2,1)S(1)}, bf16[200,128]{1,0:T(8,128)(2,1)}, u32[]{:S(2)}) copy-start(bf16[200,128]{1,0:T(8,128)(2,1)} %upward.1._) | copy-start | bytes 153604
  14.8 16.2 %collective-permute-start.2 = (bf16[200,128]{1,0:T(8,128)(2,1)}, bf16[200,128]{1,0:T(8,128)(2,1)S(1)}, u32[]{:S(2)}, u32[]{:S(2)}) collective-permute-start(bf16[200,128]{1,0:T(8,128)(2,1)} %upward.1._), channel_id=1, source_target_pairs={{0,4},{1,5},{2,6},{3,7},{4,0},{5,1},{6,2},{7,3},{8,12},{9,13},{10,... | collective-permute-start | bytes 153608 | tf_op jit(solution)/shard_map/ppermute | solution.py:536
  31.1 13.5 %collective-permute-start.5 = (bf16[400,128]{1,0:T(8,128)(2,1)S(1)}, bf16[400,128]{1,0:T(8,128)(2,1)S(1)}, u32[]{:S(2)}, u32[]{:S(2)}) collective-permute-start(bf16[400,128]{1,0:T(8,128)(2,1)S(1)} %pad_maximum_fusion._.refs_2_), channel_id=1, source_target_pairs={{0,3},{1,2},{2,1},{3,0},{4,7},{5,6},{6,5},{7,4},{8,11},{9,10},{10,... | collective-permute-start | bytes 307208 | tf_op jit(solution)/shard_map/ppermute | solution.py:549
  31.1 13.4 %collective-permute-start.4 = (bf16[400,128]{1,0:T(8,128)(2,1)S(1)}, bf16[400,128]{1,0:T(8,128)(2,1)S(1)}, u32[]{:S(2)}, u32[]{:S(2)}) collective-permute-start(bf16[400,128]{1,0:T(8,128)(2,1)S(1)} %pad_maximum_fusion._.refs_2_), channel_id=1, source_target_pairs={{0,2},{1,3},{2,0},{3,1},{4,6},{5,7},{6,4},{7,5},{8,10},{9,11},{10,... | collective-permute-start | bytes 307208 | tf_op jit(solution)/shard_map/ppermute | solution.py:549
  34.1 10.5 %collective-permute-start.3 = (bf16[400,128]{1,0:T(8,128)(2,1)S(1)}, bf16[400,128]{1,0:T(8,128)(2,1)S(1)}, u32[]{:S(2)}, u32[]{:S(2)}) collective-permute-start(bf16[400,128]{1,0:T(8,128)(2,1)S(1)} %pad_maximum_fusion._.refs_2_), channel_id=1, source_target_pairs={{0,1},{1,0},{2,3},{3,2},{4,5},{5,4},{6,7},{7,6},{8,9},{9,8},{10,11... | collective-permute-start | bytes 307208 | tf_op jit(solution)/shard_map/ppermute | solution.py:549
  34.6 4.7 %collective-permute-start = (bf16[80,128]{1,0:T(8,128)(2,1)S(1)}, bf16[80,128]{1,0:T(8,128)(2,1)S(1)}, u32[]{:S(2)}, u32[]{:S(2)}) collective-permute-start(bf16[80,128]{1,0:T(8,128)(2,1)S(1)} %get-tuple-element.18), channel_id=1, source_target_pairs={{0,1},{1,0},{2,3},{3,2},{4,5},{5,4},{6,7},{7,6},{8,9},{9,8},{10,11... | collective-permute-start | bytes 61448 | tf_op jit(solution)/shard_map/ppermute | solution.py:518
  36.1 3.3 %collective-permute-start.1 = (bf16[80,128]{1,0:T(8,128)(2,1)S(1)}, bf16[80,128]{1,0:T(8,128)(2,1)S(1)}, u32[]{:S(2)}, u32[]{:S(2)}) collective-permute-start(bf16[80,128]{1,0:T(8,128)(2,1)S(1)} %get-tuple-element.19), channel_id=1, source_target_pairs={{1,2},{2,1},{3,4},{4,3},{5,6},{6,5},{7,8},{8,7},{9,10},{10,9},{11,... | collective-permute-start | bytes 61448 | tf_op jit(solution)/shard_map/ppermute | solution.py:517
  46.0 9.4 %collective-permute-start.8 = (bf16[40,128]{1,0:T(8,128)(2,1)}, bf16[40,128]{1,0:T(8,128)(2,1)S(1)}, u32[]{:S(2)}, u32[]{:S(2)}) collective-permute-start(bf16[40,128]{1,0:T(8,128)(2,1)} %top.1.refs_1_), channel_id=1, source_target_pairs={{0,24},{8,16},{16,8},{24,0},{1,25},{9,17},{17,9},{25,1},{2,26},{10... | collective-permute-start | bytes 30728 | tf_op jit(solution)/shard_map/ppermute | solution.py:580
  49.7 5.7 %collective-permute-start.7 = (bf16[40,128]{1,0:T(8,128)(2,1)}, bf16[40,128]{1,0:T(8,128)(2,1)S(1)}, u32[]{:S(2)}, u32[]{:S(2)}) collective-permute-start(bf16[40,128]{1,0:T(8,128)(2,1)} %top.1.refs_1_), channel_id=1, source_target_pairs={{0,16},{8,24},{16,0},{24,8},{1,17},{9,25},{17,1},{25,9},{2,18},{10... | collective-permute-start | bytes 30728 | tf_op jit(solution)/shard_map/ppermute | solution.py:580
  52.9 2.5 %collective-permute-start.6 = (bf16[40,128]{1,0:T(8,128)(2,1)}, bf16[40,128]{1,0:T(8,128)(2,1)S(1)}, u32[]{:S(2)}, u32[]{:S(2)}) collective-permute-start(bf16[40,128]{1,0:T(8,128)(2,1)} %top.1.refs_1_), channel_id=1, source_target_pairs={{0,8},{8,0},{16,24},{24,16},{1,9},{9,1},{17,25},{25,17},{2,10},{10... | collective-permute-start | bytes 30728 | tf_op jit(solution)/shard_map/ppermute | solution.py:580

commit v5 on v4

--- a/solution.py
+++ b/solution.py
@@ -11,7 +11,7 @@
 REACH = 4
 FAN = 8
 ROUND = 8
-PAIRS = 4
+PAIRS = 2
 
 INV_FOUR_PI = 1.0 / (4.0 * math.pi)
 SOFTEN = 0.25
@@ -31,6 +31,12 @@
 
 def dot_0(a, b):
     return lax.dot_general(a, b, (((0,), (0,)), ((), ())), preferred_element_type=F32)
+
+
+def fetch(source, target, sem):
+    copy = pltpu.make_async_copy(source, target, sem)
+    copy.start()
+    return copy
 
 
 def low_half(shape):
@@ -117,11 +123,14 @@
     return dot_t(gathered(slots, moment_ref), couplings(target, slots, source_ref, tail))
 
 
-def listed_kernel(
-    send_ref, charges_ref, points_ref, basis_ref, proxy_ref, moment_ref, own_ref, out_ref, inner_ref, outer_ref, tile_ref
+def upward_kernel(
+    send_ref, charges_ref, points_ref, basis_ref, proxy_ref, up_leaf_hbm, up_branch_ref, up_device_ref, pbranch_ref,
+    pdevice_ref, moment_ref, own_ref, out_ref, inner_ref, outer_ref, shared_ref, tile_ref, up_leaf_ref, scratch_ref,
+    branch_ref, sem,
 ):
     slots, devices = send_ref.shape
     leaves, rhs, rank2 = moment_ref.shape
+    transfers = fetch(up_leaf_hbm, up_leaf_ref, sem)
     low = low_half((rhs, rank2))
     put_rows(tile_ref, source_rows(*[twice(jnp.transpose(proxy_ref[c].astype(F32))) for c in range(3)]), leaves)
     own_ref[...] = tile_ref[...].astype(BF16).reshape(own_ref.shape)
@@ -162,6 +171,10 @@
             points = points_ref[:, columns].astype(F32)
             rows = jnp.concatenate([points, jnp.zeros((ROWS - 3, rank2), F32)], axis=0)
             ref[base + rhs : base + rhs + ROWS, :] = rows.astype(BF16)
+    transfers.wait()
+    raise_moments(
+        moment_ref, up_leaf_ref, up_branch_ref, up_device_ref, pbranch_ref, pdevice_ref, shared_ref, scratch_ref, branch_ref
+    )
 
 
 def relayout(x_ref, scratch_ref):
@@ -185,7 +198,7 @@
     return jnp.concatenate([jnp.where(low, block, zero), jnp.where(low, zero, block)], axis=0)
 
 
-def upward_kernel(
+def raise_moments(
     moment_ref, up_leaf_ref, up_branch_ref, up_device_ref, pbranch_ref, pdevice_ref, out_ref, scratch_ref, branch_ref
 ):
     leaves, rhs, rank2 = moment_ref.shape
@@ -232,37 +245,15 @@
     down_ref[...] = scratch_ref[...].astype(BF16)
 
 
-def near_kernel(
-    near_ref, charges_ref, points_ref, inner_ref, outer_ref, _, out_ref,
-    wide_ref, source_ref, target_ref, weight_ref, kern_a_ref, kern_b_ref,
-):
-    rhs, total = charges_ref.shape
-    _, leaves = near_ref.shape
-    size = total // leaves
-    halo = REACH * size
+def point_rows(points):
+    return stack_rows(source_rows(*[points[c : c + 1, :] for c in range(3)]))
+
+
+def near_weights(near_ref, size, weight_ref):
+    near = near_ref[...]
+    leaves = near.shape[1]
+    reach = weight_ref.shape[2]
     span = 2 * REACH + 1
-    reach = (span + 1) * size
-    odd = lax.rem(lax.axis_index("dev"), 2) == 1
-    wide_ref[:, halo : halo + total] = charges_ref[...]
-    lanes = 2 * size
-    sides = [[], []]
-    for n in range(halo // lanes):
-        rows = slice(n * (rhs + ROWS), (n + 1) * (rhs + ROWS))
-        inner, outer = inner_ref[rows, :], outer_ref[rows, :]
-        for side, block in enumerate((jnp.where(odd, inner, outer), jnp.where(odd, outer, inner))):
-            start = side * (halo + total) + n * lanes
-            wide_ref[:, start : start + lanes] = block[:rhs, :]
-            sides[side].append(block[rhs:, :].astype(F32))
-    left, right = (jnp.concatenate(side, axis=1) for side in sides)
-    coords = [
-        jnp.concatenate([left[c : c + 1, :], points_ref[c : c + 1, :].astype(F32), right[c : c + 1, :]], axis=1)
-        for c in range(3)
-    ]
-    rows = stack_rows(source_rows(*coords))
-    source_ref[...] = jnp.concatenate([rows.astype(BF16), source_tail(total + 2 * halo)], axis=0)
-    target_ref[...] = target_of(rows[:, halo : halo + total])
-
-    near = near_ref[...]
     counts = [jnp.sum((near == o - REACH).astype(F32), axis=0, keepdims=True) for o in range(span)]
     counts = jnp.concatenate(counts + [jnp.zeros((2 * ROWS - span, leaves), F32)], axis=0).astype(BF16)
     offset = lax.broadcasted_iota(jnp.int32, (2 * ROWS, reach), 0)
@@ -270,23 +261,51 @@
     for h in range(2):
         weight_ref[h] = dot_0(counts, (block == offset + h).astype(BF16))
 
+
+def near_couplings(target, source, weights, kern_ref):
+    kern = kern_of(dot_0(target, source))
+    size, reach = kern.shape[0] // 2, kern.shape[1]
+    for h in range(2):
+        weight = jnp.broadcast_to(weights[h], (2 * ROWS, reach)).astype(BF16)
+        for s in range(h * size, (h + 1) * size, 2 * ROWS):
+            kern_ref[s : s + 2 * ROWS, :] = kern[s : s + 2 * ROWS, :] * weight
+
+
+def near_kernel(
+    near_ref, charges_ref, points_ref, _, out_ref, source_ref, target_ref, weight_ref, kern_a_ref, kern_b_ref
+):
+    rhs, total = charges_ref.shape
+    size = total // near_ref.shape[1]
+    halo = REACH * size
+    lanes = 2 * size
+    reach = weight_ref.shape[2]
+    rows = point_rows(points_ref[...].astype(F32))
+    source_ref[...] = jnp.concatenate([rows.astype(BF16), source_tail(total)], axis=0)
+    target_ref[...] = target_of(rows)
+    near_weights(near_ref, size, weight_ref)
+    out_ref[:, :halo] = jnp.zeros((rhs, halo), F32)
+    out_ref[:, total - halo :] = jnp.zeros((rhs, halo), F32)
+    width = kern_a_ref.shape[0]
+    first = halo // lanes
+    rounds = (total - 2 * halo) // lanes // width
+
     def evaluate(i, kern_ref):
         for n in range(width):
-            j = i * width + n
-            start = pl.multiple_of(j * 2 * size, 2 * size)
-            kern = kern_of(dot_0(target_ref[:, pl.ds(start, 2 * size)], source_ref[:, pl.ds(start, reach)]))
-            for h in range(2):
-                weight = jnp.broadcast_to(weight_ref[h, pl.ds(2 * j + h, 1), :], (2 * ROWS, reach)).astype(BF16)
-                for s in range(h * size, (h + 1) * size, 2 * ROWS):
-                    kern_ref[n, s : s + 2 * ROWS, :] = kern[s : s + 2 * ROWS, :] * weight
+            j = first + i * width + n
+            start = pl.multiple_of(j * lanes, lanes)
+            near_couplings(
+                target_ref[:, pl.ds(start, lanes)],
+                source_ref[:, pl.ds(pl.multiple_of(start - halo, lanes), reach)],
+                [weight_ref[h, pl.ds(2 * j + h, 1), :] for h in range(2)],
+                kern_ref.at[n],
+            )
 
     def apply(i, kern_ref):
         for n in range(width):
-            start = pl.multiple_of((i * width + n) * 2 * size, 2 * size)
-            out_ref[:, pl.ds(start, 2 * size)] = dot_t(wide_ref[:, pl.ds(start, reach)], kern_ref[n])
-
-    width = kern_a_ref.shape[0]
-    rounds = leaves // 2 // width
+            start = pl.multiple_of((first + i * width + n) * lanes, lanes)
+            columns = pl.ds(pl.multiple_of(start - halo, lanes), reach)
+            out_ref[:, pl.ds(start, lanes)] = dot_t(charges_ref[:, columns], kern_ref[n])
+
     evaluate(0, kern_a_ref)
 
     def step(t, carry):
@@ -297,6 +316,39 @@
         return carry
 
     lax.fori_loop(0, rounds // 2, step, 0)
+
+
+def edge_pairs(near_ref, ends_ref, end_points_ref, inner_ref, outer_ref, out_ref, weight_ref, kern_ref):
+    rhs = ends_ref.shape[1]
+    leaves = near_ref.shape[1]
+    halo = out_ref.shape[1] // 2
+    lanes = inner_ref.shape[1]
+    size = lanes // 2
+    count = halo // lanes
+    reach = weight_ref.shape[2]
+    odd = lax.rem(lax.axis_index("dev"), 2) == 1
+    near_weights(near_ref, size, weight_ref)
+    inner, outer = inner_ref[...], outer_ref[...]
+    height = inner.shape[0] // count
+    for side, block in enumerate((jnp.where(odd, inner, outer), jnp.where(odd, outer, inner))):
+        beyond = jnp.concatenate([block[n * height : (n + 1) * height, :] for n in range(count)], axis=1)
+        parts = [(beyond[:rhs, :], beyond[rhs : rhs + 3, :].astype(F32)), (ends_ref[side], end_points_ref[side].astype(F32))]
+        parts = parts if side == 0 else parts[::-1]
+        wide = jnp.concatenate([p[0] for p in parts], axis=1)
+        rows = point_rows(jnp.concatenate([p[1] for p in parts], axis=1))
+        source = jnp.concatenate([rows.astype(BF16), source_tail(rows.shape[1])], axis=0)
+        target = target_of(rows[:, halo : 2 * halo])
+        for j in range(count):
+            leaf = 2 * j + side * (leaves - 2 * count)
+            place = side * count + j
+            near_couplings(
+                target[:, j * lanes : (j + 1) * lanes],
+                source[:, j * lanes : j * lanes + reach],
+                [weight_ref[h, leaf + h : leaf + h + 1, :] for h in range(2)],
+                kern_ref.at[place],
+            )
+            columns = slice(place * lanes, (place + 1) * lanes)
+            out_ref[:, columns] = dot_t(wide[:, j * lanes : j * lanes + reach], kern_ref[place])
 
 
 def put_pair(ref, slot, tile, row=0):
@@ -327,11 +379,19 @@
 
 
 def group_kernel(*refs, members):
-    far_ref, _ = refs[:2]
+    far_ref, near_ref, charges_hbm, points_hbm, inner_ref, outer_ref, _ = refs[:7]
     count = members // 2
-    parts = refs[2 : 2 + count]
-    fb_ref, ld_ref = refs[2 + count : 4 + count]
-    moment_ref, source_ref, dev_m_ref, dev_source_ref = refs[4 + count :]
+    parts = refs[7 : 7 + count]
+    fb_ref, ld_ref, edge_ref = refs[7 + count : 10 + count]
+    (
+        moment_ref, source_ref, dev_m_ref, dev_source_ref, ends_ref, end_points_ref, weight_ref, kern_ref, sems,
+    ) = refs[10 + count :]
+    total, width = charges_hbm.shape[1], ends_ref.shape[2]
+    copies = []
+    for side in range(2):
+        columns = slice(side * (total - width), side * (total - width) + width)
+        copies.append(fetch(charges_hbm.at[:, columns], ends_ref.at[side], sems.at[2 * side]))
+        copies.append(fetch(points_hbm.at[:, columns], end_points_ref.at[side], sems.at[2 * side + 1]))
     branches, entries = far_ref.shape
     rhs, rank2 = moment_ref.shape[1:]
     rank = rank2 // 2
@@ -354,13 +414,16 @@
         fb_ref[c] = interact(target, [far_ref[c, e] for e in range(entries)], source_ref, tail, moment_ref)
     target = target_of(dev_source_ref[me][:, :rank])
     ld_ref[...] = interact(target, list(range(members)), dev_source_ref, tail, dev_m_ref)
+    for copy in copies:
+        copy.wait()
+    edge_pairs(near_ref, ends_ref, end_points_ref, inner_ref, outer_ref, edge_ref, weight_ref, kern_ref)
 
 
 def downward_kernel(*refs, groups):
     far_ref = refs[0]
     tiles = refs[1 : 1 + groups]
     (
-        fb_ref, ld_ref, down_device_ref, down_branch_ref, down_ref, own_ref, own_m_ref, recv_ref, basis_ref, near_ref,
+        fb_ref, ld_ref, down_device_ref, down_branch_ref, down_ref, own_ref, own_m_ref, recv_ref, basis_ref, near_ref, edge_ref,
         out_ref, table_ref, grp_m_ref, grp_source_ref, branch_ref, parent_ref, *buffers,
     ) = refs[1 + groups :]
     leaves, entries = far_ref.shape
@@ -398,7 +461,7 @@
             put_pair(table_ref, slot, recv_ref[p, base + q * ROWS : base + (q + 1) * ROWS, :], rhs)
         return carry
 
-    lax.fori_loop(0, devices, unpack, 0, unroll=4)
+    lax.fori_loop(0, devices, unpack, 0, unroll=min(devices, 32))
     low_d = low_half((half, rank2))
 
     width = buffers[0].shape[0]
@@ -461,6 +524,9 @@
     sums = lax.fori_loop(0, rounds // 2, step, (jnp.zeros((rhs, rank), BF16),) * width)
     finish(rounds - 2, sums)
     finish(rounds - 1, apply(rounds - 1, odd[2], odd[3]))
+    total, halo = out_ref.shape[1], edge_ref.shape[1] // 2
+    out_ref[:, :halo] += edge_ref[:, :halo]
+    out_ref[:, total - halo :] += edge_ref[:, halo:]
 
 
 VMEM = functools.partial(pl.BlockSpec, memory_space=pltpu.VMEM)
@@ -495,44 +561,42 @@
     halo = REACH * size
     assert rank == size and slots % 2 == 0 and branches % 2 == 0 and members % 2 == 0
 
-    moments, own, listed, inner, outer = pl.pallas_call(
-        listed_kernel,
+    moments, own, listed, inner, outer, shared = pl.pallas_call(
+        upward_kernel,
         out_shape=(
             pltpu.VMEM((leaves, rhs, rank2), BF16),
             hbm((leaves, ROWS, rank2), BF16),
             hbm((devices, slots // 2 * (rhs + ROWS), rank2), BF16),
             pltpu.VMEM((halo // rank2 * (rhs + ROWS), rank2), BF16),
             pltpu.VMEM((halo // rank2 * (rhs + ROWS), rank2), BF16),
+            hbm(((branches // 2 + 1) * (rhs + ROWS), rank2), BF16),
         ),
-        in_specs=[SMEM()] + [VMEM()] * 4,
-        out_specs=(VMEM(),) * 5,
-        scratch_shapes=[pltpu.VMEM((leaves * ROWS, rank2), F32)],
-        compiler_params=PARAMS,
-        name="listed",
-    )(send_leaf, charges, points, basis, proxy_leaf)
-    (moments,) = vmem(moments)
-    received = lax.all_to_all(listed, ("grp", "dev"), split_axis=0, concat_axis=0, tiled=True)
-
-    swaps = [(i, i + 1 if i % 2 else i - 1) for i in range(1, devices - 1)]
-    outer = lax.ppermute(outer, ("grp", "dev"), swaps)
-    inner = lax.ppermute(inner, "dev", [(i, i ^ 1) for i in range(members)])
-
-    shared = pl.pallas_call(
-        upward_kernel,
-        out_shape=hbm(((branches // 2 + 1) * (rhs + ROWS), rank2), BF16),
-        in_specs=[VMEM()] * 6,
-        out_specs=VMEM(),
-        scratch_shapes=[pltpu.VMEM((leaves * half, rank2), F32), pltpu.VMEM((rank * branches, rank2), F32)],
+        in_specs=[SMEM()] + [VMEM()] * 4 + [ANY()] + [VMEM()] * 4,
+        out_specs=(VMEM(),) * 6,
+        scratch_shapes=[
+            pltpu.VMEM((leaves * ROWS, rank2), F32),
+            pltpu.VMEM(up_leaf.shape, BF16),
+            pltpu.VMEM((leaves * half, rank2), F32),
+            pltpu.VMEM((rank * branches, rank2), F32),
+            pltpu.SemaphoreType.DMA(()),
+        ],
         compiler_params=PARAMS,
         name="upward",
     )(
-        moments,
+        send_leaf,
+        charges,
+        points,
+        basis,
+        proxy_leaf,
         up_leaf,
         jnp.transpose(up_branch, (0, 2, 1)),
         up_device[:, :, 0],
         jnp.transpose(proxy_branch, (0, 2, 1)),
         proxy_device[:, :, 0],
     )
+    (moments,) = vmem(moments)
+    received = lax.all_to_all(listed, ("grp", "dev"), split_axis=0, concat_axis=0, tiled=True)
+
     partner = lax.ppermute(shared, "dev", [(i, i ^ members // 2) for i in range(members)])
     down, far_turned = pl.pallas_call(
         turn_kernel,
@@ -545,19 +609,18 @@
     )(down_leaf, far_leaf, shared)
     partner, down = lax.optimization_barrier((partner, down))
     both = jnp.concatenate([shared, partner], axis=0)
-    parts = [both] + [
-        lax.ppermute(both, "dev", [(i, i ^ s) for i in range(members)]) for s in range(1, members // 2)
-    ]
+    parts = [both]
+    for s in range(1, members // 2):
+        parts.append(lax.ppermute(both, "dev", [(i, i ^ s) for i in range(members)]))
 
     reach = (2 * REACH + 2) * size
     near = pl.pallas_call(
         near_kernel,
         out_shape=pltpu.VMEM((rhs, total), F32),
-        in_specs=[VMEM()] * 6,
+        in_specs=[VMEM()] * 4,
         out_specs=VMEM(),
         scratch_shapes=[
-            pltpu.VMEM((rhs, total + 2 * halo), BF16),
-            pltpu.VMEM((2 * ROWS, total + 2 * halo), BF16),
+            pltpu.VMEM((2 * ROWS, total), BF16),
             pltpu.VMEM((2 * ROWS, total), BF16),
             pltpu.VMEM((2, leaves, reach), F32),
             pltpu.VMEM((PAIRS, 2 * size, reach), BF16),
@@ -565,7 +628,12 @@
         ],
         compiler_params=PARAMS,
         name="near",
-    )(near_leaf, charges, points, *vmem(inner, outer, both))
+    )(near_leaf, charges, points, *vmem(both))
+
+    swaps = [(i, i + 1 if i % 2 else i - 1) for i in range(1, devices - 1)]
+    inner, outer, near = lax.optimization_barrier((inner, outer, near))
+    outer = lax.ppermute(outer, ("grp", "dev"), swaps)
+    inner = lax.ppermute(inner, "dev", [(i, i ^ 1) for i in range(members)])
 
     parts = vmem(*parts)
     tile = pl.pallas_call(
@@ -578,26 +646,31 @@
     )(*vmem(near), proxy_group[:, :, 0], *parts)
     assert groups & (groups - 1) == 0 and members & (members - 1) == 0
     tiles = [tile] + [lax.ppermute(tile, "grp", [(i, i ^ s) for i in range(groups)]) for s in range(1, groups)]
-    far_b, part_d = pl.pallas_call(
+    far_b, part_d, edge = pl.pallas_call(
         functools.partial(group_kernel, members=members),
-        out_shape=(hbm((branches, rhs, rank), F32), hbm((rhs, rank), F32)),
-        in_specs=[SMEM(), ANY()] + [VMEM()] * len(parts),
-        out_specs=(VMEM(), VMEM()),
+        out_shape=(hbm((branches, rhs, rank), F32), hbm((rhs, rank), F32), pltpu.VMEM((rhs, 2 * halo), F32)),
+        in_specs=[SMEM(), VMEM(), ANY(), ANY(), VMEM(), VMEM(), ANY()] + [VMEM()] * len(parts),
+        out_specs=(VMEM(),) * 3,
         scratch_shapes=[
             pltpu.VMEM((members * branches, rhs, rank2), BF16),
             pltpu.VMEM((members * branches, ROWS, rank2), BF16),
             pltpu.VMEM((members, rhs, rank2), BF16),
             pltpu.VMEM((members, ROWS, rank2), BF16),
+            pltpu.VMEM((2, rhs, 2 * halo), BF16),
+            pltpu.VMEM((2, 3, 2 * halo), BF16),
+            pltpu.VMEM((2, leaves, reach), F32),
+            pltpu.VMEM((REACH, 2 * size, reach), BF16),
+            pltpu.SemaphoreType.DMA((4,)),
         ],
         compiler_params=PARAMS,
         name="group",
-    )(jnp.transpose(far_branch), tile, *parts)
+    )(jnp.transpose(far_branch), near_leaf, charges, points, *vmem(inner, outer), tile, *parts)
 
     table = leaves + devices * slots
     return pl.pallas_call(
         functools.partial(downward_kernel, groups=groups),
         out_shape=hbm((rhs, total), F32),
-        in_specs=[SMEM()] + [VMEM()] * (groups + 10),
+        in_specs=[SMEM()] + [VMEM()] * (groups + 11),
         out_specs=VMEM(),
         scratch_shapes=[
             pltpu.VMEM((table, rhs + ROWS, rank2), BF16),
@@ -628,7 +701,7 @@
         moments,
         *vmem(received),
         basis,
-        *vmem(near),
+        *vmem(near, edge),
     )
 
 

time: 67.3 us -> 65.5 us (0.973)
  the two profiles are of different devices: /device:TPU:0 before, /device:TPU:2 now
where the time goes in v5:
time: 65.5 us; the launch traced here: 65 us
  Pallas kernels  29.2 us (45%)
  starting transfers between devices  18.7 us (29%)
  waiting for transfers between devices  17 us (26%)
    ppermute x1, waiting for transfers between devices, on_device(): lax.ppermute(shared, 'dev', [(i, i ^ members // 2) for i in range(members)])  14.8 us
    pallas_call x1, Pallas kernels, on_device(): pl.pallas_call(functools.partial(downward_kernel, groups=groups), out_sha...  10.8 us
    all_to_all x1, starting transfers between devices, on_device(): lax.all_to_all(listed, ('grp', 'dev'), split_axis=0, concat_axis=0, tiled...  6.13 us
    pallas_call x1, Pallas kernels, on_device(): pl.pallas_call(upward_kernel, out_shape=(pltpu.VMEM((leaves, rhs, rank2),...  5.39 us
    pallas_call x1, Pallas kernels, on_device(): pl.pallas_call(near_kernel, out_shape=pltpu.VMEM((rhs, total), F32), in_s...  5.18 us
    pallas_call x1, Pallas kernels, on_device(): pl.pallas_call(functools.partial(group_kernel, members=members), out_shap...  3.97 us
    ppermute x3, starting transfers between devices, on_device(): lax.ppermute(both, 'dev', [(i, i ^ s) for i in range(members)])  3.55 us
    ppermute x3, starting transfers between devices, on_device(): lax.ppermute(tile, 'grp', [(i, i ^ s) for i in range(groups)])  3.15 us
  transfers between devices with their start and end apart: 10, of which 2 were waited for; matrix products, arithmetic and copies ran while one was open for 0% of the time, Pallas kernels for 20%

profile of v5, /device:TPU:2, one launch (start us, length us, event | category | flops | bytes accessed | tf_op | source)
XLA Modules:
  0.0 65.0 jit_solution(3153985446506636533)
XLA Ops:
  0.0 5.4 %upward.1 = (bf16[64,32,128]{2,1,0:T(8,128)(2,1)S(1)}, bf16[64,8,128]{2,1,0:T(8,128)(2,1)}, bf16[32,80,128]{2,1,0:T(8,128)(2,1)}, bf16[80,128]{1,0:T(8,128)(2,1)...) custom-call(s32[4,32]{1,0:T(4,128)} %send_ref.1, bf16[32,4096]{1,0:T(8,128)(2,1)} %refs_2_.1, ...), custom_call_target="tpu_custom_call" | custom-call | tf_op jit(solution)/shard_map/upward/pallas_call | solution.py:564
  5.4 0.0 copy-start
  5.4 6.1 %all-to-all-start = ((bf16[32,80,128]{2,1,0:T(8,128)(2,1)}), bf16[32,80,128]{2,1,0:T(8,128)(2,1)S(1)}, u32[]{:S(2)}, u32[]{:S(2)}) async-start(bf16[32,80,128]{2,1,0:T(8,128)(2,1)} %get-tuple-element.35), calls=%async_computation | async-start | bytes 1310720 | tf_op jit(solution)/shard_map/all_to_all | solution.py:598
  11.6 2.4 %collective-permute-start = (bf16[200,128]{1,0:T(8,128)(2,1)S(1)}, bf16[200,128]{1,0:T(8,128)(2,1)S(1)}, u32[]{:S(2)}, u32[]{:S(2)}) collective-permute-start(bf16[200,128]{1,0:T(8,128)(2,1)S(1)} %copy-done), channel_id=1, source_target_pairs={{0,4},{1,5},{2,6},{3,7},{4,0},{5,1},{6,2},{7,3},{8,12},{9,13},{10,... | collective-permute-start | bytes 153608 | tf_op jit(solution)/shard_map/ppermute | solution.py:600
  14.0 2.5 %turn.1 = (bf16[2048,128]{1,0:T(8,128)(2,1)S(1)}, s32[64,16]{1,0:T(8,128)}) custom-call(bf16[64,64,64]{2,1,0:T(8,128)(2,1)} %down_leaf_ref.1, s32[16,64]{1,0:T(8,128)} %far_ref.1, bf16[200,128]{1,0:T(8,128)(2,1)} %get-tuple-element.21._), custom_call_target="tpu_custom_call" | custom-call | tf_op jit(solution)/shard_map/turn/pallas_call | solution.py:601
  16.5 14.8 %collective-permute-done = bf16[200,128]{1,0:T(8,128)(2,1)S(1)} collective-permute-done((bf16[200,128]{1,0:T(8,128)(2,1)S(1)}, bf16[200,128]{1,0:T(8,128)(2,1)S(1)}, u32[]{:S(2)}, u32[]{:S(2)}) %collective-permute-start) | collective-permute-done | bytes 51232 | tf_op jit(solution)/shard_map/ppermute | solution.py:600
  31.2 0.1 collective-permute-start.3
  31.3 2.9 %collective-permute-start.2 = (bf16[400,128]{1,0:T(8,128)(2,1)S(1)}, bf16[400,128]{1,0:T(8,128)(2,1)S(1)}, u32[]{:S(2)}, u32[]{:S(2)}) collective-permute-start(bf16[400,128]{1,0:T(8,128)(2,1)S(1)} %constant_dynamic-update-slice_fusion._.refs_2_.refs_7_), channel_id=1, source_target_pairs={{0,2},{1,3},{2,0},{3,1},{4,6},{5,7},{6,4},{7,5},{8,10},{9,11},{10,... | collective-permute-start | bytes 307208 | tf_op jit(solution)/shard_map/ppermute | solution.py:614
  34.3 0.5 collective-permute-start.1
  34.8 5.2 %near.1.refs_0_.refs_14_ = f32[32,4096]{1,0:T(8,128)S(1)} custom-call(s32[16,64]{1,0:T(8,128)} %refs_1_.1, bf16[32,4096]{1,0:T(8,128)(2,1)} %refs_2_.1, bf16[3,4096]{1,0:T(4,128)(2,1)} %refs_3_.1, bf16[400,128]{1,0:T(8,128)(2,1)S(1)} %constant_dynamic-update-slice_fusion._.refs_2_.refs_7_), custom_call_target="tpu_custom_call" | custom-call | tf_op jit(solution)/shard_map/near/pallas_call | solution.py:617
  40.0 1.6 %collective-permute-start.7 = (bf16[80,128]{1,0:T(8,128)(2,1)S(1)}, bf16[80,128]{1,0:T(8,128)(2,1)S(1)}, u32[]{:S(2)}, u32[]{:S(2)}) collective-permute-start(bf16[80,128]{1,0:T(8,128)(2,1)S(1)} %get-tuple-element.28), channel_id=1, source_target_pairs={{0,1},{1,0},{2,3},{3,2},{4,5},{5,4},{6,7},{7,6},{8,9},{9,8},{10,11... | collective-permute-start | bytes 61448 | tf_op jit(solution)/shard_map/ppermute | solution.py:636
  41.5 1.9 %collective-permute-start.8 = (bf16[80,128]{1,0:T(8,128)(2,1)S(1)}, bf16[80,128]{1,0:T(8,128)(2,1)S(1)}, u32[]{:S(2)}, u32[]{:S(2)}) collective-permute-start(bf16[80,128]{1,0:T(8,128)(2,1)S(1)} %get-tuple-element.29), channel_id=1, source_target_pairs={{1,2},{2,1},{3,4},{4,3},{5,6},{6,5},{7,8},{8,7},{9,10},{10,9},{11,... | collective-permute-start | bytes 61448 | tf_op jit(solution)/shard_map/ppermute | solution.py:635
  43.4 0.0 collective-permute-done.3.refs_5_.refs_10_
  43.5 0.0 collective-permute-done.2.refs_4_.refs_9_
  43.5 0.0 collective-permute-done.1.refs_3_.refs_8_
  43.5 1.4 %top.1.refs_6_.refs_1_ = bf16[40,128]{1,0:T(8,128)(2,1)} custom-call(f32[32,4096]{1,0:T(8,128)S(1)} %near.1.refs_0_.refs_14_, bf16[3,64]{1,0:T(4,128)(2,1)} %bitcast.15, bf16[400,128]{1,0:T(8,128)(2,1)S(1)} %constant_dynamic-update-slice_fusion._.refs_2_.refs_7_, bf16[400,128]{1,0:T(8,128)(2,1)S(1)} %collective-permute-done.1.refs_3_.refs_8_, ...), custom_call_target="tpu_custom_call" | custom-call | tf_op jit(solution)/shard_map/top/pallas_call | solution.py:639
  44.8 1.5 %collective-permute-start.6 = (bf16[40,128]{1,0:T(8,128)(2,1)}, bf16[40,128]{1,0:T(8,128)(2,1)S(1)}, u32[]{:S(2)}, u32[]{:S(2)}) collective-permute-start(bf16[40,128]{1,0:T(8,128)(2,1)} %top.1.refs_6_.refs_1_), channel_id=1, source_target_pairs={{0,24},{8,16},{16,8},{24,0},{1,25},{9,17},{17,9},{25,1},{2,26},{10... | collective-permute-start | bytes 30728 | tf_op jit(solution)/shard_map/ppermute | solution.py:648
  46.4 1.6 %collective-permute-start.5 = (bf16[40,128]{1,0:T(8,128)(2,1)}, bf16[40,128]{1,0:T(8,128)(2,1)S(1)}, u32[]{:S(2)}, u32[]{:S(2)}) collective-permute-start(bf16[40,128]{1,0:T(8,128)(2,1)} %top.1.refs_6_.refs_1_), channel_id=1, source_target_pairs={{0,16},{8,24},{16,0},{24,8},{1,17},{9,25},{17,1},{25,9},{2,18},{10... | collective-permute-start | bytes 30728 | tf_op jit(solution)/shard_map/ppermute | solution.py:648
  48.0 0.0 collective-permute-done.7.refs_4_
  48.0 2.2 %collective-permute-done.8.refs_5_ = bf16[80,128]{1,0:T(8,128)(2,1)S(1)} collective-permute-done((bf16[80,128]{1,0:T(8,128)(2,1)S(1)}, bf16[80,128]{1,0:T(8,128)(2,1)S(1)}, u32[]{:S(2)}, u32[]{:S(2)}) %collective-permute-start.8) | collective-permute-done | bytes 20512 | tf_op jit(solution)/shard_map/ppermute | solution.py:635
  50.2 4.0 %group.1 = (f32[8,32,64]{2,1,0:T(8,128)}, f32[32,64]{1,0:T(8,128)}, f32[32,512]{1,0:T(8,128)S(1)}) custom-call(s32[8,16]{1,0:T(8,128)} %bitcast.13, s32[16,64]{1,0:T(8,128)} %refs_1_.1, bf16[32,4096]{1,0:T(8,128)(2,1)} %refs_2_.1, bf16[3,4096]{1,0:T(4,128)(2,1)} %refs_3_.1, bf16[80,128]{1,0:T(8,128)(2,1)S(1)} %collective-permute-done.7.refs_4_, ...), custom_call_target="tpu_custom_call" | custom-call | tf_op jit(solution)/shard_map/group/pallas_call | solution.py:649
  54.2 0.0 collective-permute-done.4.refs_2_
  54.2 0.0 all-to-all-done.refs_12_
  54.2 10.8 %downward.1 = f32[32,4096]{1,0:T(8,128)} custom-call(s32[64,16]{1,0:T(8,128)} %get-tuple-element.22.refs_0_, bf16[40,128]{1,0:T(8,128)(2,1)} %top.1.refs_6_.refs_1_, bf16[40,128]{1,0:T(8,128)(2,1)S(1)} %collective-permute-done.4.refs_2_, bf16[40,128]{1,0:T(8,128)(2,1)S(1)} %collective-permute-done.5.refs_3_, ...), custom_call_target="tpu_custom_call" | custom-call | tf_op jit(solution)/shard_map/downward/pallas_call | solution.py:670
  (6 shorter events, 0.0 us)
Async XLA Ops:
  5.4 6.2 %copy-start = (bf16[200,128]{1,0:T(8,128)(2,1)S(1)}, bf16[200,128]{1,0:T(8,128)(2,1)}, u32[]{:S(2)}) copy-start(bf16[200,128]{1,0:T(8,128)(2,1)} %get-tuple-element.21._) | copy-start | bytes 153604
  5.4 48.8 %all-to-all-start = ((bf16[32,80,128]{2,1,0:T(8,128)(2,1)}), bf16[32,80,128]{2,1,0:T(8,128)(2,1)S(1)}, u32[]{:S(2)}, u32[]{:S(2)}) async-start(bf16[32,80,128]{2,1,0:T(8,128)(2,1)} %get-tuple-element.35), calls=%async_computation | async-start | bytes 1310720 | tf_op jit(solution)/shard_map/all_to_all | solution.py:598
  11.6 19.7 %collective-permute-start = (bf16[200,128]{1,0:T(8,128)(2,1)S(1)}, bf16[200,128]{1,0:T(8,128)(2,1)S(1)}, u32[]{:S(2)}, u32[]{:S(2)}) collective-permute-start(bf16[200,128]{1,0:T(8,128)(2,1)S(1)} %copy-done), channel_id=1, source_target_pairs={{0,4},{1,5},{2,6},{3,7},{4,0},{5,1},{6,2},{7,3},{8,12},{9,13},{10,... | collective-permute-start | bytes 153608 | tf_op jit(solution)/shard_map/ppermute | solution.py:600
  31.2 12.2 %collective-permute-start.3 = (bf16[400,128]{1,0:T(8,128)(2,1)S(1)}, bf16[400,128]{1,0:T(8,128)(2,1)S(1)}, u32[]{:S(2)}, u32[]{:S(2)}) collective-permute-start(bf16[400,128]{1,0:T(8,128)(2,1)S(1)} %constant_dynamic-update-slice_fusion._.refs_2_.refs_7_), channel_id=1, source_target_pairs={{0,3},{1,2},{2,1},{3,0},{4,7},{5,6},{6,5},{7,4},{8,11},{9,10},{10,... | collective-permute-start | bytes 307208 | tf_op jit(solution)/shard_map/ppermute | solution.py:614
  31.3 12.1 %collective-permute-start.2 = (bf16[400,128]{1,0:T(8,128)(2,1)S(1)}, bf16[400,128]{1,0:T(8,128)(2,1)S(1)}, u32[]{:S(2)}, u32[]{:S(2)}) collective-permute-start(bf16[400,128]{1,0:T(8,128)(2,1)S(1)} %constant_dynamic-update-slice_fusion._.refs_2_.refs_7_), channel_id=1, source_target_pairs={{0,2},{1,3},{2,0},{3,1},{4,6},{5,7},{6,4},{7,5},{8,10},{9,11},{10,... | collective-permute-start | bytes 307208 | tf_op jit(solution)/shard_map/ppermute | solution.py:614
  34.3 9.2 %collective-permute-start.1 = (bf16[400,128]{1,0:T(8,128)(2,1)S(1)}, bf16[400,128]{1,0:T(8,128)(2,1)S(1)}, u32[]{:S(2)}, u32[]{:S(2)}) collective-permute-start(bf16[400,128]{1,0:T(8,128)(2,1)S(1)} %constant_dynamic-update-slice_fusion._.refs_2_.refs_7_), channel_id=1, source_target_pairs={{0,1},{1,0},{2,3},{3,2},{4,5},{5,4},{6,7},{7,6},{8,9},{9,8},{10,11... | collective-permute-start | bytes 307208 | tf_op jit(solution)/shard_map/ppermute | solution.py:614
  40.0 8.0 %collective-permute-start.7 = (bf16[80,128]{1,0:T(8,128)(2,1)S(1)}, bf16[80,128]{1,0:T(8,128)(2,1)S(1)}, u32[]{:S(2)}, u32[]{:S(2)}) collective-permute-start(bf16[80,128]{1,0:T(8,128)(2,1)S(1)} %get-tuple-element.28), channel_id=1, source_target_pairs={{0,1},{1,0},{2,3},{3,2},{4,5},{5,4},{6,7},{7,6},{8,9},{9,8},{10,11... | collective-permute-start | bytes 61448 | tf_op jit(solution)/shard_map/ppermute | solution.py:636
  41.5 8.7 %collective-permute-start.8 = (bf16[80,128]{1,0:T(8,128)(2,1)S(1)}, bf16[80,128]{1,0:T(8,128)(2,1)S(1)}, u32[]{:S(2)}, u32[]{:S(2)}) collective-permute-start(bf16[80,128]{1,0:T(8,128)(2,1)S(1)} %get-tuple-element.29), channel_id=1, source_target_pairs={{1,2},{2,1},{3,4},{4,3},{5,6},{6,5},{7,8},{8,7},{9,10},{10,9},{11,... | collective-permute-start | bytes 61448 | tf_op jit(solution)/shard_map/ppermute | solution.py:635
  44.8 9.4 %collective-permute-start.6 = (bf16[40,128]{1,0:T(8,128)(2,1)}, bf16[40,128]{1,0:T(8,128)(2,1)S(1)}, u32[]{:S(2)}, u32[]{:S(2)}) collective-permute-start(bf16[40,128]{1,0:T(8,128)(2,1)} %top.1.refs_6_.refs_1_), channel_id=1, source_target_pairs={{0,24},{8,16},{16,8},{24,0},{1,25},{9,17},{17,9},{25,1},{2,26},{10... | collective-permute-start | bytes 30728 | tf_op jit(solution)/shard_map/ppermute | solution.py:648
  46.4 7.8 %collective-permute-start.5 = (bf16[40,128]{1,0:T(8,128)(2,1)}, bf16[40,128]{1,0:T(8,128)(2,1)S(1)}, u32[]{:S(2)}, u32[]{:S(2)}) collective-permute-start(bf16[40,128]{1,0:T(8,128)(2,1)} %top.1.refs_6_.refs_1_), channel_id=1, source_target_pairs={{0,16},{8,24},{16,0},{24,8},{1,17},{9,25},{17,1},{25,9},{2,18},{10... | collective-permute-start | bytes 30728 | tf_op jit(solution)/shard_map/ppermute | solution.py:648
  48.0 6.2 %collective-permute-start.4 = (bf16[40,128]{1,0:T(8,128)(2,1)}, bf16[40,128]{1,0:T(8,128)(2,1)S(1)}, u32[]{:S(2)}, u32[]{:S(2)}) collective-permute-start(bf16[40,128]{1,0:T(8,128)(2,1)} %top.1.refs_6_.refs_1_), channel_id=1, source_target_pairs={{0,8},{8,0},{16,24},{24,16},{1,9},{9,1},{17,25},{25,17},{2,10},{10... | collective-permute-start | bytes 30728 | tf_op jit(solution)/shard_map/ppermute | solution.py:648

commit v6 on v5

--- a/solution.py
+++ b/solution.py
@@ -11,7 +11,7 @@
 REACH = 4
 FAN = 8
 ROUND = 8
-PAIRS = 2
+PAIRS = 7
 
 INV_FOUR_PI = 1.0 / (4.0 * math.pi)
 SOFTEN = 0.25
@@ -89,9 +89,9 @@
     return jnp.concatenate([upper, lower], axis=0).astype(BF16)
 
 
-def put_rows(ref, rows, count):
+def put_rows(ref, rows, count, first=0):
     for f in range(ROWS):
-        value = rows[f] if f < len(rows) else jnp.zeros_like(rows[0])
+        value = rows[f - first] if 0 <= f - first < len(rows) else jnp.zeros_like(rows[0])
         ref[pl.ds(f, count, stride=ROWS), :] = value
 
 
@@ -125,15 +125,18 @@
 
 def upward_kernel(
     send_ref, charges_ref, points_ref, basis_ref, proxy_ref, up_leaf_hbm, up_branch_ref, up_device_ref, pbranch_ref,
-    pdevice_ref, moment_ref, own_ref, out_ref, inner_ref, outer_ref, shared_ref, tile_ref, up_leaf_ref, scratch_ref,
-    branch_ref, sem,
+    pdevice_ref, moment_ref, own_ref, out_ref, inner_ref, outer_ref, shared_ref, tile_ref, late_ref, up_leaf_ref,
+    scratch_ref, branch_ref, sem,
 ):
     slots, devices = send_ref.shape
     leaves, rhs, rank2 = moment_ref.shape
     transfers = fetch(up_leaf_hbm, up_leaf_ref, sem)
     low = low_half((rhs, rank2))
-    put_rows(tile_ref, source_rows(*[twice(jnp.transpose(proxy_ref[c].astype(F32))) for c in range(3)]), leaves)
+    rows = source_rows(*[twice(jnp.transpose(proxy_ref[c].astype(F32))) for c in range(3)])
+    put_rows(tile_ref, rows, leaves)
     own_ref[...] = tile_ref[...].astype(BF16).reshape(own_ref.shape)
+    put_rows(tile_ref, rows[:3], leaves)
+    put_rows(late_ref, rows[:3], leaves, 3)
 
     def leaf_pair(i, carry):
         columns = pl.ds(pl.multiple_of(i * rank2, rank2), rank2)
@@ -152,10 +155,19 @@
 
     def pack(p, carry):
         s = [send_ref[t, p] for t in range(slots)]
+        tiles = []
         for q in range(slots // 2):
             first, second = s[2 * q], s[2 * q + 1]
             out_ref[p, q * rhs : (q + 1) * rhs, :] = pair(low, moment_ref[first], moment_ref[second])
-            out_ref[p, base + q * ROWS : base + (q + 1) * ROWS, :] = pair(low8, own_ref[first], own_ref[second])
+            ref = (tile_ref, late_ref)[q]
+            tiles.append(
+                pair(
+                    low8,
+                    ref[pl.ds(pl.multiple_of(first * ROWS, ROWS), ROWS), :],
+                    ref[pl.ds(pl.multiple_of(second * ROWS, ROWS), ROWS), :],
+                )
+            )
+        out_ref[p, base:, :] = (tiles[0] + tiles[1]).astype(BF16)
         return carry
 
     lax.fori_loop(0, devices, pack, 0, unroll=4)
@@ -289,30 +301,31 @@
     first = halo // lanes
     rounds = (total - 2 * halo) // lanes // width
 
-    def evaluate(i, kern_ref):
+    def evaluate(i, n, kern_ref):
+        j = first + i * width + n
+        start = pl.multiple_of(j * lanes, lanes)
+        near_couplings(
+            target_ref[:, pl.ds(start, lanes)],
+            source_ref[:, pl.ds(pl.multiple_of(start - halo, lanes), reach)],
+            [weight_ref[h, pl.ds(2 * j + h, 1), :] for h in range(2)],
+            kern_ref.at[n],
+        )
+
+    def apply(i, n, kern_ref):
+        start = pl.multiple_of((first + i * width + n) * lanes, lanes)
+        columns = pl.ds(pl.multiple_of(start - halo, lanes), reach)
+        out_ref[:, pl.ds(start, lanes)] = dot_t(charges_ref[:, columns], kern_ref[n])
+
+    for n in range(width):
+        evaluate(0, n, kern_a_ref)
+
+    def step(t, carry):
         for n in range(width):
-            j = first + i * width + n
-            start = pl.multiple_of(j * lanes, lanes)
-            near_couplings(
-                target_ref[:, pl.ds(start, lanes)],
-                source_ref[:, pl.ds(pl.multiple_of(start - halo, lanes), reach)],
-                [weight_ref[h, pl.ds(2 * j + h, 1), :] for h in range(2)],
-                kern_ref.at[n],
-            )
-
-    def apply(i, kern_ref):
+            evaluate(2 * t + 1, n, kern_b_ref)
+            apply(2 * t, n, kern_a_ref)
         for n in range(width):
-            start = pl.multiple_of((first + i * width + n) * lanes, lanes)
-            columns = pl.ds(pl.multiple_of(start - halo, lanes), reach)
-            out_ref[:, pl.ds(start, lanes)] = dot_t(charges_ref[:, columns], kern_ref[n])
-
-    evaluate(0, kern_a_ref)
-
-    def step(t, carry):
-        evaluate(2 * t + 1, kern_b_ref)
-        apply(2 * t, kern_a_ref)
-        evaluate(jnp.minimum(2 * t + 2, rounds - 1), kern_a_ref)
-        apply(2 * t + 1, kern_b_ref)
+            evaluate(jnp.minimum(2 * t + 2, rounds - 1), n, kern_a_ref)
+            apply(2 * t + 1, n, kern_b_ref)
         return carry
 
     lax.fori_loop(0, rounds // 2, step, 0)
@@ -454,11 +467,24 @@
     table_ref[:leaves, rhs:, :] = own_ref[...]
     base = slots // 2 * rhs
 
+    row = lax.broadcasted_iota(jnp.int32, (ROWS, rank2), 0)
+    low_r = low_half((ROWS, rank2))
+    zero = jnp.zeros((ROWS, rank2), F32)
+
     def unpack(p, carry):
+        tile = recv_ref[p, base:, :].astype(F32)
+        squares = 0.25 * tile * tile
+        parts = three(squares + pltpu.roll(squares, ROWS - 1, 0) + pltpu.roll(squares, ROWS - 2, 0))
         for q in range(slots // 2):
             slot = leaves + p * slots + 2 * q
             put_pair(table_ref, slot, recv_ref[p, q * rhs : (q + 1) * rhs, :], 0)
-            put_pair(table_ref, slot, recv_ref[p, base + q * ROWS : base + (q + 1) * ROWS, :], rhs)
+            rows = jnp.where(row < 3, pltpu.roll(tile, ROWS - 3, 0) if q else tile, zero)
+            for n, part in enumerate(parts):
+                shift = 3 + n - 3 * q
+                rows = jnp.where(row == 3 + n, pltpu.roll(part, shift, 0) if shift else part, rows)
+            other = pltpu.roll(rows, rank, 1)
+            table_ref[slot, rhs:, :] = pair(low_r, rows, other).astype(BF16)
+            table_ref[slot + 1, rhs:, :] = pair(low_r, other, rows).astype(BF16)
         return carry
 
     lax.fori_loop(0, devices, unpack, 0, unroll=min(devices, 32))
@@ -473,48 +499,48 @@
             first, second = far_ref[b, e], far_ref[b, e + 1]
             ref[:, e * rank : (e + 2) * rank] = pair(low, table_ref[first, rows, :], table_ref[second, rows, :])
 
-    def collect_sources(i, targets_ref, sources_ref):
-        for h in range(width):
-            b = width * i + h
-            targets_ref[h] = jnp.transpose(target_of(table_ref[b, rhs:, :rank]))
-            gather(b, low_s, slice(rhs, None), sources_ref.at[h])
-
-    def collect_moments(i, moments_ref):
-        for h in range(width):
-            gather(width * i + h, low, slice(None, rhs), moments_ref.at[h])
-
-    def evaluate(targets_ref, sources_ref, kern_ref):
-        for h in range(width):
-            sources = jnp.concatenate([sources_ref[h], source_tail(sources_ref.shape[2])], axis=0)
-            kern_ref[h] = kern_of(dot(targets_ref[h], sources))
-
-    def apply(i, moments_ref, kern_ref):
-        sums = []
-        for h in range(width):
-            b = width * i + h
-            far = dot_t(moments_ref[h], kern_ref[h])
-            rows = down_ref[pl.ds(pl.multiple_of(b * half, half), half), :]
-            sums.append((far + dot_t(parent_ref[b // FAN], spread_rows(rows, low_d))).astype(BF16))
-        return tuple(sums)
-
-    def finish(i, sums):
-        for h in range(0, width, 2):
+    def collect_sources(i, h, targets_ref, sources_ref):
+        b = width * i + h
+        targets_ref[h] = jnp.transpose(target_of(table_ref[b, rhs:, :rank]))
+        gather(b, low_s, slice(rhs, None), sources_ref.at[h])
+
+    def collect_moments(i, h, moments_ref):
+        gather(width * i + h, low, slice(None, rhs), moments_ref.at[h])
+
+    def evaluate(h, targets_ref, sources_ref, kern_ref):
+        sources = jnp.concatenate([sources_ref[h], source_tail(sources_ref.shape[2])], axis=0)
+        kern_ref[h] = kern_of(dot(targets_ref[h], sources))
+
+    def apply(i, h, moments_ref, kern_ref):
+        b = width * i + h
+        far = dot_t(moments_ref[h], kern_ref[h])
+        rows = down_ref[pl.ds(pl.multiple_of(b * half, half), half), :]
+        return (far + dot_t(parent_ref[b // FAN], spread_rows(rows, low_d))).astype(BF16)
+
+    def finish(i, sums, starts=None):
+        for h in starts or range(0, width, 2):
             columns = pl.ds(pl.multiple_of((width * i + h) * rank, rank2), rank2)
             product = dot(jnp.concatenate(sums[h : h + 2], axis=0), basis_ref[:, columns])
             out_ref[:, columns] = near_ref[:, columns] + pair(low, product[:rhs], product[rhs:])
 
     def stage(i, sums, this, other):
-        finish(jnp.maximum(i - 2, 0), sums)
-        evaluate(this[0], this[1], this[3])
-        sums = apply(jnp.maximum(i - 1, 0), other[2], other[3])
-        collect_sources(jnp.minimum(i + 2, rounds - 1), this[0], this[1])
-        collect_moments(jnp.minimum(i + 1, rounds - 1), other[2])
-        return sums
+        done, last = jnp.maximum(i - 2, 0), sums
+        before, after, later = jnp.maximum(i - 1, 0), jnp.minimum(i + 1, rounds - 1), jnp.minimum(i + 2, rounds - 1)
+        sums = []
+        for h in range(width):
+            evaluate(h, this[0], this[1], this[3])
+            sums.append(apply(before, h, other[2], other[3]))
+            if h % 2 == 0:
+                finish(done, last, (h,))
+            collect_sources(later, h, this[0], this[1])
+            collect_moments(after, h, other[2])
+        return tuple(sums)
 
     even, odd = buffers[:4], buffers[4:]
-    collect_sources(0, *even[:2])
-    collect_sources(1, *odd[:2])
-    collect_moments(0, even[2])
+    for h in range(width):
+        collect_sources(0, h, *even[:2])
+        collect_sources(1, h, *odd[:2])
+        collect_moments(0, h, even[2])
     odd[2][...] = jnp.zeros_like(odd[2])
     odd[3][...] = jnp.zeros_like(odd[3])
 
@@ -523,7 +549,7 @@
 
     sums = lax.fori_loop(0, rounds // 2, step, (jnp.zeros((rhs, rank), BF16),) * width)
     finish(rounds - 2, sums)
-    finish(rounds - 1, apply(rounds - 1, odd[2], odd[3]))
+    finish(rounds - 1, tuple(apply(rounds - 1, h, odd[2], odd[3]) for h in range(width)))
     total, halo = out_ref.shape[1], edge_ref.shape[1] // 2
     out_ref[:, :halo] += edge_ref[:, :halo]
     out_ref[:, total - halo :] += edge_ref[:, halo:]
@@ -559,14 +585,14 @@
     rank2 = 2 * rank
     half = rank // 2
     halo = REACH * size
-    assert rank == size and slots % 2 == 0 and branches % 2 == 0 and members % 2 == 0
+    assert rank == size and slots == 4 and branches % 2 == 0 and members % 2 == 0
 
     moments, own, listed, inner, outer, shared = pl.pallas_call(
         upward_kernel,
         out_shape=(
             pltpu.VMEM((leaves, rhs, rank2), BF16),
             hbm((leaves, ROWS, rank2), BF16),
-            hbm((devices, slots // 2 * (rhs + ROWS), rank2), BF16),
+            hbm((devices, slots // 2 * rhs + ROWS, rank2), BF16),
             pltpu.VMEM((halo // rank2 * (rhs + ROWS), rank2), BF16),
             pltpu.VMEM((halo // rank2 * (rhs + ROWS), rank2), BF16),
             hbm(((branches // 2 + 1) * (rhs + ROWS), rank2), BF16),
@@ -574,6 +600,7 @@
         in_specs=[SMEM()] + [VMEM()] * 4 + [ANY()] + [VMEM()] * 4,
         out_specs=(VMEM(),) * 6,
         scratch_shapes=[
+            pltpu.VMEM((leaves * ROWS, rank2), F32),
             pltpu.VMEM((leaves * ROWS, rank2), F32),
             pltpu.VMEM(up_leaf.shape, BF16),
             pltpu.VMEM((leaves * half, rank2), F32),

time: 65.5 us -> 62.1 us (0.948)
  Pallas kernels: 29.2 us -> 27.1 us
  waiting for transfers between devices: 17 us -> 15.6 us
    ppermute x1, waiting for transfers between devices: 14.8 us -> 13.4 us  [on_device(): lax.ppermute(shared, 'dev', [(i, i ^ members // 2) for i in range(members)])]
    pallas_call x1, Pallas kernels: 10.8 us -> 9.57 us  [on_device(): pl.pallas_call(functools.partial(downward_kernel, groups=groups), out_sha...]
    pallas_call x1, Pallas kernels: 5.18 us -> 4.34 us  [on_device(): pl.pallas_call(near_kernel, out_shape=pltpu.VMEM((rhs, total), F32), in_s...]
where the time goes in v6:
time: 62.1 us; the launch traced here: 61.6 us
  Pallas kernels  27.1 us (44%)
  starting transfers between devices  18.7 us (30%)
  waiting for transfers between devices  15.6 us (25%)
    ppermute x1, waiting for transfers between devices, on_device(): lax.ppermute(shared, 'dev', [(i, i ^ members // 2) for i in range(members)])  13.4 us
    pallas_call x1, Pallas kernels, on_device(): pl.pallas_call(functools.partial(downward_kernel, groups=groups), out_sha...  9.57 us
    all_to_all x1, starting transfers between devices, on_device(): lax.all_to_all(listed, ('grp', 'dev'), split_axis=0, concat_axis=0, tiled...  6.13 us
    pallas_call x1, Pallas kernels, on_device(): pl.pallas_call(upward_kernel, out_shape=(pltpu.VMEM((leaves, rhs, rank2),...  5.43 us
    pallas_call x1, Pallas kernels, on_device(): pl.pallas_call(near_kernel, out_shape=pltpu.VMEM((rhs, total), F32), in_s...  4.34 us
    pallas_call x1, Pallas kernels, on_device(): pl.pallas_call(functools.partial(group_kernel, members=members), out_shap...  3.98 us
    ppermute x3, starting transfers between devices, on_device(): lax.ppermute(both, 'dev', [(i, i ^ s) for i in range(members)])  3.55 us
    ppermute x3, starting transfers between devices, on_device(): lax.ppermute(tile, 'grp', [(i, i ^ s) for i in range(groups)])  3.15 us
  transfers between devices with their start and end apart: 10, of which 2 were waited for; matrix products, arithmetic and copies ran while one was open for 0% of the time, Pallas kernels for 20%

profile of v6, /device:TPU:2, one launch (start us, length us, event | category | flops | bytes accessed | tf_op | source)
XLA Modules:
  0.0 61.6 jit_solution(9187306721164112603)
XLA Ops:
  0.0 5.4 %upward.1 = (bf16[64,32,128]{2,1,0:T(8,128)(2,1)S(1)}, bf16[64,8,128]{2,1,0:T(8,128)(2,1)}, bf16[32,72,128]{2,1,0:T(8,128)(2,1)}, bf16[80,128]{1,0:T(8,128)(2,1)...) custom-call(s32[4,32]{1,0:T(4,128)} %send_ref.1, bf16[32,4096]{1,0:T(8,128)(2,1)} %refs_2_.1, ...), custom_call_target="tpu_custom_call" | custom-call | tf_op jit(solution)/shard_map/upward/pallas_call | solution.py:590
  5.4 0.0 copy-start
  5.4 6.1 %all-to-all-start = ((bf16[32,72,128]{2,1,0:T(8,128)(2,1)}), bf16[32,72,128]{2,1,0:T(8,128)(2,1)S(1)}, u32[]{:S(2)}, u32[]{:S(2)}) async-start(bf16[32,72,128]{2,1,0:T(8,128)(2,1)} %get-tuple-element.35), calls=%async_computation | async-start | bytes 1179648 | tf_op jit(solution)/shard_map/all_to_all | solution.py:625
  11.6 2.4 %collective-permute-start = (bf16[200,128]{1,0:T(8,128)(2,1)S(1)}, bf16[200,128]{1,0:T(8,128)(2,1)S(1)}, u32[]{:S(2)}, u32[]{:S(2)}) collective-permute-start(bf16[200,128]{1,0:T(8,128)(2,1)S(1)} %copy-done), channel_id=1, source_target_pairs={{0,4},{1,5},{2,6},{3,7},{4,0},{5,1},{6,2},{7,3},{8,12},{9,13},{10,... | collective-permute-start | bytes 153608 | tf_op jit(solution)/shard_map/ppermute | solution.py:627
  14.0 2.5 %turn.1 = (bf16[2048,128]{1,0:T(8,128)(2,1)S(1)}, s32[64,16]{1,0:T(8,128)}) custom-call(bf16[64,64,64]{2,1,0:T(8,128)(2,1)} %down_leaf_ref.1, s32[16,64]{1,0:T(8,128)} %far_ref.1, bf16[200,128]{1,0:T(8,128)(2,1)} %get-tuple-element.21._), custom_call_target="tpu_custom_call" | custom-call | tf_op jit(solution)/shard_map/turn/pallas_call | solution.py:628
  16.5 13.4 %collective-permute-done = bf16[200,128]{1,0:T(8,128)(2,1)S(1)} collective-permute-done((bf16[200,128]{1,0:T(8,128)(2,1)S(1)}, bf16[200,128]{1,0:T(8,128)(2,1)S(1)}, u32[]{:S(2)}, u32[]{:S(2)}) %collective-permute-start) | collective-permute-done | bytes 51232 | tf_op jit(solution)/shard_map/ppermute | solution.py:627
  29.9 0.1 collective-permute-start.3
  29.9 2.9 %collective-permute-start.2 = (bf16[400,128]{1,0:T(8,128)(2,1)S(1)}, bf16[400,128]{1,0:T(8,128)(2,1)S(1)}, u32[]{:S(2)}, u32[]{:S(2)}) collective-permute-start(bf16[400,128]{1,0:T(8,128)(2,1)S(1)} %constant_dynamic-update-slice_fusion._.refs_2_.refs_7_), channel_id=1, source_target_pairs={{0,2},{1,3},{2,0},{3,1},{4,6},{5,7},{6,4},{7,5},{8,10},{9,11},{10,... | collective-permute-start | bytes 307208 | tf_op jit(solution)/shard_map/ppermute | solution.py:641
  32.9 0.5 collective-permute-start.1
  33.4 4.3 %near.1.refs_0_.refs_14_ = f32[32,4096]{1,0:T(8,128)S(1)} custom-call(s32[16,64]{1,0:T(8,128)} %refs_1_.1, bf16[32,4096]{1,0:T(8,128)(2,1)} %refs_2_.1, bf16[3,4096]{1,0:T(4,128)(2,1)} %refs_3_.1, bf16[400,128]{1,0:T(8,128)(2,1)S(1)} %constant_dynamic-update-slice_fusion._.refs_2_.refs_7_), custom_call_target="tpu_custom_call" | custom-call | tf_op jit(solution)/shard_map/near/pallas_call | solution.py:644
  37.8 1.6 %collective-permute-start.7 = (bf16[80,128]{1,0:T(8,128)(2,1)S(1)}, bf16[80,128]{1,0:T(8,128)(2,1)S(1)}, u32[]{:S(2)}, u32[]{:S(2)}) collective-permute-start(bf16[80,128]{1,0:T(8,128)(2,1)S(1)} %get-tuple-element.28), channel_id=1, source_target_pairs={{0,1},{1,0},{2,3},{3,2},{4,5},{5,4},{6,7},{7,6},{8,9},{9,8},{10,11... | collective-permute-start | bytes 61448 | tf_op jit(solution)/shard_map/ppermute | solution.py:663
  39.3 1.9 %collective-permute-start.8 = (bf16[80,128]{1,0:T(8,128)(2,1)S(1)}, bf16[80,128]{1,0:T(8,128)(2,1)S(1)}, u32[]{:S(2)}, u32[]{:S(2)}) collective-permute-start(bf16[80,128]{1,0:T(8,128)(2,1)S(1)} %get-tuple-element.29), channel_id=1, source_target_pairs={{1,2},{2,1},{3,4},{4,3},{5,6},{6,5},{7,8},{8,7},{9,10},{10,9},{11,... | collective-permute-start | bytes 61448 | tf_op jit(solution)/shard_map/ppermute | solution.py:662
  41.3 0.0 collective-permute-done.3.refs_5_.refs_10_
  41.3 0.0 collective-permute-done.1.refs_3_.refs_8_
  41.3 1.4 %top.1.refs_6_.refs_1_ = bf16[40,128]{1,0:T(8,128)(2,1)} custom-call(f32[32,4096]{1,0:T(8,128)S(1)} %near.1.refs_0_.refs_14_, bf16[3,64]{1,0:T(4,128)(2,1)} %bitcast.15, bf16[400,128]{1,0:T(8,128)(2,1)S(1)} %constant_dynamic-update-slice_fusion._.refs_2_.refs_7_, bf16[400,128]{1,0:T(8,128)(2,1)S(1)} %collective-permute-done.1.refs_3_.refs_8_, ...), custom_call_target="tpu_custom_call" | custom-call | tf_op jit(solution)/shard_map/top/pallas_call | solution.py:666
  42.7 1.5 %collective-permute-start.6 = (bf16[40,128]{1,0:T(8,128)(2,1)}, bf16[40,128]{1,0:T(8,128)(2,1)S(1)}, u32[]{:S(2)}, u32[]{:S(2)}) collective-permute-start(bf16[40,128]{1,0:T(8,128)(2,1)} %top.1.refs_6_.refs_1_), channel_id=1, source_target_pairs={{0,24},{8,16},{16,8},{24,0},{1,25},{9,17},{17,9},{25,1},{2,26},{10... | collective-permute-start | bytes 30728 | tf_op jit(solution)/shard_map/ppermute | solution.py:675
  44.2 1.6 %collective-permute-start.5 = (bf16[40,128]{1,0:T(8,128)(2,1)}, bf16[40,128]{1,0:T(8,128)(2,1)S(1)}, u32[]{:S(2)}, u32[]{:S(2)}) collective-permute-start(bf16[40,128]{1,0:T(8,128)(2,1)} %top.1.refs_6_.refs_1_), channel_id=1, source_target_pairs={{0,16},{8,24},{16,0},{24,8},{1,17},{9,25},{17,1},{25,9},{2,18},{10... | collective-permute-start | bytes 30728 | tf_op jit(solution)/shard_map/ppermute | solution.py:675
  45.8 0.0 collective-permute-start.4
  45.8 0.0 collective-permute-done.7.refs_4_
  45.8 2.2 %collective-permute-done.8.refs_5_ = bf16[80,128]{1,0:T(8,128)(2,1)S(1)} collective-permute-done((bf16[80,128]{1,0:T(8,128)(2,1)S(1)}, bf16[80,128]{1,0:T(8,128)(2,1)S(1)}, u32[]{:S(2)}, u32[]{:S(2)}) %collective-permute-start.8) | collective-permute-done | bytes 20512 | tf_op jit(solution)/shard_map/ppermute | solution.py:662
  48.0 4.0 %group.1 = (f32[8,32,64]{2,1,0:T(8,128)}, f32[32,64]{1,0:T(8,128)}, f32[32,512]{1,0:T(8,128)S(1)}) custom-call(s32[8,16]{1,0:T(8,128)} %bitcast.13, s32[16,64]{1,0:T(8,128)} %refs_1_.1, bf16[32,4096]{1,0:T(8,128)(2,1)} %refs_2_.1, bf16[3,4096]{1,0:T(4,128)(2,1)} %refs_3_.1, bf16[80,128]{1,0:T(8,128)(2,1)S(1)} %collective-permute-done.7.refs_4_, ...), custom_call_target="tpu_custom_call" | custom-call | tf_op jit(solution)/shard_map/group/pallas_call | solution.py:676
  52.0 0.0 collective-permute-done.5.refs_3_
  52.0 0.0 collective-permute-done.4.refs_2_
  52.1 9.6 %downward.1 = f32[32,4096]{1,0:T(8,128)} custom-call(s32[64,16]{1,0:T(8,128)} %get-tuple-element.22.refs_0_, bf16[40,128]{1,0:T(8,128)(2,1)} %top.1.refs_6_.refs_1_, bf16[40,128]{1,0:T(8,128)(2,1)S(1)} %collective-permute-done.4.refs_2_, bf16[40,128]{1,0:T(8,128)(2,1)S(1)} %collective-permute-done.5.refs_3_, ...), custom_call_target="tpu_custom_call" | custom-call | tf_op jit(solution)/shard_map/downward/pallas_call | solution.py:697
  (6 shorter events, 0.0 us)
Async XLA Ops:
  5.4 6.2 %copy-start = (bf16[200,128]{1,0:T(8,128)(2,1)S(1)}, bf16[200,128]{1,0:T(8,128)(2,1)}, u32[]{:S(2)}) copy-start(bf16[200,128]{1,0:T(8,128)(2,1)} %get-tuple-element.21._) | copy-start | bytes 153604
  5.4 46.6 %all-to-all-start = ((bf16[32,72,128]{2,1,0:T(8,128)(2,1)}), bf16[32,72,128]{2,1,0:T(8,128)(2,1)S(1)}, u32[]{:S(2)}, u32[]{:S(2)}) async-start(bf16[32,72,128]{2,1,0:T(8,128)(2,1)} %get-tuple-element.35), calls=%async_computation | async-start | bytes 1179648 | tf_op jit(solution)/shard_map/all_to_all | solution.py:625
  11.6 18.3 %collective-permute-start = (bf16[200,128]{1,0:T(8,128)(2,1)S(1)}, bf16[200,128]{1,0:T(8,128)(2,1)S(1)}, u32[]{:S(2)}, u32[]{:S(2)}) collective-permute-start(bf16[200,128]{1,0:T(8,128)(2,1)S(1)} %copy-done), channel_id=1, source_target_pairs={{0,4},{1,5},{2,6},{3,7},{4,0},{5,1},{6,2},{7,3},{8,12},{9,13},{10,... | collective-permute-start | bytes 153608 | tf_op jit(solution)/shard_map/ppermute | solution.py:627
  29.9 11.4 %collective-permute-start.3 = (bf16[400,128]{1,0:T(8,128)(2,1)S(1)}, bf16[400,128]{1,0:T(8,128)(2,1)S(1)}, u32[]{:S(2)}, u32[]{:S(2)}) collective-permute-start(bf16[400,128]{1,0:T(8,128)(2,1)S(1)} %constant_dynamic-update-slice_fusion._.refs_2_.refs_7_), channel_id=1, source_target_pairs={{0,3},{1,2},{2,1},{3,0},{4,7},{5,6},{6,5},{7,4},{8,11},{9,10},{10,... | collective-permute-start | bytes 307208 | tf_op jit(solution)/shard_map/ppermute | solution.py:641
  29.9 11.3 %collective-permute-start.2 = (bf16[400,128]{1,0:T(8,128)(2,1)S(1)}, bf16[400,128]{1,0:T(8,128)(2,1)S(1)}, u32[]{:S(2)}, u32[]{:S(2)}) collective-permute-start(bf16[400,128]{1,0:T(8,128)(2,1)S(1)} %constant_dynamic-update-slice_fusion._.refs_2_.refs_7_), channel_id=1, source_target_pairs={{0,2},{1,3},{2,0},{3,1},{4,6},{5,7},{6,4},{7,5},{8,10},{9,11},{10,... | collective-permute-start | bytes 307208 | tf_op jit(solution)/shard_map/ppermute | solution.py:641
  32.9 8.4 %collective-permute-start.1 = (bf16[400,128]{1,0:T(8,128)(2,1)S(1)}, bf16[400,128]{1,0:T(8,128)(2,1)S(1)}, u32[]{:S(2)}, u32[]{:S(2)}) collective-permute-start(bf16[400,128]{1,0:T(8,128)(2,1)S(1)} %constant_dynamic-update-slice_fusion._.refs_2_.refs_7_), channel_id=1, source_target_pairs={{0,1},{1,0},{2,3},{3,2},{4,5},{5,4},{6,7},{7,6},{8,9},{9,8},{10,11... | collective-permute-start | bytes 307208 | tf_op jit(solution)/shard_map/ppermute | solution.py:641
  37.8 8.0 %collective-permute-start.7 = (bf16[80,128]{1,0:T(8,128)(2,1)S(1)}, bf16[80,128]{1,0:T(8,128)(2,1)S(1)}, u32[]{:S(2)}, u32[]{:S(2)}) collective-permute-start(bf16[80,128]{1,0:T(8,128)(2,1)S(1)} %get-tuple-element.28), channel_id=1, source_target_pairs={{0,1},{1,0},{2,3},{3,2},{4,5},{5,4},{6,7},{7,6},{8,9},{9,8},{10,11... | collective-permute-start | bytes 61448 | tf_op jit(solution)/shard_map/ppermute | solution.py:663
  39.3 8.7 %collective-permute-start.8 = (bf16[80,128]{1,0:T(8,128)(2,1)S(1)}, bf16[80,128]{1,0:T(8,128)(2,1)S(1)}, u32[]{:S(2)}, u32[]{:S(2)}) collective-permute-start(bf16[80,128]{1,0:T(8,128)(2,1)S(1)} %get-tuple-element.29), channel_id=1, source_target_pairs={{1,2},{2,1},{3,4},{4,3},{5,6},{6,5},{7,8},{8,7},{9,10},{10,9},{11,... | collective-permute-start | bytes 61448 | tf_op jit(solution)/shard_map/ppermute | solution.py:662
  42.7 9.4 %collective-permute-start.6 = (bf16[40,128]{1,0:T(8,128)(2,1)}, bf16[40,128]{1,0:T(8,128)(2,1)S(1)}, u32[]{:S(2)}, u32[]{:S(2)}) collective-permute-start(bf16[40,128]{1,0:T(8,128)(2,1)} %top.1.refs_6_.refs_1_), channel_id=1, source_target_pairs={{0,24},{8,16},{16,8},{24,0},{1,25},{9,17},{17,9},{25,1},{2,26},{10... | collective-permute-start | bytes 30728 | tf_op jit(solution)/shard_map/ppermute | solution.py:675
  44.2 7.9 %collective-permute-start.5 = (bf16[40,128]{1,0:T(8,128)(2,1)}, bf16[40,128]{1,0:T(8,128)(2,1)S(1)}, u32[]{:S(2)}, u32[]{:S(2)}) collective-permute-start(bf16[40,128]{1,0:T(8,128)(2,1)} %top.1.refs_6_.refs_1_), channel_id=1, source_target_pairs={{0,16},{8,24},{16,0},{24,8},{1,17},{9,25},{17,1},{25,9},{2,18},{10... | collective-permute-start | bytes 30728 | tf_op jit(solution)/shard_map/ppermute | solution.py:675
  45.8 6.2 %collective-permute-start.4 = (bf16[40,128]{1,0:T(8,128)(2,1)}, bf16[40,128]{1,0:T(8,128)(2,1)S(1)}, u32[]{:S(2)}, u32[]{:S(2)}) collective-permute-start(bf16[40,128]{1,0:T(8,128)(2,1)} %top.1.refs_6_.refs_1_), channel_id=1, source_target_pairs={{0,8},{8,0},{16,24},{24,16},{1,9},{9,1},{17,25},{25,17},{2,10},{10... | collective-permute-start | bytes 30728 | tf_op jit(solution)/shard_map/ppermute | solution.py:675

commit v7 on v6

--- a/solution.py
+++ b/solution.py
@@ -125,7 +125,7 @@
 
 def upward_kernel(
     send_ref, charges_ref, points_ref, basis_ref, proxy_ref, up_leaf_hbm, up_branch_ref, up_device_ref, pbranch_ref,
-    pdevice_ref, moment_ref, own_ref, out_ref, inner_ref, outer_ref, shared_ref, tile_ref, late_ref, up_leaf_ref,
+    pdevice_ref, pgroup_ref, moment_ref, own_ref, out_ref, inner_ref, outer_ref, shared_ref, tile_ref, late_ref, up_leaf_ref,
     scratch_ref, branch_ref, sem,
 ):
     slots, devices = send_ref.shape
@@ -150,6 +150,14 @@
         return carry
 
     lax.fori_loop(0, leaves // 2, leaf_pair, 0, unroll=8)
+    transfers.wait()
+    share = raise_moments(
+        moment_ref, up_leaf_ref, up_branch_ref, up_device_ref, pbranch_ref, pdevice_ref, shared_ref, scratch_ref, branch_ref
+    )
+    share = jnp.concatenate([share[: rhs // 2], share[rhs // 2 :]], axis=1)
+    gx, gy, gz = (-2.0 * pgroup_ref[c : c + 1, :].astype(F32) for c in range(3))
+    group_rows = [jnp.concatenate([gx, gy], axis=1), jnp.concatenate([gz, jnp.zeros_like(gz)], axis=1)]
+    group_rows = jnp.concatenate([jnp.zeros((ROWS - 2, rank2), F32)] + group_rows, axis=0)
     low8 = low_half((ROWS, rank2))
     base = slots // 2 * rhs
 
@@ -167,7 +175,8 @@
                     ref[pl.ds(pl.multiple_of(second * ROWS, ROWS), ROWS), :],
                 )
             )
-        out_ref[p, base:, :] = (tiles[0] + tiles[1]).astype(BF16)
+        out_ref[p, base : base + ROWS, :] = (tiles[0] + tiles[1] + group_rows).astype(BF16)
+        out_ref[p, base + ROWS :, :] = share
         return carry
 
     lax.fori_loop(0, devices, pack, 0, unroll=4)
@@ -183,10 +192,6 @@
             points = points_ref[:, columns].astype(F32)
             rows = jnp.concatenate([points, jnp.zeros((ROWS - 3, rank2), F32)], axis=0)
             ref[base + rhs : base + rhs + ROWS, :] = rows.astype(BF16)
-    transfers.wait()
-    raise_moments(
-        moment_ref, up_leaf_ref, up_branch_ref, up_device_ref, pbranch_ref, pdevice_ref, shared_ref, scratch_ref, branch_ref
-    )
 
 
 def relayout(x_ref, scratch_ref):
@@ -249,6 +254,7 @@
     out_ref[base : base + rhs, :] = jnp.concatenate([m_device, share], axis=1)
     rows = source_rows(*[twice(pdevice_ref[c : c + 1, :].astype(F32)) for c in range(3)])
     out_ref[base + rhs :, :] = stack_rows(rows).astype(BF16)
+    return share
 
 
 def turn_kernel(down_leaf_ref, far_ref, _, down_ref, turned_ref, scratch_ref):
@@ -377,34 +383,12 @@
     return parts[s // 2].at[s % 2 * length : (s % 2 + 1) * length], owner
 
 
-def top_kernel(*refs, members):
-    _, pgroup_ref, *parts, out_ref = refs
-    rhs = out_ref.shape[0] - ROWS
-    rank2 = out_ref.shape[1]
-    m_group = jnp.zeros((rhs, rank2), F32)
-    for s in range(members):
-        part, _ = part_of(parts, s, members)
-        base = part.shape[0] - rhs - ROWS
-        m_group = m_group + part[base : base + rhs, :].astype(F32)
-    out_ref[:rhs, :] = twice(m_group[:, rank2 // 2 :]).astype(BF16)
-    rows = source_rows(*[twice(pgroup_ref[c : c + 1, :].astype(F32)) for c in range(3)])
-    out_ref[rhs:, :] = stack_rows(rows).astype(BF16)
-
-
 def group_kernel(*refs, members):
-    far_ref, near_ref, charges_hbm, points_hbm, inner_ref, outer_ref, _ = refs[:7]
+    far_ref = refs[0]
     count = members // 2
-    parts = refs[7 : 7 + count]
-    fb_ref, ld_ref, edge_ref = refs[7 + count : 10 + count]
-    (
-        moment_ref, source_ref, dev_m_ref, dev_source_ref, ends_ref, end_points_ref, weight_ref, kern_ref, sems,
-    ) = refs[10 + count :]
-    total, width = charges_hbm.shape[1], ends_ref.shape[2]
-    copies = []
-    for side in range(2):
-        columns = slice(side * (total - width), side * (total - width) + width)
-        copies.append(fetch(charges_hbm.at[:, columns], ends_ref.at[side], sems.at[2 * side]))
-        copies.append(fetch(points_hbm.at[:, columns], end_points_ref.at[side], sems.at[2 * side + 1]))
+    parts = refs[1 : 1 + count]
+    fb_ref, ld_ref = refs[1 + count : 3 + count]
+    moment_ref, source_ref, dev_m_ref, dev_source_ref = refs[3 + count :]
     branches, entries = far_ref.shape
     rhs, rank2 = moment_ref.shape[1:]
     rank = rank2 // 2
@@ -427,18 +411,15 @@
         fb_ref[c] = interact(target, [far_ref[c, e] for e in range(entries)], source_ref, tail, moment_ref)
     target = target_of(dev_source_ref[me][:, :rank])
     ld_ref[...] = interact(target, list(range(members)), dev_source_ref, tail, dev_m_ref)
-    for copy in copies:
-        copy.wait()
-    edge_pairs(near_ref, ends_ref, end_points_ref, inner_ref, outer_ref, edge_ref, weight_ref, kern_ref)
 
 
 def downward_kernel(*refs, groups):
     far_ref = refs[0]
-    tiles = refs[1 : 1 + groups]
     (
-        fb_ref, ld_ref, down_device_ref, down_branch_ref, down_ref, own_ref, own_m_ref, recv_ref, basis_ref, near_ref, edge_ref,
-        out_ref, table_ref, grp_m_ref, grp_source_ref, branch_ref, parent_ref, *buffers,
-    ) = refs[1 + groups :]
+        fb_ref, ld_ref, down_device_ref, down_branch_ref, down_ref, own_ref, own_m_ref, recv_ref, basis_ref, near_ref,
+        list_ref, charges_hbm, points_hbm, inner_ref, outer_ref, out_ref, edge_ref, ends_ref, end_points_ref, weight_ref,
+        edge_kern_ref, sems, table_ref, grp_m_ref, grp_source_ref, branch_ref, parent_ref, *buffers,
+    ) = refs[1:]
     leaves, entries = far_ref.shape
     rhs, rank2 = parent_ref.shape[1:]
     rank = rank2 // 2
@@ -446,16 +427,33 @@
     branches = leaves // FAN
     devices = recv_ref.shape[0]
     slots = (table_ref.shape[0] - leaves) // devices
+    columns_all, width = charges_hbm.shape[1], ends_ref.shape[2]
+    copies = []
+    for side in range(2):
+        columns = slice(side * (columns_all - width), side * (columns_all - width) + width)
+        copies.append(fetch(charges_hbm.at[:, columns], ends_ref.at[side], sems.at[2 * side]))
+        copies.append(fetch(points_hbm.at[:, columns], end_points_ref.at[side], sems.at[2 * side + 1]))
     me = lax.axis_index("grp")
     low = low_half((rhs, rank2))
     tail = source_tail(rank2)
 
-    for s, tile_ref in enumerate(tiles):
-        owner = me ^ s
-        keep = (jnp.abs(owner - me) >= 2).astype(F32)
-        grp_m_ref[owner] = (tile_ref[:rhs, :].astype(F32) * keep).astype(BF16)
-        grp_source_ref[owner] = tile_ref[rhs:, :]
-    target = target_of(tiles[0][rhs:, :rank])
+    base = slots // 2 * rhs
+    members = devices // groups
+    low_g = low_half((ROWS, rank2))
+    for g in range(groups):
+        total = jnp.zeros((rhs // 2, rank2), F32)
+        for p in range(g * members, (g + 1) * members):
+            total = total + recv_ref[p, base + ROWS :, :].astype(F32)
+        total = jnp.concatenate([total[:, :rank], total[:, rank:]], axis=0).astype(BF16).astype(F32)
+        keep = (jnp.abs(g - me) >= 2).astype(F32)
+        grp_m_ref[g] = twice(total * keep).astype(BF16)
+        tile = recv_ref[g * members, base : base + ROWS, :].astype(F32)
+        other = pltpu.roll(tile, rank, 1)
+        left, right = pair(low_g, tile, other), pair(low_g, other, tile)
+        x, y, z = left[ROWS - 2 : ROWS - 1, :], right[ROWS - 2 : ROWS - 1, :], left[ROWS - 1 :, :]
+        rows = (x, y, z) + three(0.25 * (x * x + y * y + z * z))
+        grp_source_ref[g] = stack_rows(rows).astype(BF16)
+    target = target_of(grp_source_ref[me][:, :rank])
     l_group = interact(target, list(range(groups)), grp_source_ref, tail, grp_m_ref).astype(BF16)
     l_device = (ld_ref[...] + dot_t(l_group, down_device_ref[...])).astype(BF16)
     branch_ref[...] = twice(down_branch_ref[...].astype(F32).reshape(rank * branches, rank))
@@ -463,6 +461,10 @@
         matrix = branch_ref[pl.ds(c, rank, stride=branches), :][:, :rank].astype(BF16)
         parent_ref[c] = twice((fb_ref[c] + dot_t(l_device, matrix)).astype(BF16))
 
+    for copy in copies:
+        copy.wait()
+    edge_pairs(list_ref, ends_ref, end_points_ref, inner_ref, outer_ref, edge_ref, weight_ref, edge_kern_ref)
+
     table_ref[:leaves, :rhs, :] = own_m_ref[...]
     table_ref[:leaves, rhs:, :] = own_ref[...]
     base = slots // 2 * rhs
@@ -472,7 +474,7 @@
     zero = jnp.zeros((ROWS, rank2), F32)
 
     def unpack(p, carry):
-        tile = recv_ref[p, base:, :].astype(F32)
+        tile = recv_ref[p, base : base + ROWS, :].astype(F32)
         squares = 0.25 * tile * tile
         parts = three(squares + pltpu.roll(squares, ROWS - 1, 0) + pltpu.roll(squares, ROWS - 2, 0))
         for q in range(slots // 2):
@@ -592,12 +594,12 @@
         out_shape=(
             pltpu.VMEM((leaves, rhs, rank2), BF16),
             hbm((leaves, ROWS, rank2), BF16),
-            hbm((devices, slots // 2 * rhs + ROWS, rank2), BF16),
+            hbm((devices, slots // 2 * rhs + ROWS + rhs // 2, rank2), BF16),
             pltpu.VMEM((halo // rank2 * (rhs + ROWS), rank2), BF16),
             pltpu.VMEM((halo // rank2 * (rhs + ROWS), rank2), BF16),
             hbm(((branches // 2 + 1) * (rhs + ROWS), rank2), BF16),
         ),
-        in_specs=[SMEM()] + [VMEM()] * 4 + [ANY()] + [VMEM()] * 4,
+        in_specs=[SMEM()] + [VMEM()] * 4 + [ANY()] + [VMEM()] * 5,
         out_specs=(VMEM(),) * 6,
         scratch_shapes=[
             pltpu.VMEM((leaves * ROWS, rank2), F32),
@@ -620,6 +622,7 @@
         up_device[:, :, 0],
         jnp.transpose(proxy_branch, (0, 2, 1)),
         proxy_device[:, :, 0],
+        proxy_group[:, :, 0],
     )
     (moments,) = vmem(moments)
     received = lax.all_to_all(listed, ("grp", "dev"), split_axis=0, concat_axis=0, tiled=True)
@@ -627,7 +630,7 @@
     partner = lax.ppermute(shared, "dev", [(i, i ^ members // 2) for i in range(members)])
     down, far_turned = pl.pallas_call(
         turn_kernel,
-        out_shape=(pltpu.VMEM((leaves * half, rank2), BF16), hbm(far_leaf.shape[::-1], jnp.int32)),
+        out_shape=(hbm((leaves * half, rank2), BF16), hbm(far_leaf.shape[::-1], jnp.int32)),
         in_specs=[VMEM(), VMEM(), ANY()],
         out_specs=(VMEM(), VMEM()),
         scratch_shapes=[pltpu.VMEM((leaves * half, rank2), F32)],
@@ -663,43 +666,35 @@
     inner = lax.ppermute(inner, "dev", [(i, i ^ 1) for i in range(members)])
 
     parts = vmem(*parts)
-    tile = pl.pallas_call(
-        functools.partial(top_kernel, members=members),
-        out_shape=hbm((rhs + ROWS, rank2), BF16),
-        in_specs=[VMEM()] * (2 + len(parts)),
-        out_specs=VMEM(),
-        compiler_params=PARAMS,
-        name="top",
-    )(*vmem(near), proxy_group[:, :, 0], *parts)
-    assert groups & (groups - 1) == 0 and members & (members - 1) == 0
-    tiles = [tile] + [lax.ppermute(tile, "grp", [(i, i ^ s) for i in range(groups)]) for s in range(1, groups)]
-    far_b, part_d, edge = pl.pallas_call(
+    assert members & (members - 1) == 0
+    far_b, part_d = pl.pallas_call(
         functools.partial(group_kernel, members=members),
-        out_shape=(hbm((branches, rhs, rank), F32), hbm((rhs, rank), F32), pltpu.VMEM((rhs, 2 * halo), F32)),
-        in_specs=[SMEM(), VMEM(), ANY(), ANY(), VMEM(), VMEM(), ANY()] + [VMEM()] * len(parts),
-        out_specs=(VMEM(),) * 3,
+        out_shape=(hbm((branches, rhs, rank), F32), hbm((rhs, rank), F32)),
+        in_specs=[SMEM()] + [VMEM()] * len(parts),
+        out_specs=(VMEM(),) * 2,
         scratch_shapes=[
             pltpu.VMEM((members * branches, rhs, rank2), BF16),
             pltpu.VMEM((members * branches, ROWS, rank2), BF16),
             pltpu.VMEM((members, rhs, rank2), BF16),
             pltpu.VMEM((members, ROWS, rank2), BF16),
+        ],
+        compiler_params=PARAMS,
+        name="group",
+    )(jnp.transpose(far_branch), *parts)
+
+    table = leaves + devices * slots
+    return pl.pallas_call(
+        functools.partial(downward_kernel, groups=groups),
+        out_shape=hbm((rhs, total), F32),
+        in_specs=[SMEM()] + [VMEM()] * 11 + [ANY(), ANY(), VMEM(), VMEM()],
+        out_specs=VMEM(),
+        scratch_shapes=[
+            pltpu.VMEM((rhs, 2 * halo), F32),
             pltpu.VMEM((2, rhs, 2 * halo), BF16),
             pltpu.VMEM((2, 3, 2 * halo), BF16),
             pltpu.VMEM((2, leaves, reach), F32),
             pltpu.VMEM((REACH, 2 * size, reach), BF16),
             pltpu.SemaphoreType.DMA((4,)),
-        ],
-        compiler_params=PARAMS,
-        name="group",
-    )(jnp.transpose(far_branch), near_leaf, charges, points, *vmem(inner, outer), tile, *parts)
-
-    table = leaves + devices * slots
-    return pl.pallas_call(
-        functools.partial(downward_kernel, groups=groups),
-        out_shape=hbm((rhs, total), F32),
-        in_specs=[SMEM()] + [VMEM()] * (groups + 11),
-        out_specs=VMEM(),
-        scratch_shapes=[
             pltpu.VMEM((table, rhs + ROWS, rank2), BF16),
             pltpu.VMEM((groups, rhs, rank2), BF16),
             pltpu.VMEM((groups, ROWS, rank2), BF16),
@@ -717,18 +712,20 @@
         name="downward",
     )(
         far_turned,
-        tile,
-        *vmem(*tiles[1:]),
         far_b,
         part_d,
         down_device[:, :, 0],
         jnp.transpose(down_branch, (0, 2, 1)),
-        *vmem(down),
+        down,
         own,
         moments,
         *vmem(received),
         basis,
-        *vmem(near, edge),
+        *vmem(near),
+        near_leaf,
+        charges,
+        points,
+        *vmem(inner, outer),
     )
 
 

time: 62.1 us -> 62.6 us (level)
  waiting for transfers between devices: 15.6 us -> 20.1 us
  starting transfers between devices: 18.7 us -> 15.6 us
  Pallas kernels: 27.1 us -> 26.4 us
    ppermute x3 -> x0, starting transfers between devices: 3.15 us -> none  [on_device(): lax.ppermute(tile, 'grp', [(i, i ^ s) for i in range(groups)])]
    ppermute x1, waiting for transfers between devices: 13.4 us -> 15.7 us  [on_device(): lax.ppermute(shared, 'dev', [(i, i ^ members // 2) for i in range(members)])]
    ppermute x1, waiting for transfers between devices: 2.22 us -> 4.36 us  [on_device(): outer = lax.ppermute(outer, ('grp', 'dev'), swaps)]
    pallas_call x1, Pallas kernels: 3.98 us -> 2.37 us  [on_device(): pl.pallas_call(functools.partial(group_kernel, members=members), out_shap...]
    pallas_call x1, Pallas kernels: 9.57 us -> 11.1 us  [on_device(): pl.pallas_call(functools.partial(downward_kernel, groups=groups), out_sha...]
    pallas_call x2 -> x1, Pallas kernels: 3.83 us -> 2.9 us  [on_device(): pl.pallas_call(turn_kernel, out_shape=(hbm((leaves * half, rank2), BF16),...]
  transfers between devices with their start and end apart: 10 -> 7, of which waited for: 2 -> 2; matrix products, arithmetic and copies ran while one was open for 0% -> 0% of each run, Pallas kernels for 20% -> 15%
where the time goes in v7:
time: 62.6 us; the launch traced here: 62.2 us
  Pallas kernels  26.4 us (42%)
  waiting for transfers between devices  20.1 us (32%)
  starting transfers between devices  15.6 us (25%)
    ppermute x1, waiting for transfers between devices, on_device(): lax.ppermute(shared, 'dev', [(i, i ^ members // 2) for i in range(members)])  15.7 us
    pallas_call x1, Pallas kernels, on_device(): pl.pallas_call(functools.partial(downward_kernel, groups=groups), out_sha...  11.1 us
    all_to_all x1, starting transfers between devices, on_device(): lax.all_to_all(listed, ('grp', 'dev'), split_axis=0, concat_axis=0, tiled...  6.13 us
    pallas_call x1, Pallas kernels, on_device(): pl.pallas_call(upward_kernel, out_shape=(pltpu.VMEM((leaves, rhs, rank2),...  5.71 us
    ppermute x1, waiting for transfers between devices, on_device(): outer = lax.ppermute(outer, ('grp', 'dev'), swaps)  4.36 us
    pallas_call x1, Pallas kernels, on_device(): pl.pallas_call(near_kernel, out_shape=pltpu.VMEM((rhs, total), F32), in_s...  4.35 us
    ppermute x3, starting transfers between devices, on_device(): lax.ppermute(both, 'dev', [(i, i ^ s) for i in range(members)])  3.55 us
    pallas_call x1, Pallas kernels, on_device(): pl.pallas_call(turn_kernel, out_shape=(hbm((leaves * half, rank2), BF16),...  2.9 us
  transfers between devices with their start and end apart: 7, of which 2 were waited for; matrix products, arithmetic and copies ran while one was open for 0% of the time, Pallas kernels for 15%

profile of v7, /device:TPU:2, one launch (start us, length us, event | category | flops | bytes accessed | tf_op | source)
XLA Modules:
  0.0 62.2 jit_solution(14088143083386019267)
XLA Ops:
  0.0 5.7 %upward.1 = (bf16[64,32,128]{2,1,0:T(8,128)(2,1)S(1)}, bf16[64,8,128]{2,1,0:T(8,128)(2,1)}, bf16[32,88,128]{2,1,0:T(8,128)(2,1)}, bf16[80,128]{1,0:T(8,128)(2,1)...) custom-call(s32[4,32]{1,0:T(4,128)} %send_ref.1, bf16[32,4096]{1,0:T(8,128)(2,1)} %refs_12_.1, ...), custom_call_target="tpu_custom_call" | custom-call | tf_op jit(solution)/shard_map/upward/pallas_call | solution.py:592
  5.7 0.0 copy-start
  5.7 6.1 %all-to-all-start = ((bf16[32,88,128]{2,1,0:T(8,128)(2,1)}), bf16[32,88,128]{2,1,0:T(8,128)(2,1)S(1)}, u32[]{:S(2)}, u32[]{:S(2)}) async-start(bf16[32,88,128]{2,1,0:T(8,128)(2,1)} %get-tuple-element.29), calls=%async_computation | async-start | bytes 1441792 | tf_op jit(solution)/shard_map/all_to_all | solution.py:628
  11.9 0.0 copy-done
  11.9 2.4 %collective-permute-start = (bf16[200,128]{1,0:T(8,128)(2,1)S(1)}, bf16[200,128]{1,0:T(8,128)(2,1)S(1)}, u32[]{:S(2)}, u32[]{:S(2)}) collective-permute-start(bf16[200,128]{1,0:T(8,128)(2,1)S(1)} %copy-done), channel_id=1, source_target_pairs={{0,4},{1,5},{2,6},{3,7},{4,0},{5,1},{6,2},{7,3},{8,12},{9,13},{10,... | collective-permute-start | bytes 153608 | tf_op jit(solution)/shard_map/ppermute | solution.py:630
  14.3 2.9 %turn.1 = (bf16[2048,128]{1,0:T(8,128)(2,1)}, s32[64,16]{1,0:T(8,128)}) custom-call(bf16[64,64,64]{2,1,0:T(8,128)(2,1)} %down_leaf_ref.1, s32[16,64]{1,0:T(8,128)} %far_ref.1, bf16[200,128]{1,0:T(8,128)(2,1)} %get-tuple-element.20._), custom_call_target="tpu_custom_call" | custom-call | tf_op jit(solution)/shard_map/turn/pallas_call | solution.py:631
  17.2 15.7 %collective-permute-done = bf16[200,128]{1,0:T(8,128)(2,1)S(1)} collective-permute-done((bf16[200,128]{1,0:T(8,128)(2,1)S(1)}, bf16[200,128]{1,0:T(8,128)(2,1)S(1)}, u32[]{:S(2)}, u32[]{:S(2)}) %collective-permute-start) | collective-permute-done | bytes 51232 | tf_op jit(solution)/shard_map/ppermute | solution.py:630
  33.0 0.1 collective-permute-start.3
  33.0 2.9 %collective-permute-start.2 = (bf16[400,128]{1,0:T(8,128)(2,1)S(1)}, bf16[400,128]{1,0:T(8,128)(2,1)S(1)}, u32[]{:S(2)}, u32[]{:S(2)}) collective-permute-start(bf16[400,128]{1,0:T(8,128)(2,1)S(1)} %constant_dynamic-update-slice_fusion.refs_1_._), channel_id=1, source_target_pairs={{0,2},{1,3},{2,0},{3,1},{4,6},{5,7},{6,4},{7,5},{8,10},{9,11},{10,... | collective-permute-start | bytes 307208 | tf_op jit(solution)/shard_map/ppermute | solution.py:644
  36.0 0.5 collective-permute-start.1
  36.5 4.3 %near.1.refs_10_ = f32[32,4096]{1,0:T(8,128)S(1)} custom-call(s32[16,64]{1,0:T(8,128)} %refs_11_.1, bf16[32,4096]{1,0:T(8,128)(2,1)} %refs_12_.1, bf16[3,4096]{1,0:T(4,128)(2,1)} %refs_13_.1, bf16[400,128]{1,0:T(8,128)(2,1)S(1)} %constant_dynamic-update-slice_fusion.refs_1_._), custom_call_target="tpu_custom_call" | custom-call | tf_op jit(solution)/shard_map/near/pallas_call | solution.py:647
  40.9 1.6 %collective-permute-start.4 = (bf16[80,128]{1,0:T(8,128)(2,1)S(1)}, bf16[80,128]{1,0:T(8,128)(2,1)S(1)}, u32[]{:S(2)}, u32[]{:S(2)}) collective-permute-start(bf16[80,128]{1,0:T(8,128)(2,1)S(1)} %get-tuple-element.33), channel_id=1, source_target_pairs={{0,1},{1,0},{2,3},{3,2},{4,5},{5,4},{6,7},{7,6},{8,9},{9,8},{10,11... | collective-permute-start | bytes 61448 | tf_op jit(solution)/shard_map/ppermute | solution.py:666
  42.4 1.9 %collective-permute-start.5 = (bf16[80,128]{1,0:T(8,128)(2,1)S(1)}, bf16[80,128]{1,0:T(8,128)(2,1)S(1)}, u32[]{:S(2)}, u32[]{:S(2)}) collective-permute-start(bf16[80,128]{1,0:T(8,128)(2,1)S(1)} %get-tuple-element.34), channel_id=1, source_target_pairs={{1,2},{2,1},{3,4},{4,3},{5,6},{6,5},{7,8},{8,7},{9,10},{10,9},{11,... | collective-permute-start | bytes 61448 | tf_op jit(solution)/shard_map/ppermute | solution.py:665
  44.3 0.0 collective-permute-done.3.refs_4_
  44.4 0.0 collective-permute-done.2.refs_3_
  44.4 0.0 collective-permute-done.1.refs_2_
  44.4 2.4 %group.1 = (f32[8,32,64]{2,1,0:T(8,128)}, f32[32,64]{1,0:T(8,128)}) custom-call(s32[8,16]{1,0:T(8,128)} %bitcast.13, bf16[400,128]{1,0:T(8,128)(2,1)S(1)} %constant_dynamic-update-slice_fusion.refs_1_._, bf16[400,128]{1,0:T(8,128)(2,1)S(1)} %collective-permute-done.1.refs_2_, bf16[400,128]{1,0:T(8,128)(2,1)S(1)} %collective-permute-done.2.refs_3_, ...), custom_call_target="tpu_custom_call" | custom-call | tf_op jit(solution)/shard_map/group/pallas_call | solution.py:670
  46.7 0.0 collective-permute-done.4.refs_14_
  46.7 4.4 %collective-permute-done.5.refs_15_ = bf16[80,128]{1,0:T(8,128)(2,1)S(1)} collective-permute-done((bf16[80,128]{1,0:T(8,128)(2,1)S(1)}, bf16[80,128]{1,0:T(8,128)(2,1)S(1)}, u32[]{:S(2)}, u32[]{:S(2)}) %collective-permute-start.5) | collective-permute-done | bytes 20512 | tf_op jit(solution)/shard_map/ppermute | solution.py:665
  51.1 0.0 all-to-all-done.refs_8_
  51.1 11.1 %downward.1 = f32[32,4096]{1,0:T(8,128)} custom-call(s32[64,16]{1,0:T(8,128)} %get-tuple-element.21.refs_0_, f32[8,32,64]{2,1,0:T(8,128)} %get-tuple-element.24.refs_1_, f32[32,64]{1,0:T(8,128)} %get-tuple-element.25.refs_2_, bf16[64,64]{1,0:T(8,128)(2,1)} %bitcast.11, bf16[64,8,64]{2,1,0:T(8,128)(2,1)} %bitcast.9, ...), custom_call_target="tpu_custom_call" | custom-call | tf_op jit(solution)/shard_map/downward/pallas_call | solution.py:686
  (2 shorter events, 0.0 us)
Async XLA Ops:
  5.7 6.2 %copy-start = (bf16[200,128]{1,0:T(8,128)(2,1)S(1)}, bf16[200,128]{1,0:T(8,128)(2,1)}, u32[]{:S(2)}) copy-start(bf16[200,128]{1,0:T(8,128)(2,1)} %get-tuple-element.20._) | copy-start | bytes 153604
  5.7 45.4 %all-to-all-start = ((bf16[32,88,128]{2,1,0:T(8,128)(2,1)}), bf16[32,88,128]{2,1,0:T(8,128)(2,1)S(1)}, u32[]{:S(2)}, u32[]{:S(2)}) async-start(bf16[32,88,128]{2,1,0:T(8,128)(2,1)} %get-tuple-element.29), calls=%async_computation | async-start | bytes 1441792 | tf_op jit(solution)/shard_map/all_to_all | solution.py:628
  11.9 21.1 %collective-permute-start = (bf16[200,128]{1,0:T(8,128)(2,1)S(1)}, bf16[200,128]{1,0:T(8,128)(2,1)S(1)}, u32[]{:S(2)}, u32[]{:S(2)}) collective-permute-start(bf16[200,128]{1,0:T(8,128)(2,1)S(1)} %copy-done), channel_id=1, source_target_pairs={{0,4},{1,5},{2,6},{3,7},{4,0},{5,1},{6,2},{7,3},{8,12},{9,13},{10,... | collective-permute-start | bytes 153608 | tf_op jit(solution)/shard_map/ppermute | solution.py:630
  33.0 11.4 %collective-permute-start.3 = (bf16[400,128]{1,0:T(8,128)(2,1)S(1)}, bf16[400,128]{1,0:T(8,128)(2,1)S(1)}, u32[]{:S(2)}, u32[]{:S(2)}) collective-permute-start(bf16[400,128]{1,0:T(8,128)(2,1)S(1)} %constant_dynamic-update-slice_fusion.refs_1_._), channel_id=1, source_target_pairs={{0,3},{1,2},{2,1},{3,0},{4,7},{5,6},{6,5},{7,4},{8,11},{9,10},{10,... | collective-permute-start | bytes 307208 | tf_op jit(solution)/shard_map/ppermute | solution.py:644
  33.0 11.3 %collective-permute-start.2 = (bf16[400,128]{1,0:T(8,128)(2,1)S(1)}, bf16[400,128]{1,0:T(8,128)(2,1)S(1)}, u32[]{:S(2)}, u32[]{:S(2)}) collective-permute-start(bf16[400,128]{1,0:T(8,128)(2,1)S(1)} %constant_dynamic-update-slice_fusion.refs_1_._), channel_id=1, source_target_pairs={{0,2},{1,3},{2,0},{3,1},{4,6},{5,7},{6,4},{7,5},{8,10},{9,11},{10,... | collective-permute-start | bytes 307208 | tf_op jit(solution)/shard_map/ppermute | solution.py:644
  36.0 8.4 %collective-permute-start.1 = (bf16[400,128]{1,0:T(8,128)(2,1)S(1)}, bf16[400,128]{1,0:T(8,128)(2,1)S(1)}, u32[]{:S(2)}, u32[]{:S(2)}) collective-permute-start(bf16[400,128]{1,0:T(8,128)(2,1)S(1)} %constant_dynamic-update-slice_fusion.refs_1_._), channel_id=1, source_target_pairs={{0,1},{1,0},{2,3},{3,2},{4,5},{5,4},{6,7},{7,6},{8,9},{9,8},{10,11... | collective-permute-start | bytes 307208 | tf_op jit(solution)/shard_map/ppermute | solution.py:644
  40.9 5.9 %collective-permute-start.4 = (bf16[80,128]{1,0:T(8,128)(2,1)S(1)}, bf16[80,128]{1,0:T(8,128)(2,1)S(1)}, u32[]{:S(2)}, u32[]{:S(2)}) collective-permute-start(bf16[80,128]{1,0:T(8,128)(2,1)S(1)} %get-tuple-element.33), channel_id=1, source_target_pairs={{0,1},{1,0},{2,3},{3,2},{4,5},{5,4},{6,7},{7,6},{8,9},{9,8},{10,11... | collective-permute-start | bytes 61448 | tf_op jit(solution)/shard_map/ppermute | solution.py:666
  42.4 8.7 %collective-permute-start.5 = (bf16[80,128]{1,0:T(8,128)(2,1)S(1)}, bf16[80,128]{1,0:T(8,128)(2,1)S(1)}, u32[]{:S(2)}, u32[]{:S(2)}) collective-permute-start(bf16[80,128]{1,0:T(8,128)(2,1)S(1)} %get-tuple-element.34), channel_id=1, source_target_pairs={{1,2},{2,1},{3,4},{4,3},{5,6},{6,5},{7,8},{8,7},{9,10},{10,9},{11,... | collective-permute-start | bytes 61448 | tf_op jit(solution)/shard_map/ppermute | solution.py:665

commit v8 on v7

--- a/solution.py
+++ b/solution.py
@@ -290,7 +290,7 @@
 
 
 def near_kernel(
-    near_ref, charges_ref, points_ref, _, out_ref, source_ref, target_ref, weight_ref, kern_a_ref, kern_b_ref
+    near_ref, charges_ref, points_ref, _, out_ref, edge_ref, source_ref, target_ref, weight_ref, kern_a_ref, kern_b_ref
 ):
     rhs, total = charges_ref.shape
     size = total // near_ref.shape[1]
@@ -301,6 +301,8 @@
     source_ref[...] = jnp.concatenate([rows.astype(BF16), source_tail(total)], axis=0)
     target_ref[...] = target_of(rows)
     near_weights(near_ref, size, weight_ref)
+    edge_ref[:, :REACH, :] = weight_ref[:, :REACH, :]
+    edge_ref[:, REACH:, :] = weight_ref[:, weight_ref.shape[1] - REACH :, :]
     out_ref[:, :halo] = jnp.zeros((rhs, halo), F32)
     out_ref[:, total - halo :] = jnp.zeros((rhs, halo), F32)
     width = kern_a_ref.shape[0]
@@ -337,16 +339,13 @@
     lax.fori_loop(0, rounds // 2, step, 0)
 
 
-def edge_pairs(near_ref, ends_ref, end_points_ref, inner_ref, outer_ref, out_ref, weight_ref, kern_ref):
+def edge_pairs(ends_ref, end_points_ref, inner_ref, outer_ref, out_ref, weight_ref, kern_ref):
     rhs = ends_ref.shape[1]
-    leaves = near_ref.shape[1]
     halo = out_ref.shape[1] // 2
     lanes = inner_ref.shape[1]
-    size = lanes // 2
     count = halo // lanes
     reach = weight_ref.shape[2]
     odd = lax.rem(lax.axis_index("dev"), 2) == 1
-    near_weights(near_ref, size, weight_ref)
     inner, outer = inner_ref[...], outer_ref[...]
     height = inner.shape[0] // count
     for side, block in enumerate((jnp.where(odd, inner, outer), jnp.where(odd, outer, inner))):
@@ -358,7 +357,7 @@
         source = jnp.concatenate([rows.astype(BF16), source_tail(rows.shape[1])], axis=0)
         target = target_of(rows[:, halo : 2 * halo])
         for j in range(count):
-            leaf = 2 * j + side * (leaves - 2 * count)
+            leaf = 2 * j + side * 2 * count
             place = side * count + j
             near_couplings(
                 target[:, j * lanes : (j + 1) * lanes],
@@ -417,7 +416,7 @@
     far_ref = refs[0]
     (
         fb_ref, ld_ref, down_device_ref, down_branch_ref, down_ref, own_ref, own_m_ref, recv_ref, basis_ref, near_ref,
-        list_ref, charges_hbm, points_hbm, inner_ref, outer_ref, out_ref, edge_ref, ends_ref, end_points_ref, weight_ref,
+        weight_ref, charges_hbm, points_hbm, inner_ref, outer_ref, out_ref, edge_ref, ends_ref, end_points_ref,
         edge_kern_ref, sems, table_ref, grp_m_ref, grp_source_ref, branch_ref, parent_ref, *buffers,
     ) = refs[1:]
     leaves, entries = far_ref.shape
@@ -436,6 +435,11 @@
     me = lax.axis_index("grp")
     low = low_half((rhs, rank2))
     tail = source_tail(rank2)
+
+    own_copies = [
+        fetch(own_m_ref, table_ref.at[:leaves, :rhs, :], sems.at[4]),
+        fetch(own_ref, table_ref.at[:leaves, rhs:, :], sems.at[5]),
+    ]
 
     base = slots // 2 * rhs
     members = devices // groups
@@ -463,10 +467,8 @@
 
     for copy in copies:
         copy.wait()
-    edge_pairs(list_ref, ends_ref, end_points_ref, inner_ref, outer_ref, edge_ref, weight_ref, edge_kern_ref)
-
-    table_ref[:leaves, :rhs, :] = own_m_ref[...]
-    table_ref[:leaves, rhs:, :] = own_ref[...]
+    edge_pairs(ends_ref, end_points_ref, inner_ref, outer_ref, edge_ref, weight_ref, edge_kern_ref)
+
     base = slots // 2 * rhs
 
     row = lax.broadcasted_iota(jnp.int32, (ROWS, rank2), 0)
@@ -490,6 +492,8 @@
         return carry
 
     lax.fori_loop(0, devices, unpack, 0, unroll=min(devices, 32))
+    for copy in own_copies:
+        copy.wait()
     low_d = low_half((half, rank2))
 
     width = buffers[0].shape[0]
@@ -644,11 +648,11 @@
         parts.append(lax.ppermute(both, "dev", [(i, i ^ s) for i in range(members)]))
 
     reach = (2 * REACH + 2) * size
-    near = pl.pallas_call(
+    near, edge_weights = pl.pallas_call(
         near_kernel,
-        out_shape=pltpu.VMEM((rhs, total), F32),
+        out_shape=(pltpu.VMEM((rhs, total), F32), hbm((2, 2 * REACH, reach), F32)),
         in_specs=[VMEM()] * 4,
-        out_specs=VMEM(),
+        out_specs=(VMEM(), VMEM()),
         scratch_shapes=[
             pltpu.VMEM((2 * ROWS, total), BF16),
             pltpu.VMEM((2 * ROWS, total), BF16),
@@ -692,9 +696,8 @@
             pltpu.VMEM((rhs, 2 * halo), F32),
             pltpu.VMEM((2, rhs, 2 * halo), BF16),
             pltpu.VMEM((2, 3, 2 * halo), BF16),
-            pltpu.VMEM((2, leaves, reach), F32),
             pltpu.VMEM((REACH, 2 * size, reach), BF16),
-            pltpu.SemaphoreType.DMA((4,)),
+            pltpu.SemaphoreType.DMA((6,)),
             pltpu.VMEM((table, rhs + ROWS, rank2), BF16),
             pltpu.VMEM((groups, rhs, rank2), BF16),
             pltpu.VMEM((groups, ROWS, rank2), BF16),
@@ -722,7 +725,7 @@
         *vmem(received),
         basis,
         *vmem(near),
-        near_leaf,
+        edge_weights,
         charges,
         points,
         *vmem(inner, outer),

time: 62.6 us -> 62.8 us (level)
  transfers between devices with their start and end apart: 7 -> 7, of which waited for: 2 -> 2; matrix products, arithmetic and copies ran while one was open for 0% -> 0% of each run, Pallas kernels for 15% -> 16%
where the time goes in v8:
time: 62.8 us; the launch traced here: 62.5 us
  Pallas kernels  26.8 us (43%)
  waiting for transfers between devices  20.1 us (32%)
  starting transfers between devices  15.5 us (25%)
    ppermute x1, waiting for transfers between devices, on_device(): lax.ppermute(shared, 'dev', [(i, i ^ members // 2) for i in range(members)])  15.7 us
    pallas_call x1, Pallas kernels, on_device(): pl.pallas_call(functools.partial(downward_kernel, groups=groups), out_sha...  10.9 us
    all_to_all x1, starting transfers between devices, on_device(): lax.all_to_all(listed, ('grp', 'dev'), split_axis=0, concat_axis=0, tiled...  6.13 us
    pallas_call x1, Pallas kernels, on_device(): pl.pallas_call(upward_kernel, out_shape=(pltpu.VMEM((leaves, rhs, rank2),...  5.73 us
    pallas_call x1, Pallas kernels, on_device(): pl.pallas_call(near_kernel, out_shape=(pltpu.VMEM((rhs, total), F32), hbm...  4.83 us
    ppermute x1, waiting for transfers between devices, on_device(): outer = lax.ppermute(outer, ('grp', 'dev'), swaps)  4.36 us
    ppermute x3, starting transfers between devices, on_device(): lax.ppermute(both, 'dev', [(i, i ^ s) for i in range(members)])  3.55 us
    pallas_call x1, Pallas kernels, on_device(): pl.pallas_call(turn_kernel, out_shape=(hbm((leaves * half, rank2), BF16),...  2.92 us
  transfers between devices with their start and end apart: 7, of which 2 were waited for; matrix products, arithmetic and copies ran while one was open for 0% of the time, Pallas kernels for 16%

profile of v8, /device:TPU:2, one launch (start us, length us, event | category | flops | bytes accessed | tf_op | source)
XLA Modules:
  0.0 62.5 jit_solution(8743543091302692157)
XLA Ops:
  0.0 5.7 %upward.1 = (bf16[64,32,128]{2,1,0:T(8,128)(2,1)S(1)}, bf16[64,8,128]{2,1,0:T(8,128)(2,1)}, bf16[32,88,128]{2,1,0:T(8,128)(2,1)}, bf16[80,128]{1,0:T(8,128)(2,1)...) custom-call(s32[4,32]{1,0:T(4,128)} %send_ref.1, bf16[32,4096]{1,0:T(8,128)(2,1)} %refs_12_.1, ...), custom_call_target="tpu_custom_call" | custom-call | tf_op jit(solution)/shard_map/upward/pallas_call | solution.py:596
  5.7 0.0 copy-start
  5.7 6.1 %all-to-all-start = ((bf16[32,88,128]{2,1,0:T(8,128)(2,1)}), bf16[32,88,128]{2,1,0:T(8,128)(2,1)S(1)}, u32[]{:S(2)}, u32[]{:S(2)}) async-start(bf16[32,88,128]{2,1,0:T(8,128)(2,1)} %get-tuple-element.31), calls=%async_computation | async-start | bytes 1441792 | tf_op jit(solution)/shard_map/all_to_all | solution.py:632
  11.9 0.0 copy-done
  11.9 2.4 %collective-permute-start = (bf16[200,128]{1,0:T(8,128)(2,1)S(1)}, bf16[200,128]{1,0:T(8,128)(2,1)S(1)}, u32[]{:S(2)}, u32[]{:S(2)}) collective-permute-start(bf16[200,128]{1,0:T(8,128)(2,1)S(1)} %copy-done), channel_id=1, source_target_pairs={{0,4},{1,5},{2,6},{3,7},{4,0},{5,1},{6,2},{7,3},{8,12},{9,13},{10,... | collective-permute-start | bytes 153608 | tf_op jit(solution)/shard_map/ppermute | solution.py:634
  14.3 2.9 %turn.1 = (bf16[2048,128]{1,0:T(8,128)(2,1)}, s32[64,16]{1,0:T(8,128)}) custom-call(bf16[64,64,64]{2,1,0:T(8,128)(2,1)} %down_leaf_ref.1, s32[16,64]{1,0:T(8,128)} %far_ref.1, bf16[200,128]{1,0:T(8,128)(2,1)} %get-tuple-element.22._), custom_call_target="tpu_custom_call" | custom-call | tf_op jit(solution)/shard_map/turn/pallas_call | solution.py:635
  17.3 15.7 %collective-permute-done = bf16[200,128]{1,0:T(8,128)(2,1)S(1)} collective-permute-done((bf16[200,128]{1,0:T(8,128)(2,1)S(1)}, bf16[200,128]{1,0:T(8,128)(2,1)S(1)}, u32[]{:S(2)}, u32[]{:S(2)}) %collective-permute-start) | collective-permute-done | bytes 51232 | tf_op jit(solution)/shard_map/ppermute | solution.py:634
  33.0 0.1 collective-permute-start.3
  33.1 2.9 %collective-permute-start.2 = (bf16[400,128]{1,0:T(8,128)(2,1)S(1)}, bf16[400,128]{1,0:T(8,128)(2,1)S(1)}, u32[]{:S(2)}, u32[]{:S(2)}) collective-permute-start(bf16[400,128]{1,0:T(8,128)(2,1)S(1)} %constant_dynamic-update-slice_fusion.refs_1_._), channel_id=1, source_target_pairs={{0,2},{1,3},{2,0},{3,1},{4,6},{5,7},{6,4},{7,5},{8,10},{9,11},{10,... | collective-permute-start | bytes 307208 | tf_op jit(solution)/shard_map/ppermute | solution.py:648
  36.0 0.5 collective-permute-start.1
  36.5 4.8 %near.1 = (f32[32,4096]{1,0:T(8,128)S(1)}, f32[2,8,640]{2,1,0:T(8,128)}) custom-call(s32[16,64]{1,0:T(8,128)} %near_ref.1, bf16[32,4096]{1,0:T(8,128)(2,1)} %refs_12_.1, bf16[3,4096]{1,0:T(4,128)(2,1)} %refs_13_.1, bf16[400,128]{1,0:T(8,128)(2,1)S(1)} %constant_dynamic-update-slice_fusion.refs_1_._), custom_call_target="tpu_custom_call" | custom-call | tf_op jit(solution)/shard_map/near/pallas_call | solution.py:651
  41.4 1.5 %collective-permute-start.4 = (bf16[80,128]{1,0:T(8,128)(2,1)S(1)}, bf16[80,128]{1,0:T(8,128)(2,1)S(1)}, u32[]{:S(2)}, u32[]{:S(2)}) collective-permute-start(bf16[80,128]{1,0:T(8,128)(2,1)S(1)} %get-tuple-element.37), channel_id=1, source_target_pairs={{0,1},{1,0},{2,3},{3,2},{4,5},{5,4},{6,7},{7,6},{8,9},{9,8},{10,11... | collective-permute-start | bytes 61448 | tf_op jit(solution)/shard_map/ppermute | solution.py:670
  42.9 1.9 %collective-permute-start.5 = (bf16[80,128]{1,0:T(8,128)(2,1)S(1)}, bf16[80,128]{1,0:T(8,128)(2,1)S(1)}, u32[]{:S(2)}, u32[]{:S(2)}) collective-permute-start(bf16[80,128]{1,0:T(8,128)(2,1)S(1)} %get-tuple-element.38), channel_id=1, source_target_pairs={{1,2},{2,1},{3,4},{4,3},{5,6},{6,5},{7,8},{8,7},{9,10},{10,9},{11,... | collective-permute-start | bytes 61448 | tf_op jit(solution)/shard_map/ppermute | solution.py:669
  44.8 0.0 collective-permute-done.3.refs_4_
  44.8 0.0 collective-permute-done.2.refs_3_
  44.8 0.0 collective-permute-done.1.refs_2_
  44.8 2.4 %group.1 = (f32[8,32,64]{2,1,0:T(8,128)}, f32[32,64]{1,0:T(8,128)}) custom-call(s32[8,16]{1,0:T(8,128)} %bitcast.13, bf16[400,128]{1,0:T(8,128)(2,1)S(1)} %constant_dynamic-update-slice_fusion.refs_1_._, bf16[400,128]{1,0:T(8,128)(2,1)S(1)} %collective-permute-done.1.refs_2_, bf16[400,128]{1,0:T(8,128)(2,1)S(1)} %collective-permute-done.2.refs_3_, ...), custom_call_target="tpu_custom_call" | custom-call | tf_op jit(solution)/shard_map/group/pallas_call | solution.py:674
  47.2 0.0 collective-permute-done.4.refs_14_
  47.2 4.4 %collective-permute-done.5.refs_15_ = bf16[80,128]{1,0:T(8,128)(2,1)S(1)} collective-permute-done((bf16[80,128]{1,0:T(8,128)(2,1)S(1)}, bf16[80,128]{1,0:T(8,128)(2,1)S(1)}, u32[]{:S(2)}, u32[]{:S(2)}) %collective-permute-start.5) | collective-permute-done | bytes 20512 | tf_op jit(solution)/shard_map/ppermute | solution.py:669
  51.5 0.0 all-to-all-done.refs_8_
  51.5 10.9 %downward.1 = f32[32,4096]{1,0:T(8,128)} custom-call(s32[64,16]{1,0:T(8,128)} %get-tuple-element.23.refs_0_, f32[8,32,64]{2,1,0:T(8,128)} %get-tuple-element.26.refs_1_, f32[32,64]{1,0:T(8,128)} %get-tuple-element.27.refs_2_, bf16[64,64]{1,0:T(8,128)(2,1)} %bitcast.11, bf16[64,8,64]{2,1,0:T(8,128)(2,1)} %bitcast.9, ...), custom_call_target="tpu_custom_call" | custom-call | tf_op jit(solution)/shard_map/downward/pallas_call | solution.py:690
  (2 shorter events, 0.0 us)
Async XLA Ops:
  5.7 6.2 %copy-start = (bf16[200,128]{1,0:T(8,128)(2,1)S(1)}, bf16[200,128]{1,0:T(8,128)(2,1)}, u32[]{:S(2)}) copy-start(bf16[200,128]{1,0:T(8,128)(2,1)} %get-tuple-element.22._) | copy-start | bytes 153604
  5.7 45.8 %all-to-all-start = ((bf16[32,88,128]{2,1,0:T(8,128)(2,1)}), bf16[32,88,128]{2,1,0:T(8,128)(2,1)S(1)}, u32[]{:S(2)}, u32[]{:S(2)}) async-start(bf16[32,88,128]{2,1,0:T(8,128)(2,1)} %get-tuple-element.31), calls=%async_computation | async-start | bytes 1441792 | tf_op jit(solution)/shard_map/all_to_all | solution.py:632
  11.9 21.1 %collective-permute-start = (bf16[200,128]{1,0:T(8,128)(2,1)S(1)}, bf16[200,128]{1,0:T(8,128)(2,1)S(1)}, u32[]{:S(2)}, u32[]{:S(2)}) collective-permute-start(bf16[200,128]{1,0:T(8,128)(2,1)S(1)} %copy-done), channel_id=1, source_target_pairs={{0,4},{1,5},{2,6},{3,7},{4,0},{5,1},{6,2},{7,3},{8,12},{9,13},{10,... | collective-permute-start | bytes 153608 | tf_op jit(solution)/shard_map/ppermute | solution.py:634
  33.0 11.8 %collective-permute-start.3 = (bf16[400,128]{1,0:T(8,128)(2,1)S(1)}, bf16[400,128]{1,0:T(8,128)(2,1)S(1)}, u32[]{:S(2)}, u32[]{:S(2)}) collective-permute-start(bf16[400,128]{1,0:T(8,128)(2,1)S(1)} %constant_dynamic-update-slice_fusion.refs_1_._), channel_id=1, source_target_pairs={{0,3},{1,2},{2,1},{3,0},{4,7},{5,6},{6,5},{7,4},{8,11},{9,10},{10,... | collective-permute-start | bytes 307208 | tf_op jit(solution)/shard_map/ppermute | solution.py:648
  33.1 11.7 %collective-permute-start.2 = (bf16[400,128]{1,0:T(8,128)(2,1)S(1)}, bf16[400,128]{1,0:T(8,128)(2,1)S(1)}, u32[]{:S(2)}, u32[]{:S(2)}) collective-permute-start(bf16[400,128]{1,0:T(8,128)(2,1)S(1)} %constant_dynamic-update-slice_fusion.refs_1_._), channel_id=1, source_target_pairs={{0,2},{1,3},{2,0},{3,1},{4,6},{5,7},{6,4},{7,5},{8,10},{9,11},{10,... | collective-permute-start | bytes 307208 | tf_op jit(solution)/shard_map/ppermute | solution.py:648
  36.0 8.8 %collective-permute-start.1 = (bf16[400,128]{1,0:T(8,128)(2,1)S(1)}, bf16[400,128]{1,0:T(8,128)(2,1)S(1)}, u32[]{:S(2)}, u32[]{:S(2)}) collective-permute-start(bf16[400,128]{1,0:T(8,128)(2,1)S(1)} %constant_dynamic-update-slice_fusion.refs_1_._), channel_id=1, source_target_pairs={{0,1},{1,0},{2,3},{3,2},{4,5},{5,4},{6,7},{7,6},{8,9},{9,8},{10,11... | collective-permute-start | bytes 307208 | tf_op jit(solution)/shard_map/ppermute | solution.py:648
  41.4 5.8 %collective-permute-start.4 = (bf16[80,128]{1,0:T(8,128)(2,1)S(1)}, bf16[80,128]{1,0:T(8,128)(2,1)S(1)}, u32[]{:S(2)}, u32[]{:S(2)}) collective-permute-start(bf16[80,128]{1,0:T(8,128)(2,1)S(1)} %get-tuple-element.37), channel_id=1, source_target_pairs={{0,1},{1,0},{2,3},{3,2},{4,5},{5,4},{6,7},{7,6},{8,9},{9,8},{10,11... | collective-permute-start | bytes 61448 | tf_op jit(solution)/shard_map/ppermute | solution.py:670
  42.9 8.7 %collective-permute-start.5 = (bf16[80,128]{1,0:T(8,128)(2,1)S(1)}, bf16[80,128]{1,0:T(8,128)(2,1)S(1)}, u32[]{:S(2)}, u32[]{:S(2)}) collective-permute-start(bf16[80,128]{1,0:T(8,128)(2,1)S(1)} %get-tuple-element.38), channel_id=1, source_target_pairs={{1,2},{2,1},{3,4},{4,3},{5,6},{6,5},{7,8},{8,7},{9,10},{10,9},{11,... | collective-permute-start | bytes 61448 | tf_op jit(solution)/shard_map/ppermute | solution.py:669
